TPU v7x, 32 devices: a whole 2x2x4 slice. The times are simulated.
32 devices in a mesh: dp: 8 (over z, y), tensor: 4 (over x, core).
Axes of the slice: x: 2, y: 2, z: 4, core: 2. Of those that a mesh axis runs over, the one named last changes fastest.
Arguments:
- tokens_in: bfloat16 [5120, 512], P(('dp', 'tensor')), may hold values from -6 to 6
- grad_out: bfloat16 [5120, 512], P(('dp', 'tensor')), may hold values from -6 to 6
- enc_states: bfloat16 [512, 512], P('dp'), may hold values from -6 to 6
- parents: int32 [40], P('dp'), may hold values from -1 to 39, as said below
- tree_ids: int32 [40], P('dp'), may hold values from 0 to 1, as said below
- timesteps: int32 [2], replicated, may hold values from 0 to 49
- time_table: bfloat16 [50, 512], P(None, 'dp'), may hold values from -3 to 3
- norm_self: bfloat16 [512], P('dp'), may hold values from 0.25 to 1.75
- w_query: bfloat16 [512, 512], P('dp', 'tensor'), may hold values from -0.5 to 0.5
- w_key: bfloat16 [512, 512], P('dp', 'tensor'), may hold values from -0.25 to 0.25
- w_value: bfloat16 [512, 512], P('dp', 'tensor'), may hold values from -0.25 to 0.25
- w_out: bfloat16 [512, 512], P('tensor', 'dp'), may hold values from -1 to 1
- norm_cross: bfloat16 [512], P('dp'), may hold values from 0.25 to 1.75
- c_query: bfloat16 [512, 512], P('dp', 'tensor'), may hold values from -0.5 to 0.5
- c_key: bfloat16 [512, 512], P('dp', 'tensor'), may hold values from -0.25 to 0.25
- c_value: bfloat16 [512, 512], P('dp', 'tensor'), may hold values from -0.25 to 0.25
- c_out: bfloat16 [512, 512], P('tensor', 'dp'), may hold values from -0.75 to 0.75
- norm_ffn: bfloat16 [512], P('dp'), may hold values from 0.25 to 1.75
- w_hidden: bfloat16 [512, 2048], P('dp', 'tensor'), may hold values from -0.25 to 0.25
- w_back: bfloat16 [2048, 512], P('tensor', 'dp'), may hold values from -0.1875 to 0.1875
Outputs:
- output: bfloat16 [5120, 512], P(('dp', 'tensor'))
- grad_inp: float32 [5120, 512], P(('dp', 'tensor'))
- grad_enc: float32 [512, 512], P('dp')
- grad_table: float32 [50, 512], P(None, 'dp')
- grad_norm_self: float32 [512], P('dp')
- grad_w_query: float32 [512, 512], P('dp', 'tensor')
- grad_w_key: float32 [512, 512], P('dp', 'tensor')
- grad_w_value: float32 [512, 512], P('dp', 'tensor')
- grad_w_out: float32 [512, 512], P('tensor', 'dp')
- grad_norm_cross: float32 [512], P('dp')
- grad_c_query: float32 [512, 512], P('dp', 'tensor')
- grad_c_key: float32 [512, 512], P('dp', 'tensor')
- grad_c_value: float32 [512, 512], P('dp', 'tensor')
- grad_c_out: float32 [512, 512], P('tensor', 'dp')
- grad_norm_ffn: float32 [512], P('dp')
- grad_w_hidden: float32 [512, 2048], P('dp', 'tensor')
- grad_w_back: float32 [2048, 512], P('tensor', 'dp')
Inputs may be any that keep to these rules, and one draw needn't show every extreme that they name: `parents`: tree s fills the 20 blocks (s * 20 + 10 + j) mod 40, j = 0 onward, in that order. Its first 8 blocks are a trunk, each the parent of the next, the first with parent -1; the next 4 blocks are branches whose parent is the last trunk block; the remaining blocks are leaves, each the child of one branch, every branch with 2 leaves. `tree_ids`: all blocks of one tree carry the same id, and the trees carry different ids.
All inputs are finite; a program needn't handle non-finite values.
Results may differ from a plain program's by a relative error of at most 0.023.
Values may be sent and summed in bfloat16 or wider, within the bound.
No kernel may reach another device: no remote copies, remote signals or barrier semaphores. Data moves between devices by JAX's collectives and lax.ppermute only.
A program may use at most 128 MiB of HBM per device.

v0:
```python
import jax
import jax.numpy as jnp
from jax import lax
from jax.sharding import PartitionSpec as P

HEADS = 8
TRUNK_BLKS = 8
BRANCHES = 4
LEAVES = 2


eps = 1e-05


def from_behind(block, axis, distance):
    devices = range(lax.axis_size(axis))
    route = [((i - distance) % len(devices), i) for i in devices]
    return lax.ppermute(block, axis, route)


def layer_norm(row_vals, gain_vec):
    average = jnp.mean(row_vals, axis=-1, keepdims=True)
    centered = row_vals - average
    variance = jnp.mean(centered * centered, axis=-1, keepdims=True)
    return centered * lax.rsqrt(variance + eps) * gain_vec


def gelu_exact(hidden_vals):
    return jax.nn.gelu(hidden_vals, approximate=False)


def spread(row_vals):
    return lax.all_gather(row_vals, "tensor", axis=0, tiled=True)


def fold_back(row_vals):
    return lax.psum_scatter(row_vals, "tensor", scatter_dimension=0, tiled=True)


def matmul(left_op, right_op):
    return jnp.dot(left_op, right_op, preferred_element_type=jnp.float32)


def matmul_left_t(left_op, right_op):
    return lax.dot_general(
        left_op, right_op, (((0,), (0,)), ((), ())), preferred_element_type=jnp.float32
    )


def matmul_right_t(left_op, right_op):
    return lax.dot_general(
        left_op, right_op, (((1,), (1,)), ((), ())), preferred_element_type=jnp.float32
    )


def split_heads(row_vals, local_heads):
    return row_vals.reshape(row_vals.shape[0], local_heads, row_vals.shape[1] // local_heads)


def scores_of(query_heads, key_heads, allowed):
    scaling = query_heads.shape[2] ** (-0.5)
    scores = (
        jnp.einsum("qhd,khd->hqk", query_heads, key_heads, preferred_element_type=jnp.float32)
        * scaling
    )
    if allowed is not None:
        scores = jnp.where(allowed[None], scores, -1e30)
    return scores


def attend(queries, key_rows, val_rows, allowed, local_heads):
    query_heads = split_heads(queries, local_heads)
    key_heads = split_heads(key_rows, local_heads)
    val_heads = split_heads(val_rows, local_heads)
    scores = scores_of(query_heads, key_heads, allowed)
    row_peak = jnp.max(scores, axis=-1, keepdims=True)
    exp_terms = jnp.exp(scores - row_peak)
    row_total = jnp.sum(exp_terms, axis=-1, keepdims=True)
    probs_low = (exp_terms / row_total).astype(jnp.bfloat16)
    mixed_heads = jnp.einsum(
        "hqk,khd->qhd", probs_low, val_heads, preferred_element_type=jnp.float32
    )
    return (mixed_heads.reshape(queries.shape), row_peak + jnp.log(row_total))


def attend_back(queries, key_rows, val_rows, allowed, local_heads, log_total, grad_mixed):
    query_heads = split_heads(queries, local_heads)
    key_heads = split_heads(key_rows, local_heads)
    val_heads = split_heads(val_rows, local_heads)
    scaling = query_heads.shape[2] ** (-0.5)
    scores = scores_of(query_heads, key_heads, allowed)
    probs_all = jnp.exp(scores - log_total)
    probs_low = probs_all.astype(jnp.bfloat16)
    grad_heads = split_heads(grad_mixed, local_heads)
    grad_vals = jnp.einsum(
        "hqk,qhd->khd", probs_low, grad_heads, preferred_element_type=jnp.float32
    )
    grad_probs = jnp.einsum(
        "qhd,khd->hqk", grad_heads, val_heads, preferred_element_type=jnp.float32
    )
    inner_sum = jnp.sum(grad_probs * probs_all, axis=-1, keepdims=True)
    grad_scores = (probs_all * (grad_probs - inner_sum)).astype(jnp.bfloat16)
    grad_query = (
        jnp.einsum("hqk,khd->qhd", grad_scores, key_heads, preferred_element_type=jnp.float32)
        * scaling
    )
    grad_keys = (
        jnp.einsum("hqk,qhd->khd", grad_scores, query_heads, preferred_element_type=jnp.float32)
        * scaling
    )
    return (
        grad_query.astype(jnp.bfloat16).reshape(queries.shape),
        grad_keys.reshape(key_rows.shape),
        grad_vals.reshape(val_rows.shape),
    )


def tree_mask(parents, block_len, hops_back, logical_dev):
    blocks_dev = parents.shape[0]
    group = hops_back + 1
    tree_blocks = TRUNK_BLKS + BRANCHES * (1 + LEAVES)
    total_blocks = lax.axis_size("dp") * blocks_dev
    lead_blocks = group // 2 * blocks_dev
    parent_log = jnp.where(parents >= 0, (parents - lead_blocks) % total_blocks, -1)
    query_block = logical_dev * blocks_dev + jnp.arange(blocks_dev, dtype=jnp.int32)
    key_block = (logical_dev - hops_back) * blocks_dev + jnp.arange(
        (hops_back + 1) * blocks_dev, dtype=jnp.int32
    )
    tree_start = (query_block // tree_blocks * tree_blocks)[:, None]
    query_col = query_block[:, None]
    key_row = key_block[None, :]
    earlier = (
        (key_row >= tree_start)
        & (key_row < query_col)
        & ((key_row - tree_start < TRUNK_BLKS) | (key_row == parent_log[:, None]))
    )
    same_block = key_row == query_col
    positions = jnp.arange(block_len, dtype=jnp.int32)
    causal = positions[None, :] <= positions[:, None]
    allowed = earlier[:, None, :, None] | same_block[:, None, :, None] & causal[None, :, None, :]
    return allowed.reshape(blocks_dev * block_len, (hops_back + 1) * blocks_dev * block_len)


def on_device(
    tokens_in,
    grad_out,
    enc_states,
    parents,
    tree_ids,
    timesteps,
    time_table,
    norm_self,
    w_query,
    w_key,
    w_value,
    w_out,
    norm_cross,
    c_query,
    c_key,
    c_value,
    c_out,
    norm_ffn,
    w_hidden,
    w_back,
):
    local_heads = HEADS // lax.axis_size("tensor")
    gathered = (
        lax.all_gather(time_table, "dp", axis=1, tiled=True),
        lax.all_gather(norm_self, "dp", axis=0, tiled=True),
        lax.all_gather(w_query, "dp", axis=0, tiled=True),
        lax.all_gather(w_key, "dp", axis=0, tiled=True),
        lax.all_gather(w_value, "dp", axis=0, tiled=True),
        lax.all_gather(w_out, "dp", axis=1, tiled=True),
        lax.all_gather(norm_cross, "dp", axis=0, tiled=True),
        lax.all_gather(c_query, "dp", axis=0, tiled=True),
        lax.all_gather(c_key, "dp", axis=0, tiled=True),
        lax.all_gather(c_value, "dp", axis=0, tiled=True),
        lax.all_gather(c_out, "dp", axis=1, tiled=True),
        lax.all_gather(norm_ffn, "dp", axis=0, tiled=True),
        lax.all_gather(w_hidden, "dp", axis=0, tiled=True),
        lax.all_gather(w_back, "dp", axis=1, tiled=True),
    )
    (
        table_full,
        gain_self,
        query_full,
        key_full,
        value_full,
        out_full,
        gain_cross,
        cquery_full,
        ckey_full,
        cvalue_full,
        cout_full,
        gain_ffn,
        up_full,
        down_full,
    ) = gathered
    tree_index = tree_ids[0]
    step_id = jnp.sum(
        jnp.where(jnp.arange(timesteps.shape[0], dtype=jnp.int32) == tree_index, timesteps, 0)
    )
    step_hot = (jnp.arange(table_full.shape[0], dtype=jnp.int32) == step_id).astype(jnp.float32)
    time_row = matmul(step_hot.astype(jnp.bfloat16)[None, :], table_full)
    resid_in = tokens_in.astype(jnp.float32) + time_row
    normed_self, norm_self_back = jax.vjp(layer_norm, resid_in, gain_self.astype(jnp.float32))
    act_self = spread(normed_self.astype(jnp.bfloat16))
    head_cols = query_full.shape[1]
    qkv_full = jnp.concatenate([query_full, key_full, value_full], axis=1)
    projected = matmul(act_self, qkv_full).astype(jnp.bfloat16)
    queries = projected[:, :head_cols]
    local_kv = jnp.stack([projected[:, head_cols : 2 * head_cols], projected[:, 2 * head_cols :]])
    token_rows = act_self.shape[0]
    blocks_dev = parents.shape[0]
    group = (TRUNK_BLKS + BRANCHES * (1 + LEAVES)) // blocks_dev
    hops_back = group - 1
    logical_dev = (lax.axis_index("dp") - group // 2) % lax.axis_size("dp")
    position = logical_dev % group
    earlier = [from_behind(local_kv, "dp", distance) for distance in range(hops_back, 0, -1)]
    kv_all = jnp.concatenate(earlier + [local_kv], axis=1)
    allowed = tree_mask(parents, token_rows // blocks_dev, hops_back, logical_dev)
    attn_mixed, lse_self = attend(queries, kv_all[0], kv_all[1], allowed, local_heads)
    attn_low = attn_mixed.astype(jnp.bfloat16)
    resid_mid = resid_in + fold_back(matmul(attn_low, out_full))
    normed_cross, norm_cross_back = jax.vjp(layer_norm, resid_mid, gain_cross.astype(jnp.float32))
    act_cross = spread(normed_cross.astype(jnp.bfloat16))
    cross_queries = matmul(act_cross, cquery_full).astype(jnp.bfloat16)
    enc_local = jnp.stack([matmul(enc_states, ckey_full), matmul(enc_states, cvalue_full)]).astype(
        jnp.bfloat16
    )
    enc_rows = enc_local.shape[1]
    tree_parts = [jnp.zeros_like(enc_local) for member in range(group)]
    for distance in range(-hops_back, group):
        if distance == 0:
            received = enc_local
        else:
            received = from_behind(enc_local, "dp", distance)
        for member in range(group):
            tree_parts[member] = jnp.where(
                position - distance == member, received, tree_parts[member]
            )
    enc_tree = jnp.concatenate(tree_parts, axis=1)
    cross_mixed, lse_cross = attend(cross_queries, enc_tree[0], enc_tree[1], None, local_heads)
    cross_low = cross_mixed.astype(jnp.bfloat16)
    resid_ffn = resid_mid + fold_back(matmul(cross_low, cout_full))
    normed_ffn, norm_ffn_back = jax.vjp(layer_norm, resid_ffn, gain_ffn.astype(jnp.float32))
    act_ffn = spread(normed_ffn.astype(jnp.bfloat16))
    hidden_pre = matmul(act_ffn, up_full)
    hidden_act, gelu_back = jax.vjp(gelu_exact, hidden_pre)
    hidden_low = hidden_act.astype(jnp.bfloat16)
    result = resid_ffn + fold_back(matmul(hidden_low, down_full))
    output = result.astype(jnp.bfloat16)
    grad_result = grad_out.astype(jnp.float32)
    grad_top = spread(grad_out)
    grad_down = matmul_left_t(hidden_low, grad_top)
    grad_hidden = matmul_right_t(grad_top, down_full)
    grad_pre = gelu_back(grad_hidden)[0].astype(jnp.bfloat16)
    grad_up = matmul_left_t(act_ffn, grad_pre)
    grad_act_ffn = fold_back(matmul_right_t(grad_pre, up_full))
    grad_resid_ffn_n, grad_gain_ffn = norm_ffn_back(grad_act_ffn)
    grad_resid_ffn = grad_result + grad_resid_ffn_n
    ffn_sums = (grad_up, grad_down)
    grad_cross_top = spread(grad_resid_ffn.astype(jnp.bfloat16))
    grad_cout = matmul_left_t(cross_low, grad_cross_top)
    grad_cross_mixed = matmul_right_t(grad_cross_top, cout_full).astype(jnp.bfloat16)
    grad_cq, grad_enc_keys, grad_enc_vals = attend_back(
        cross_queries, enc_tree[0], enc_tree[1], None, local_heads, lse_cross, grad_cross_mixed
    )
    grad_cquery = matmul_left_t(act_cross, grad_cq)
    grad_act_cross = fold_back(matmul_right_t(grad_cq, cquery_full))
    grad_resid_mid_n, grad_gain_cross = norm_cross_back(grad_act_cross)
    grad_resid_mid = grad_resid_ffn + grad_resid_mid_n
    enc_grads = jnp.stack([grad_enc_keys, grad_enc_vals])
    grad_parts = enc_grads.reshape(2, group, enc_rows, head_cols)
    enc_total = jnp.zeros((2, enc_rows, head_cols), jnp.float32)
    for distance in range(-hops_back, group):
        outgoing = jnp.zeros((2, enc_rows, head_cols), jnp.float32)
        for member in range(group):
            outgoing = jnp.where(position + distance == member, grad_parts[:, member], outgoing)
        if distance == 0:
            enc_total = enc_total + outgoing
        else:
            enc_total = enc_total + from_behind(
                outgoing.astype(jnp.bfloat16), "dp", distance
            ).astype(outgoing.dtype)
    enc_sum = enc_total.astype(jnp.bfloat16)
    grad_ckey = matmul_left_t(enc_states, enc_sum[0])
    grad_cvalue = matmul_left_t(enc_states, enc_sum[1])
    grad_enc_part = matmul_right_t(enc_sum[0], ckey_full) + matmul_right_t(enc_sum[1], cvalue_full)
    cross_sums = (grad_cquery, grad_ckey, grad_cvalue, grad_cout)
    grad_self_top = spread(grad_resid_mid.astype(jnp.bfloat16))
    grad_wout = matmul_left_t(attn_low, grad_self_top)
    grad_attn = matmul_right_t(grad_self_top, out_full).astype(jnp.bfloat16)
    grad_query, grad_keys, grad_vals = attend_back(
        queries, kv_all[0], kv_all[1], allowed, local_heads, lse_self, grad_attn
    )
    grad_kv = jnp.stack([grad_keys, grad_vals]).reshape(2, hops_back + 1, token_rows, head_cols)
    total_kv = grad_kv[:, hops_back]
    for distance in range(hops_back, 0, -1):
        total_kv = total_kv + from_behind(
            grad_kv[:, hops_back - distance].astype(jnp.bfloat16), "dp", -distance
        ).astype(jnp.float32)
    total_low = total_kv.astype(jnp.bfloat16)
    grad_qkv = jnp.concatenate([grad_query, total_low[0], total_low[1]], axis=1)
    grad_qkv_w = matmul_left_t(act_self, grad_qkv)
    grad_act_self = fold_back(matmul_right_t(grad_qkv, qkv_full))
    grad_resid_in_n, grad_gain_self = norm_self_back(grad_act_self)
    grad_in = grad_resid_mid + grad_resid_in_n
    grad_table_part = step_hot[:, None] * jnp.sum(grad_in, axis=0)[None, :]
    tensor_sums = (
        lax.psum(grad_gain_self.astype(jnp.bfloat16), "tensor").astype(jnp.float32),
        lax.psum(grad_gain_cross.astype(jnp.bfloat16), "tensor").astype(jnp.float32),
        lax.psum(grad_gain_ffn.astype(jnp.bfloat16), "tensor").astype(jnp.float32),
        lax.psum(grad_table_part.astype(jnp.bfloat16), "tensor").astype(jnp.float32),
        lax.psum(grad_enc_part.astype(jnp.bfloat16), "tensor").astype(jnp.float32),
    )
    sum_self, sum_cross, sum_ffn, sum_table, grad_enc = tensor_sums
    last_sums = (
        lax.psum_scatter(sum_table, "dp", scatter_dimension=1, tiled=True),
        lax.psum_scatter(sum_self, "dp", scatter_dimension=0, tiled=True),
        lax.psum_scatter(sum_cross, "dp", scatter_dimension=0, tiled=True),
        lax.psum_scatter(sum_ffn, "dp", scatter_dimension=0, tiled=True),
        lax.psum_scatter(grad_qkv_w[:, :head_cols], "dp", scatter_dimension=0, tiled=True),
        lax.psum_scatter(
            grad_qkv_w[:, head_cols : 2 * head_cols], "dp", scatter_dimension=0, tiled=True
        ),
        lax.psum_scatter(grad_qkv_w[:, 2 * head_cols :], "dp", scatter_dimension=0, tiled=True),
        lax.psum_scatter(grad_wout, "dp", scatter_dimension=1, tiled=True),
    )
    rest_sums = (
        lax.psum_scatter(cross_sums[0], "dp", scatter_dimension=0, tiled=True),
        lax.psum_scatter(cross_sums[1], "dp", scatter_dimension=0, tiled=True),
        lax.psum_scatter(cross_sums[2], "dp", scatter_dimension=0, tiled=True),
        lax.psum_scatter(cross_sums[3], "dp", scatter_dimension=1, tiled=True),
        lax.psum_scatter(ffn_sums[0], "dp", scatter_dimension=0, tiled=True),
        lax.psum_scatter(ffn_sums[1], "dp", scatter_dimension=1, tiled=True),
    )
    cross_done = rest_sums[:4]
    ffn_done = rest_sums[4:]
    return (
        output,
        grad_in,
        grad_enc,
        last_sums[0],
        last_sums[1],
        last_sums[4],
        last_sums[5],
        last_sums[6],
        last_sums[7],
        last_sums[2],
        cross_done[0],
        cross_done[1],
        cross_done[2],
        cross_done[3],
        last_sums[3],
        ffn_done[0],
        ffn_done[1],
    )


def solution(mesh):
    in_specs = (
        P(("dp", "tensor"), None),
        P(("dp", "tensor"), None),
        P("dp", None),
        P("dp"),
        P("dp"),
        P(),
        P(None, "dp"),
        P("dp"),
        P("dp", "tensor"),
        P("dp", "tensor"),
        P("dp", "tensor"),
        P("tensor", "dp"),
        P("dp"),
        P("dp", "tensor"),
        P("dp", "tensor"),
        P("dp", "tensor"),
        P("tensor", "dp"),
        P("dp"),
        P("dp", "tensor"),
        P("tensor", "dp"),
    )
    out_specs = (
        P(("dp", "tensor"), None),
        P(("dp", "tensor"), None),
        P("dp", None),
        P(None, "dp"),
        P("dp"),
        P("dp", "tensor"),
        P("dp", "tensor"),
        P("dp", "tensor"),
        P("tensor", "dp"),
        P("dp"),
        P("dp", "tensor"),
        P("dp", "tensor"),
        P("dp", "tensor"),
        P("tensor", "dp"),
        P("dp"),
        P("dp", "tensor"),
        P("tensor", "dp"),
    )
    return jax.shard_map(
        on_device, mesh=mesh, in_specs=in_specs, out_specs=out_specs, check_vma=False
    )
```

profile of v0, /device:TPU:0, one launch (start us, length us, event | category | flops | bytes accessed | tf_op | source)
XLA Modules:
  0.0 1434.1 jit_solution(7578143181505670846)
XLA Ops:
  35.5 30.8 %all-gather = bf16[8,64,50]{1,2,0:T(8,128)(2,1)S(1)} all-gather(bf16[1,64,50]{1,2,0:T(8,128)(2,1)} %bitcast.382), channel_id=1, replica_groups=mesh['dp'=8,'tensor'=4] {'dp'}, dimensions={0}, use_global_device_ids=true | all-gather | bytes 57600 | tf_op jit(solution)/shard_map/all_gather | solution.py:168
  71.3 30.7 %all_gather.63 = bf16[512,128]{1,0:T(8,128)(2,1)S(1)} all-gather(bf16[64,128]{1,0:T(8,128)(2,1)} %param.28), channel_id=1, replica_groups=mesh['dp'=8,'tensor'=4] {'dp'}, dimensions={0}, use_global_device_ids=true | all-gather | bytes 147456 | tf_op jit(solution)/shard_map/all_gather | solution.py:170
  102.1 30.7 %all_gather.64 = bf16[512,128]{1,0:T(8,128)(2,1)S(1)} all-gather(bf16[64,128]{1,0:T(8,128)(2,1)} %param.29), channel_id=1, replica_groups=mesh['dp'=8,'tensor'=4] {'dp'}, dimensions={0}, use_global_device_ids=true | all-gather | bytes 147456 | tf_op jit(solution)/shard_map/all_gather | solution.py:171
  132.8 30.7 %all_gather.65 = bf16[512,128]{1,0:T(8,128)(2,1)S(1)} all-gather(bf16[64,128]{1,0:T(8,128)(2,1)} %param.30), channel_id=1, replica_groups=mesh['dp'=8,'tensor'=4] {'dp'}, dimensions={0}, use_global_device_ids=true | all-gather | bytes 147456 | tf_op jit(solution)/shard_map/all_gather | solution.py:172
  177.4 46.1 %all_gather.66 = bf16[128,512]{0,1:T(8,128)(2,1)S(1)} all-gather(bf16[128,64]{0,1:T(8,128)(2,1)S(1)} %copy-done.82), channel_id=1, replica_groups=mesh['dp'=8,'tensor'=4] {'dp'}, dimensions={1}, use_global_device_ids=true | all-gather | bytes 147456 | tf_op jit(solution)/shard_map/all_gather | solution.py:173
  236.2 30.7 %all_gather.67 = bf16[512,128]{1,0:T(8,128)(2,1)S(1)} all-gather(bf16[64,128]{1,0:T(8,128)(2,1)S(1)} %copy-done.83), channel_id=1, replica_groups=mesh['dp'=8,'tensor'=4] {'dp'}, dimensions={0}, use_global_device_ids=true | all-gather | bytes 147456 | tf_op jit(solution)/shard_map/all_gather | solution.py:176
  266.9 30.6 %all_gather.68 = bf16[512,128]{1,0:T(8,128)(2,1)S(1)} all-gather(bf16[64,128]{1,0:T(8,128)(2,1)S(1)} %copy-done.84), channel_id=1, replica_groups=mesh['dp'=8,'tensor'=4] {'dp'}, dimensions={0}, use_global_device_ids=true | all-gather | bytes 147456 | tf_op jit(solution)/shard_map/all_gather | solution.py:177
  302.0 30.5 %all_gather.71 = bf16[512,128]{1,0:T(8,128)(2,1)S(1)} all-gather(bf16[64,128]{1,0:T(8,128)(2,1)S(1)} %copy-done.85), channel_id=1, replica_groups=mesh['dp'=8,'tensor'=4] {'dp'}, dimensions={0}, use_global_device_ids=true | all-gather | bytes 147456 | tf_op jit(solution)/shard_map/all_gather | solution.py:175
  332.6 31.9 %all_gather.72 = bf16[128,512]{0,1:T(8,128)(2,1)S(1)} all-gather(bf16[128,64]{0,1:T(8,128)(2,1)S(1)} %copy-done.86), channel_id=1, replica_groups=mesh['dp'=8,'tensor'=4] {'dp'}, dimensions={1}, use_global_device_ids=true | all-gather | bytes 147456 | tf_op jit(solution)/shard_map/all_gather | solution.py:178
  378.0 33.3 %all_gather.75 = bf16[512,512]{1,0:T(8,128)(2,1)} all-gather(bf16[64,512]{1,0:T(8,128)(2,1)S(1)} %copy-done.66), channel_id=1, replica_groups=mesh['dp'=8,'tensor'=4] {'dp'}, dimensions={0}, use_global_device_ids=true | all-gather | bytes 589824 | tf_op jit(solution)/shard_map/all_gather | solution.py:180
  411.3 33.4 %all_gather.76 = bf16[512,512]{0,1:T(8,128)(2,1)} all-gather(bf16[512,64]{0,1:T(8,128)(2,1)S(1)} %copy-done.67), channel_id=1, replica_groups=mesh['dp'=8,'tensor'=4] {'dp'}, dimensions={1}, use_global_device_ids=true | all-gather | bytes 589824 | tf_op jit(solution)/shard_map/all_gather | solution.py:181
  499.3 26.8 %reduce-scatter.28.cloned.1.call-done = f32[160,512]{1,0:T(8,128)} async-done(((f32[640,512]{1,0:T(8,128)}), f32[160,512]{1,0:T(8,128)}) %reduce-scatter.28.cloned.1.call-update) | async-done | bytes 327696 | tf_op jit(solution)/shard_map/reduce_scatter | solution.py:37
  540.9 27.0 %reduce-scatter.32.cloned.1.call-done = f32[160,512]{1,0:T(8,128)} async-done(((f32[640,512]{1,0:T(8,128)}), f32[160,512]{1,0:T(8,128)}) %reduce-scatter.32.cloned.1.call-update) | async-done | bytes 327696 | tf_op jit(solution)/shard_map/reduce_scatter | solution.py:37
  737.8 40.1 %reduce-scatter.52.cloned.1.call-done = f32[64,50]{1,0:T(8,128)} async-done(((f32[512,50]{1,0:T(8,128)}), f32[64,50]{1,0:T(8,128)}) %reduce-scatter.52.cloned.1.call-update) | async-done | bytes 12816
  779.3 65.5 %reduce-scatter.50.cloned.1.call-done = f32[512,64]{0,1:T(8,128)} async-done(((f32[512,512]{0,1:T(8,128)}), f32[512,64]{0,1:T(8,128)}) %reduce-scatter.50.cloned.1.call-update) | async-done | bytes 131088 | tf_op jit(solution)/shard_map/reduce_scatter | solution.py:336
  844.8 66.3 %reduce-scatter.48.cloned.1.call-done = f32[64,512]{1,0:T(8,128)} async-done(((f32[512,512]{1,0:T(8,128)}), f32[64,512]{1,0:T(8,128)}) %reduce-scatter.48.cloned.1.call-update) | async-done | bytes 131088 | tf_op jit(solution)/shard_map/reduce_scatter | solution.py:335
  911.2 64.6 %reduce-scatter.46.cloned.1.call-done = f32[128,64]{0,1:T(8,128)} async-done(((f32[128,512]{0,1:T(8,128)}), f32[128,64]{0,1:T(8,128)}) %reduce-scatter.46.cloned.1.call-update) | async-done | bytes 32784 | tf_op jit(solution)/shard_map/reduce_scatter | solution.py:334
  975.7 64.4 %reduce-scatter.44.cloned.1.call-done = f32[64,128]{1,0:T(8,128)} async-done(((f32[512,128]{1,0:T(8,128)}), f32[64,128]{1,0:T(8,128)}) %reduce-scatter.44.cloned.1.call-update) | async-done | bytes 32784 | tf_op jit(solution)/shard_map/reduce_scatter | solution.py:331
  1040.1 64.6 %reduce-scatter.56.cloned.1.call-done = f32[64,128]{1,0:T(8,128)} async-done(((f32[512,128]{1,0:T(8,128)}), f32[64,128]{1,0:T(8,128)}) %reduce-scatter.56.cloned.1.call-update) | async-done | bytes 32784
  1104.7 64.5 %reduce-scatter.54.cloned.1.call-done = f32[64,128]{1,0:T(8,128)} async-done(((f32[512,128]{1,0:T(8,128)}), f32[64,128]{1,0:T(8,128)}) %reduce-scatter.54.cloned.1.call-update) | async-done | bytes 32784
  1169.2 64.5 %reduce-scatter.42.cloned.1.call-done = f32[128,64]{0,1:T(8,128)} async-done(((f32[128,512]{0,1:T(8,128)}), f32[128,64]{0,1:T(8,128)}) %reduce-scatter.42.cloned.1.call-update) | async-done | bytes 32784 | tf_op jit(solution)/shard_map/reduce_scatter | solution.py:328
  1233.6 64.4 %reduce-scatter.40.cloned.1.call-done = f32[64,128]{1,0:T(8,128)} async-done(((f32[512,128]{1,0:T(8,128)}), f32[64,128]{1,0:T(8,128)}) %reduce-scatter.40.cloned.1.call-update) | async-done | bytes 32784 | tf_op jit(solution)/shard_map/reduce_scatter | solution.py:327
  1298.1 64.4 %reduce-scatter.38.cloned.1.call-done = f32[64,128]{1,0:T(8,128)} async-done(((f32[512,128]{1,0:T(8,128)}), f32[64,128]{1,0:T(8,128)}) %reduce-scatter.38.cloned.1.call-update) | async-done | bytes 32784 | tf_op jit(solution)/shard_map/reduce_scatter | solution.py:324
  1362.5 64.4 %reduce-scatter.36.cloned.1.call-done = f32[64,128]{1,0:T(8,128)} async-done(((f32[512,128]{1,0:T(8,128)}), f32[64,128]{1,0:T(8,128)}) %reduce-scatter.36.cloned.1.call-update) | async-done | bytes 32784 | tf_op jit(solution)/shard_map/reduce_scatter | solution.py:323
  (432 shorter events, 315.5 us)
Async XLA Ops:
  7.2 357.8 %reduce-scatter.24.cloned.1.call-start = ((), (), s32[]{:S(2)}) async-start(), calls=%async_computation.17 | async-start | bytes 1638400 | tf_op jit(solution)/shard_map/reduce_scatter | solution.py:37
  172.6 51.0 %collective-permute-start.2 = (bf16[2,640,128]{1,2,0:T(8,128)(2,1)S(1)}, bf16[2,640,128]{1,2,0:T(8,128)(2,1)S(1)}, u32[]{:S(2)}, u32[]{:S(2)}) collective-permute-start(bf16[2,640,128]{1,2,0:T(8,128)(2,1)S(1)} %pad_maximum_fusion.1), channel_id=1, source_target_pairs={{28,0},{0,4},{4,8},{8,12},{12,16},{16,20},{20,24},{24,28},{29,1},{... | collective-permute-start | bytes 983048 | tf_op jit(solution)/shard_map/ppermute | solution.py:18
  172.6 51.0 %collective-permute-start.1 = (bf16[2,640,128]{1,2,0:T(8,128)(2,1)S(1)}, bf16[2,640,128]{1,2,0:T(8,128)(2,1)S(1)}, u32[]{:S(2)}, u32[]{:S(2)}) collective-permute-start(bf16[2,640,128]{1,2,0:T(8,128)(2,1)S(1)} %pad_maximum_fusion.1), channel_id=1, source_target_pairs={{24,0},{28,4},{0,8},{4,12},{8,16},{12,20},{16,24},{20,28},{25,1},{... | collective-permute-start | bytes 983048 | tf_op jit(solution)/shard_map/ppermute | solution.py:18
  236.1 217.0 %reduce-scatter.26.cloned.1.call-start = ((), (), s32[]{:S(2)}) async-start(), calls=%async_computation.18 | async-start | bytes 1638400 | tf_op jit(solution)/shard_map/reduce_scatter | solution.py:37
  297.9 66.7 %collective-permute-start.7 = (bf16[2,64,128]{2,1,0:T(8,128)(2,1)S(1)}, bf16[2,64,128]{2,1,0:T(8,128)(2,1)S(1)}, u32[]{:S(2)}, u32[]{:S(2)}) collective-permute-start(bf16[2,64,128]{2,1,0:T(8,128)(2,1)S(1)} %pad_maximum_fusion.6), channel_id=1, source_target_pairs={{8,0},{12,4},{16,8},{20,12},{24,16},{28,20},{0,24},{4,28},{9,1},{1... | collective-permute-start | bytes 98312 | tf_op jit(solution)/shard_map/ppermute | solution.py:18
  298.5 66.0 %collective-permute-start.6 = (bf16[2,64,128]{2,1,0:T(8,128)(2,1)S(1)}, bf16[2,64,128]{2,1,0:T(8,128)(2,1)S(1)}, u32[]{:S(2)}, u32[]{:S(2)}) collective-permute-start(bf16[2,64,128]{2,1,0:T(8,128)(2,1)S(1)} %pad_maximum_fusion.6), channel_id=1, source_target_pairs={{4,0},{8,4},{12,8},{16,12},{20,16},{24,20},{28,24},{0,28},{5,1},{9... | collective-permute-start | bytes 98312 | tf_op jit(solution)/shard_map/ppermute | solution.py:18
  300.4 64.1 %collective-permute-start.5 = (bf16[2,64,128]{2,1,0:T(8,128)(2,1)S(1)}, bf16[2,64,128]{2,1,0:T(8,128)(2,1)S(1)}, u32[]{:S(2)}, u32[]{:S(2)}) collective-permute-start(bf16[2,64,128]{2,1,0:T(8,128)(2,1)S(1)} %pad_maximum_fusion.6), channel_id=1, source_target_pairs={{28,0},{0,4},{4,8},{8,12},{12,16},{16,20},{20,24},{24,28},{29,1},{... | collective-permute-start | bytes 98312 | tf_op jit(solution)/shard_map/ppermute | solution.py:18
  300.5 64.0 %collective-permute-start.4 = (bf16[2,64,128]{2,1,0:T(8,128)(2,1)S(1)}, bf16[2,64,128]{2,1,0:T(8,128)(2,1)S(1)}, u32[]{:S(2)}, u32[]{:S(2)}) collective-permute-start(bf16[2,64,128]{2,1,0:T(8,128)(2,1)S(1)} %pad_maximum_fusion.6), channel_id=1, source_target_pairs={{24,0},{28,4},{0,8},{4,12},{8,16},{12,20},{16,24},{20,28},{25,1},{... | collective-permute-start | bytes 98312 | tf_op jit(solution)/shard_map/ppermute | solution.py:18
  377.9 119.1 %reduce-scatter.30.cloned.1.call-start = ((), (), s32[]{:S(2)}) async-start(), calls=%async_computation.20 | async-start | bytes 1638400 | tf_op jit(solution)/shard_map/reduce_scatter | solution.py:37
  471.7 54.4 %reduce-scatter.28.cloned.1.call-start = ((), (), s32[]{:S(2)}) async-start(), calls=%async_computation.19 | async-start | bytes 1638400 | tf_op jit(solution)/shard_map/reduce_scatter | solution.py:37
  476.3 91.5 %reduce-scatter.32.cloned.1.call-start = ((), (), s32[]{:S(2)}) async-start(), calls=%async_computation.21 | async-start | bytes 1638400 | tf_op jit(solution)/shard_map/reduce_scatter | solution.py:37
  540.8 138.1 %reduce-scatter.34.cloned.1.call-start = ((), (), s32[]{:S(2)}) async-start(), calls=%async_computation.22 | async-start | bytes 1638400 | tf_op jit(solution)/shard_map/reduce_scatter | solution.py:37
  645.3 67.6 %all-reduce.11.cloned.1.call-start = ((), (), s32[]{:S(2)}) async-start(), calls=%async_computation.23 | async-start | bytes 131072 | tf_op jit(solution)/shard_map/psum | solution.py:315
  671.7 106.2 %reduce-scatter.52.cloned.1.call-start = ((), (), s32[]{:S(2)}) async-start(), calls=%async_computation.32 | async-start | bytes 294912
  695.6 149.2 %reduce-scatter.50.cloned.1.call-start = ((), (), s32[]{:S(2)}) async-start(), calls=%async_computation.31 | async-start | bytes 1179648 | tf_op jit(solution)/shard_map/reduce_scatter | solution.py:336
  697.4 213.8 %reduce-scatter.48.cloned.1.call-start = ((), (), s32[]{:S(2)}) async-start(), calls=%async_computation.30 | async-start | bytes 1179648 | tf_op jit(solution)/shard_map/reduce_scatter | solution.py:335
  700.2 275.5 %reduce-scatter.46.cloned.1.call-start = ((), (), s32[]{:S(2)}) async-start(), calls=%async_computation.29 | async-start | bytes 294912 | tf_op jit(solution)/shard_map/reduce_scatter | solution.py:334
  701.7 338.4 %reduce-scatter.44.cloned.1.call-start = ((), (), s32[]{:S(2)}) async-start(), calls=%async_computation.28 | async-start | bytes 294912 | tf_op jit(solution)/shard_map/reduce_scatter | solution.py:331
  702.9 401.8 %reduce-scatter.56.cloned.1.call-start = ((), (), s32[]{:S(2)}) async-start(), calls=%async_computation.34 | async-start | bytes 294912
  704.0 465.2 %reduce-scatter.54.cloned.1.call-start = ((), (), s32[]{:S(2)}) async-start(), calls=%async_computation.33 | async-start | bytes 294912
  705.1 528.5 %reduce-scatter.42.cloned.1.call-start = ((), (), s32[]{:S(2)}) async-start(), calls=%async_computation.27 | async-start | bytes 294912 | tf_op jit(solution)/shard_map/reduce_scatter | solution.py:328
  706.4 591.7 %reduce-scatter.40.cloned.1.call-start = ((), (), s32[]{:S(2)}) async-start(), calls=%async_computation.26 | async-start | bytes 294912 | tf_op jit(solution)/shard_map/reduce_scatter | solution.py:327
  708.0 654.5 %reduce-scatter.38.cloned.1.call-start = ((), (), s32[]{:S(2)}) async-start(), calls=%async_computation.25 | async-start | bytes 294912 | tf_op jit(solution)/shard_map/reduce_scatter | solution.py:324
  708.6 718.3 %reduce-scatter.36.cloned.1.call-start = ((), (), s32[]{:S(2)}) async-start(), calls=%async_computation.24 | async-start | bytes 294912 | tf_op jit(solution)/shard_map/reduce_scatter | solution.py:323
  (116 other events, 2606.3 us)
Sparse Core Ops, SparseCore 0:
  236.2 22.8 reduce-scatter.23
  378.0 26.0 reduce-scatter.25
  471.8 25.1 reduce-scatter.29
  499.5 26.5 reduce-scatter.27
  540.9 26.9 reduce-scatter.31
  645.4 33.4 reduce-scatter.33
  681.8 31.0 all-reduce.10
  716.6 61.2 reduce-scatter.51
  782.3 62.5 reduce-scatter.49
  848.6 62.4 reduce-scatter.47
  915.4 60.2 reduce-scatter.45
  979.8 60.2 reduce-scatter.43
  1044.4 60.2 reduce-scatter.55
  1108.8 60.3 reduce-scatter.53
  1173.3 60.3 reduce-scatter.41
  1237.7 60.2 reduce-scatter.39
  1302.2 60.2 reduce-scatter.37
  1366.6 60.2 reduce-scatter.35
where the time goes:
time: 1450 us; the launch traced here: 1430 us
  waiting for transfers between devices  799 us (55%)
  blocking collectives  462 us (32%)
  matrix products  53.6 us (4%)
  other arithmetic  39.3 us (3%)
  local copies, waits for them, and re-layouts  32.7 us (2%)
  starting transfers between devices  29.9 us (2%)
  between operations  17.7 us (1%)
    unnamed x21, waiting for transfers between devices  170 us
    reduce_scatter x6, waiting for transfers between devices, fold_back(): return lax.psum_scatter(row_vals, 'tensor', scatter_dimension=0, tiled=True)  81.6 us
    reduce_scatter x1, waiting for transfers between devices, on_device(): lax.psum_scatter(ffn_sums[0], 'dp', scatter_dimension=0, tiled=True)  66.3 us
    reduce_scatter x1, waiting for transfers between devices, on_device(): lax.psum_scatter(ffn_sums[1], 'dp', scatter_dimension=1, tiled=True)  65.5 us
    reduce_scatter x1, waiting for transfers between devices, on_device(): lax.psum_scatter(cross_sums[3], 'dp', scatter_dimension=1, tiled=True)  64.6 us
    reduce_scatter x1, waiting for transfers between devices, on_device(): lax.psum_scatter(grad_wout, 'dp', scatter_dimension=1, tiled=True)  64.5 us
    reduce_scatter x1, waiting for transfers between devices, on_device(): lax.psum_scatter(grad_qkv_w[:, 2 * head_cols:], 'dp', scatter_dimension=0...  64.4 us
    reduce_scatter x1, waiting for transfers between devices, on_device(): lax.psum_scatter(grad_qkv_w[:, :head_cols], 'dp', scatter_dimension=0, ti...  64.4 us
  transfers between devices with their start and end apart: 36, of which 21 were waited for; matrix products, arithmetic and copies ran while one was open for 2% of the time, Pallas kernels for 0%

commit v1 on v0

v1 whole, which is shorter than its diff:
```python
import jax
import jax.numpy as jnp
from jax import lax
from jax.sharding import PartitionSpec as P

HEADS = 8
TRUNK_BLKS = 8
BRANCHES = 4
LEAVES = 2
eps = 1e-05
bf16 = jnp.bfloat16
f32 = jnp.float32


def layer_norm(row_vals, gain_vec):
    average = jnp.mean(row_vals, axis=-1, keepdims=True)
    centered = row_vals - average
    variance = jnp.mean(centered * centered, axis=-1, keepdims=True)
    inv = lax.rsqrt(variance + eps)
    return centered * inv * gain_vec, inv, centered * inv


def layer_norm_back(grad_act, normed, inv, gain_vec):
    scaled = grad_act * gain_vec
    mean_g = jnp.mean(scaled, axis=-1, keepdims=True)
    mean_gx = jnp.mean(scaled * normed, axis=-1, keepdims=True)
    return inv * (scaled - mean_g - normed * mean_gx)


def gelu_exact(hidden_vals):
    return jax.nn.gelu(hidden_vals, approximate=False)


def mm(a, b):
    return jnp.dot(a, b, preferred_element_type=f32)


def mm_tn(a, b):
    return lax.dot_general(a, b, (((0,), (0,)), ((), ())), preferred_element_type=f32)


def mm_nt(a, b):
    return lax.dot_general(a, b, (((1,), (1,)), ((), ())), preferred_element_type=f32)


def split_heads(row_vals, local_heads):
    return row_vals.reshape(row_vals.shape[0], local_heads, row_vals.shape[1] // local_heads)


def scores_of(query_heads, key_heads, allowed):
    scaling = query_heads.shape[2] ** (-0.5)
    scores = jnp.einsum("qhd,khd->hqk", query_heads, key_heads, preferred_element_type=f32) * scaling
    if allowed is not None:
        scores = jnp.where(allowed[None], scores, -1e30)
    return scores


def attend(queries, key_rows, val_rows, allowed, local_heads):
    query_heads = split_heads(queries, local_heads)
    key_heads = split_heads(key_rows, local_heads)
    val_heads = split_heads(val_rows, local_heads)
    scores = scores_of(query_heads, key_heads, allowed)
    row_peak = jnp.max(scores, axis=-1, keepdims=True)
    exp_terms = jnp.exp(scores - row_peak)
    row_total = jnp.sum(exp_terms, axis=-1, keepdims=True)
    probs_low = (exp_terms / row_total).astype(bf16)
    mixed_heads = jnp.einsum("hqk,khd->qhd", probs_low, val_heads, preferred_element_type=f32)
    return (mixed_heads.reshape(queries.shape), row_peak + jnp.log(row_total))


def attend_back(queries, key_rows, val_rows, allowed, local_heads, log_total, grad_mixed):
    query_heads = split_heads(queries, local_heads)
    key_heads = split_heads(key_rows, local_heads)
    val_heads = split_heads(val_rows, local_heads)
    scaling = query_heads.shape[2] ** (-0.5)
    scores = scores_of(query_heads, key_heads, allowed)
    probs_all = jnp.exp(scores - log_total)
    probs_low = probs_all.astype(bf16)
    grad_heads = split_heads(grad_mixed, local_heads)
    grad_vals = jnp.einsum("hqk,qhd->khd", probs_low, grad_heads, preferred_element_type=f32)
    grad_probs = jnp.einsum("qhd,khd->hqk", grad_heads, val_heads, preferred_element_type=f32)
    inner_sum = jnp.sum(grad_probs * probs_all, axis=-1, keepdims=True)
    grad_scores = (probs_all * (grad_probs - inner_sum)).astype(bf16)
    grad_query = jnp.einsum("hqk,khd->qhd", grad_scores, key_heads, preferred_element_type=f32) * scaling
    grad_keys = jnp.einsum("hqk,qhd->khd", grad_scores, query_heads, preferred_element_type=f32) * scaling
    return (
        grad_query.astype(bf16).reshape(queries.shape),
        grad_keys.reshape(key_rows.shape),
        grad_vals.reshape(val_rows.shape),
    )


def tree_mask(parents, block_len, hops_back, logical_dev):
    blocks_dev = parents.shape[0]
    group = hops_back + 1
    tree_blocks = TRUNK_BLKS + BRANCHES * (1 + LEAVES)
    total_blocks = lax.axis_size("dp") * blocks_dev
    lead_blocks = group // 2 * blocks_dev
    parent_log = jnp.where(parents >= 0, (parents - lead_blocks) % total_blocks, -1)
    query_block = logical_dev * blocks_dev + jnp.arange(blocks_dev, dtype=jnp.int32)
    key_block = (logical_dev - hops_back) * blocks_dev + jnp.arange((hops_back + 1) * blocks_dev, dtype=jnp.int32)
    tree_start = (query_block // tree_blocks * tree_blocks)[:, None]
    query_col = query_block[:, None]
    key_row = key_block[None, :]
    earlier = (
        (key_row >= tree_start)
        & (key_row < query_col)
        & ((key_row - tree_start < TRUNK_BLKS) | (key_row == parent_log[:, None]))
    )
    same_block = key_row == query_col
    positions = jnp.arange(block_len, dtype=jnp.int32)
    causal = positions[None, :] <= positions[:, None]
    allowed = earlier[:, None, :, None] | same_block[:, None, :, None] & causal[None, :, None, :]
    return allowed.reshape(blocks_dev * block_len, (hops_back + 1) * blocks_dev * block_len)


def xor_route(axis, bit):
    return [(i, i ^ bit) for i in range(lax.axis_size(axis))]


def sibling(x):
    return lax.ppermute(x, "tensor", xor_route("tensor", 1))


def across(x):
    return lax.ppermute(x, "tensor", xor_route("tensor", 2))


def pick(x, index, axis):
    return lax.dynamic_index_in_dim(x, index, axis, False)


def halve(partial, low_bit):
    rows = partial.shape[0] // 4
    parts = partial.reshape(2, 2, rows, partial.shape[1])
    kept = pick(parts, low_bit, 1)
    sent = pick(parts, 1 - low_bit, 1).astype(bf16)
    return kept + sibling(sent).astype(f32)


def reduce_half(partial, low_bit):
    chip = halve(partial, low_bit).astype(bf16)
    return chip.astype(f32) + across(chip).astype(f32)


def reduce_own(partial, low_bit, high_bit):
    chip = halve(partial, low_bit)
    sent = pick(chip, 1 - high_bit, 0).astype(bf16)
    return pick(chip, high_bit, 0) + across(sent).astype(f32)


def spread_half(half, low_bit):
    other = sibling(half)
    even = jnp.where(low_bit == 0, half, other)
    odd = jnp.where(low_bit == 0, other, half)
    return jnp.stack([even, odd], axis=1).reshape(-1, half.shape[-1])


def gather_dp(x, groups=None):
    count = lax.axis_size("dp") if groups is None else len(groups[0])
    copies = jnp.broadcast_to(x[None], (count,) + x.shape)
    return lax.all_to_all(copies, "dp", 0, 0, axis_index_groups=groups)


def scatter_dp(full):
    count = lax.axis_size("dp")
    parts = full.astype(bf16).reshape(count, full.shape[0] // count, full.shape[1])
    return jnp.sum(lax.all_to_all(parts, "dp", 0, 0).astype(f32), axis=0)


def on_device(
    tokens_in, grad_out, enc_states, parents, tree_ids, timesteps, time_table, norm_self,
    w_query, w_key, w_value, w_out, norm_cross, c_query, c_key, c_value, c_out, norm_ffn,
    w_hidden, w_back,
):
    count = lax.axis_size("dp")
    tensor = lax.axis_size("tensor")
    local_heads = HEADS // tensor
    blocks_dev = parents.shape[0]
    group = (TRUNK_BLKS + BRANCHES * (1 + LEAVES)) // blocks_dev
    hops_back = group - 1
    me = lax.axis_index("tensor")
    low_bit, high_bit = me % 2, me // 2
    logical_dev = (lax.axis_index("dp") - group // 2) % count
    trees = timesteps.shape[0]
    width = tokens_in.shape[1]
    shard = norm_self.shape[0]
    groups = [
        [(tree * group + member + group // 2) % count for member in range(group)]
        for tree in range(count // group)
    ]
    steps_hot = (jnp.arange(time_table.shape[0], dtype=jnp.int32)[None, :] == timesteps[:, None]).astype(bf16)
    table_rows = mm(steps_hot, time_table).astype(bf16)
    small = jnp.concatenate([norm_self[None], norm_cross[None], norm_ffn[None], table_rows], axis=0)
    qkv_cols = 3 * w_query.shape[1]
    small_rows = -(-small.shape[0] // 16) * 16
    small = jnp.pad(small, ((0, small_rows - small.shape[0]), (0, qkv_cols - shard)))
    first = gather_dp(jnp.concatenate([w_query, w_key, w_value], axis=1))
    small_all = gather_dp(small)
    both = lax.all_gather(jnp.stack([tokens_in, grad_out]), "tensor", axis=1)
    enc_tree = gather_dp(enc_states, groups).reshape(-1, width)
    second = gather_dp(jnp.concatenate([w_out.T, c_query, c_key, c_value, c_out.T], axis=1)).reshape(width, -1)
    third = gather_dp(jnp.concatenate([w_hidden, w_back.T], axis=1)).reshape(width, -1)
    head_cols = w_query.shape[1]
    qkv_full = first.reshape(width, qkv_cols)
    rows_all = small_all[:, :, :shard].transpose(1, 0, 2).reshape(small_rows, width).astype(f32)
    gain_self, gain_cross, gain_ffn = rows_all[0:1], rows_all[1:2], rows_all[2:3]
    tree_index = tree_ids[0]
    tree_hot = jnp.arange(trees, dtype=jnp.int32) == tree_index
    step_id = jnp.sum(jnp.where(tree_hot, timesteps, 0))
    time_row = jnp.sum(jnp.where(tree_hot[:, None], rows_all[3 : 3 + trees], 0.0), axis=0, keepdims=True)
    out_t, cq, ck, cv, co_t = [second[:, i * head_cols : (i + 1) * head_cols] for i in range(5)]
    hidden_cols = w_hidden.shape[1]
    up, down_t = third[:, :hidden_cols], third[:, hidden_cols:]
    resid_all = both[0].astype(f32) + time_row
    act_self, inv_self, normed_self = layer_norm(resid_all, gain_self)
    act_self = act_self.astype(bf16).reshape(-1, width)
    rows_own = tokens_in.shape[0]
    resid_half = pick(resid_all.reshape(2, 2, rows_own, width), low_bit, 1)
    projected = mm(act_self, qkv_full).astype(bf16)
    queries = projected[:, :head_cols]
    local_kv = projected[:, head_cols:]
    token_rows = act_self.shape[0]

    def later(distance):
        return [
            ((l + group // 2) % count, (l + distance + group // 2) % count)
            for l in range(count)
            if l % group + distance < group
        ]

    earlier = [lax.ppermute(local_kv, "dp", later(distance)) for distance in range(hops_back, 0, -1)]
    kv_all = jnp.concatenate(earlier + [local_kv], axis=0)
    key_all, val_all = kv_all[:, :head_cols], kv_all[:, head_cols:]
    allowed = tree_mask(parents, token_rows // blocks_dev, hops_back, logical_dev)
    attn_mixed, lse_self = attend(queries, key_all, val_all, allowed, local_heads)
    attn_low = attn_mixed.astype(bf16)
    resid_mid = resid_half + reduce_half(mm_nt(attn_low, out_t), low_bit)
    act_half, inv_cross, normed_cross = layer_norm(resid_mid, gain_cross)
    act_cross = spread_half(act_half.astype(bf16), low_bit)
    cross_queries = mm(act_cross, cq).astype(bf16)
    enc_keys = mm(enc_tree, ck).astype(bf16)
    enc_vals = mm(enc_tree, cv).astype(bf16)
    cross_mixed, lse_cross = attend(cross_queries, enc_keys, enc_vals, None, local_heads)
    cross_low = cross_mixed.astype(bf16)
    resid_ffn = resid_mid + reduce_half(mm_nt(cross_low, co_t), low_bit)
    act_half, inv_ffn, normed_ffn = layer_norm(resid_ffn, gain_ffn)
    act_ffn = spread_half(act_half.astype(bf16), low_bit)
    hidden_pre = mm(act_ffn, up)
    hidden_act, gelu_back = jax.vjp(gelu_exact, hidden_pre)
    hidden_low = hidden_act.astype(bf16)
    grad_top = both[1].reshape(-1, width)
    grad_hidden = mm(grad_top, down_t)
    grad_pre = gelu_back(grad_hidden)[0].astype(bf16)
    grad_act_ffn = reduce_half(mm_nt(grad_pre, up), low_bit)
    output = (
        pick(resid_ffn, high_bit, 0) + reduce_own(mm_nt(hidden_low, down_t), low_bit, high_bit)
    ).astype(bf16)
    ffn_sums = scatter_dp(jnp.concatenate([mm_tn(act_ffn, grad_pre), mm_tn(grad_top, hidden_low)], axis=1))
    grad_gain_ffn = jnp.sum(pick(grad_act_ffn * normed_ffn, high_bit, 0), axis=0)
    grad_half = pick(both[1].reshape(2, 2, rows_own, width), low_bit, 1).astype(f32)
    grad_resid_ffn = grad_half + layer_norm_back(grad_act_ffn, normed_ffn, inv_ffn, gain_ffn)
    grad_cross_top = spread_half(grad_resid_ffn.astype(bf16), low_bit)
    grad_cross_mixed = mm(grad_cross_top, co_t).astype(bf16)
    grad_cq, grad_enc_keys, grad_enc_vals = attend_back(
        cross_queries, enc_keys, enc_vals, None, local_heads, lse_cross, grad_cross_mixed
    )
    grad_act_cross = reduce_half(mm_nt(grad_cq, cq), low_bit)
    grad_gain_cross = jnp.sum(pick(grad_act_cross * normed_cross, high_bit, 0), axis=0)
    grad_resid_mid = grad_resid_ffn + layer_norm_back(grad_act_cross, normed_cross, inv_cross, gain_cross)
    enc_parts = jnp.concatenate([grad_enc_keys, grad_enc_vals], axis=1).astype(bf16)
    enc_parts = enc_parts.reshape(group, -1, 2 * head_cols)
    enc_sum = jnp.sum(
        lax.all_to_all(enc_parts, "dp", 0, 0, axis_index_groups=groups).astype(f32), axis=0
    ).astype(bf16)
    grad_kv_enc = mm_tn(enc_states, enc_sum)
    enc_part = (mm_nt(enc_sum[:, :head_cols], ck) + mm_nt(enc_sum[:, head_cols:], cv)).astype(bf16)
    enc_part = enc_part.astype(f32) + sibling(enc_part).astype(f32)
    enc_chip = enc_part.astype(bf16)
    grad_enc = enc_chip.astype(f32) + across(enc_chip).astype(f32)
    cross_sums = scatter_dp(
        jnp.concatenate([mm_tn(act_cross, grad_cq), grad_kv_enc, mm_tn(grad_cross_top, cross_low)], axis=1)
    )
    grad_self_top = spread_half(grad_resid_mid.astype(bf16), low_bit)
    grad_attn = mm(grad_self_top, out_t).astype(bf16)
    grad_query, grad_keys, grad_vals = attend_back(
        queries, key_all, val_all, allowed, local_heads, lse_self, grad_attn
    )
    grad_kv = jnp.concatenate([grad_keys, grad_vals], axis=1).reshape(group, token_rows, 2 * head_cols)
    total_kv = grad_kv[hops_back]
    for distance in range(hops_back, 0, -1):
        back = [(b, a) for a, b in later(distance)]
        total_kv = total_kv + lax.ppermute(
            grad_kv[hops_back - distance].astype(bf16), "dp", back
        ).astype(f32)
    grad_qkv = jnp.concatenate([grad_query, total_kv.astype(bf16)], axis=1)
    self_sums = scatter_dp(jnp.concatenate([mm_tn(act_self, grad_qkv), mm_tn(grad_self_top, attn_low)], axis=1))
    grad_act_self = reduce_own(mm_nt(grad_qkv, qkv_full), low_bit, high_bit)
    own_normed, own_inv = pick(normed_self, me, 0), pick(inv_self, me, 0)
    grad_gain_self = jnp.sum(grad_act_self * own_normed, axis=0)
    grad_in = pick(grad_resid_mid, high_bit, 0) + layer_norm_back(grad_act_self, own_normed, own_inv, gain_self)
    vectors = jnp.stack(
        [
            grad_gain_self, grad_gain_cross, grad_gain_ffn, jnp.sum(grad_in, axis=0),
            jnp.full((width,), step_id.astype(f32)),
        ]
    )
    vectors = vectors.reshape(5, count, 1, shard).transpose(1, 2, 0, 3)
    vectors = jnp.broadcast_to(vectors, (count, tensor, 5, shard)).reshape(count * tensor, 5, shard)
    received = lax.all_to_all(vectors, ("dp", "tensor"), 0, 0)
    gain_sums = jnp.sum(received[:, :3], axis=0)
    table_hot = jnp.arange(time_table.shape[0], dtype=jnp.int32)[:, None, None] == received[:, 4].astype(jnp.int32)[None]
    grad_table = jnp.sum(jnp.where(table_hot, received[:, 3][None], 0.0), axis=1)
    gq, gk, gv, go = [self_sums[:, i * head_cols : (i + 1) * head_cols] for i in range(4)]
    gcq, gck, gcv, gco = [cross_sums[:, i * head_cols : (i + 1) * head_cols] for i in range(4)]
    return (
        output, grad_in, grad_enc, grad_table, gain_sums[0], gq, gk, gv, go.T, gain_sums[1],
        gcq, gck, gcv, gco.T, gain_sums[2], ffn_sums[:, :hidden_cols], ffn_sums[:, hidden_cols:].T,
    )


def solution(mesh):
    rows, cols, repl = P(("dp", "tensor"), None), P("dp", "tensor"), P("tensor", "dp")
    in_specs = (
        rows, rows, P("dp", None), P("dp"), P("dp"), P(), P(None, "dp"), P("dp"), cols, cols, cols, repl,
        P("dp"), cols, cols, cols, repl, P("dp"), cols, repl,
    )
    out_specs = (
        rows, rows, P("dp", None), P(None, "dp"), P("dp"), cols, cols, cols, repl, P("dp"), cols, cols, cols,
        repl, P("dp"), cols, repl,
    )
    return jax.shard_map(on_device, mesh=mesh, in_specs=in_specs, out_specs=out_specs, check_vma=False)
```

time: 1450 us -> 352 us (0.24)
  waiting for transfers between devices: 799 us -> 95.4 us
  blocking collectives: 462 us -> 0 us
  starting transfers between devices: 29.9 us -> 82.4 us
    reduce_scatter x14 -> x0, waiting for transfers between devices: 600 us -> none  [the longest x6 81.6 us: fold_back(): return lax.psum_scatter(row_vals, 'tensor', scatter_dimension=0, tiled=True)]
    all_gather x17 -> x0, blocking collectives: 406 us -> none  [the longest x6 46.3 us: spread(): return lax.all_gather(row_vals, 'tensor', axis=0, tiled=True)]
    unnamed x21 -> x1, waiting for transfers between devices: 170 us -> 0.02 us
    all_to_all x0 -> x10, starting transfers between devices: none -> 58.2 us  [the longest x5 35.2 us: gather_dp(): return lax.all_to_all(copies, 'dp', 0, 0, axis_index_groups=groups)]
    unnamed x2 -> x0, blocking collectives: 45.3 us -> none
    all_to_all x0 -> x10, waiting for transfers between devices: none -> 39.2 us  [the longest x3 19.4 us: scatter_dp(): return jnp.sum(lax.all_to_all(parts, 'dp', 0, 0).astype(f32), axis=0)]
    ppermute x18 -> x24, waiting for transfers between devices: 25 us -> 45.8 us  [the longest x7 27.6 us: across(): return lax.ppermute(x, 'tensor', xor_route('tensor', 2))]
    dot_general x27 -> x26, matrix products: 29.4 us -> 28 us  [the longest x9 14.2 us: mm(): return jnp.dot(a, b, preferred_element_type=f32)]
  transfers between devices with their start and end apart: 36 -> 35, of which waited for: 21 -> 17; matrix products, arithmetic and copies ran while one was open for 2% -> 31% of each run, Pallas kernels for 0% -> 0%
where the time goes in v1:
time: 352 us; the launch traced here: 347 us
  waiting for transfers between devices  95.4 us (27%)
  starting transfers between devices  82.4 us (23%)
  matrix products  56.1 us (16%)
  other arithmetic  51.4 us (15%)
  local copies, waits for them, and re-layouts  44.7 us (13%)
  between operations  16.7 us (5%)
    all_to_all x5, starting transfers between devices, gather_dp(): return lax.all_to_all(copies, 'dp', 0, 0, axis_index_groups=groups)  35.2 us
    ppermute x7, waiting for transfers between devices, across(): return lax.ppermute(x, 'tensor', xor_route('tensor', 2))  27.6 us
    all_to_all x3, waiting for transfers between devices, scatter_dp(): return jnp.sum(lax.all_to_all(parts, 'dp', 0, 0).astype(f32), axis=0)  19.4 us
    unnamed x161, local copies, waits for them, and re-layouts  16.5 us
    dot_general x9, matrix products, mm(): return jnp.dot(a, b, preferred_element_type=f32)  14.2 us
    all_to_all x5, waiting for transfers between devices, gather_dp(): return lax.all_to_all(copies, 'dp', 0, 0, axis_index_groups=groups)  12.4 us
    all_to_all x3, starting transfers between devices, scatter_dp(): return jnp.sum(lax.all_to_all(parts, 'dp', 0, 0).astype(f32), axis=0)  12.2 us
    ppermute x3, waiting for transfers between devices, on_device(): lax.ppermute(local_kv, 'dp', later(distance))  12.1 us
  transfers between devices with their start and end apart: 35, of which 17 were waited for; matrix products, arithmetic and copies ran while one was open for 31% of the time, Pallas kernels for 0%

profile of v1, /device:TPU:0, one launch (start us, length us, event | category | flops | bytes accessed | tf_op | source)
XLA Modules:
  0.0 346.7 jit_solution(5050754871419236448)
XLA Ops:
  10.1 7.3 %all-to-all-start = ((bf16[8,16,384]{2,1,0:T(8,128)(2,1)}), bf16[8,16,384]{2,1,0:T(8,128)(2,1)S(1)}, u32[]{:S(2)}, u32[]{:S(2)}) async-start(bf16[8,16,384]{2,1,0:T(8,128)(2,1)} %broadcast_in_dim.68), calls=%async_computation | async-start | bytes 196608 | tf_op jit(solution)/shard_map/all_to_all | solution.py:162
  19.6 4.9 %all-to-all-done = bf16[8,16,384]{2,1,0:T(8,128)(2,1)S(1)} async-done(((bf16[8,16,384]{2,1,0:T(8,128)(2,1)}), bf16[8,16,384]{2,1,0:T(8,128)(2,1)S(1)}, u32[]{:S(2)}, u32[]{:S(2)}) %all-to-all-start) | async-done | bytes 98336 | tf_op jit(solution)/shard_map/all_to_all | solution.py:162
  29.6 10.3 %all-gather.3.cloned.1.call-done = bf16[2,640,512]{2,1,0:T(8,128)(2,1)} async-done(((bf16[2,160,512]{2,1,0:T(8,128)(2,1)}), bf16[2,640,512]{2,1,0:T(8,128)(2,1)}) %all-gather.3.cloned.1.call-update) | async-done | bytes 1310736 | tf_op jit(solution)/shard_map/all_gather | solution.py:200
  45.4 5.5 %all-to-all-start.2 = ((bf16[8,64,640]{2,1,0:T(8,128)(2,1)}), bf16[8,64,640]{2,1,0:T(8,128)(2,1)S(1)}, u32[]{:S(2)}, u32[]{:S(2)}) async-start(bf16[8,64,640]{2,1,0:T(8,128)(2,1)} %broadcast_in_dim.73), calls=%async_computation.2 | async-start | bytes 1310720 | tf_op jit(solution)/shard_map/all_to_all | solution.py:162
  62.8 12.1 %collective-permute-done.2 = bf16[640,256]{0,1:T(8,128)(2,1)S(1)} collective-permute-done((bf16[640,256]{0,1:T(8,128)(2,1)S(1)}, bf16[640,256]{0,1:T(8,128)(2,1)S(1)}, u32[]{:S(2)}, u32[]{:S(2)}) %collective-permute-start.2) | collective-permute-done | bytes 327712 | tf_op jit(solution)/shard_map/ppermute | solution.py:232
  94.5 11.4 %all-to-all-start.3 = ((bf16[4,64,512]{2,1,0:T(8,128)(2,1)}), bf16[4,64,512]{2,1,0:T(8,128)(2,1)S(1)}, u32[]{:S(2)}, u32[]{:S(2)}) async-start(bf16[4,64,512]{2,1,0:T(8,128)(2,1)} %broadcast_in_dim.74), calls=%async_computation.3 | async-start | bytes 524288 | tf_op jit(solution)/shard_map/all_to_all | solution.py:162
  116.5 7.6 %all-to-all-start.4 = ((bf16[8,64,1024]{2,1,0:T(8,128)(2,1)}), bf16[8,64,1024]{2,1,0:T(8,128)(2,1)}, u32[]{:S(2)}, u32[]{:S(2)}) async-start(bf16[8,64,1024]{2,1,0:T(8,128)(2,1)} %broadcast_in_dim.75), calls=%async_computation.4 | async-start | bytes 2097152 | tf_op jit(solution)/shard_map/all_to_all | solution.py:162
  130.8 7.3 %collective-permute-done.7 = bf16[2,160,512]{2,1,0:T(8,128)(2,1)} collective-permute-done((bf16[2,160,512]{2,1,0:T(8,128)(2,1)S(1)}, bf16[2,160,512]{2,1,0:T(8,128)(2,1)}, u32[]{:S(2)}, u32[]{:S(2)}) %collective-permute-start.7) | collective-permute-done | bytes 327712 | tf_op jit(solution)/shard_map/ppermute | solution.py:126
  144.1 6.4 %all-to-all-done.4 = bf16[8,64,1024]{2,1,0:T(8,128)(2,1)} async-done(((bf16[8,64,1024]{2,1,0:T(8,128)(2,1)}), bf16[8,64,1024]{2,1,0:T(8,128)(2,1)}, u32[]{:S(2)}, u32[]{:S(2)}) %all-to-all-start.4) | async-done | bytes 1048608 | tf_op jit(solution)/shard_map/all_to_all | solution.py:162
  150.5 8.6 %multiply_convert_fusion.2 = (bf16[640,512]{1,0:T(8,128)(2,1)S(1)}, f32[640,512]{1,0:T(8,128)S(1)}, f32[640,512]{1,0:T(8,128)S(1)}) fusion(bf16[640,512]{1,0:T(8,128)(2,1)} %bitcast.367, bf16[512,1024]{1,0:T(8,128)(2,1)} %bitcast.43), kind=kOutput, calls=%fused_computation.32 | convolution fusion | flops 356843520 | bytes 4456448 | tf_op jit(solution)/shard_map/dot_general | solution.py:35
  175.5 8.3 %collective-permute-done.12 = bf16[2,160,512]{2,1,0:T(8,128)(2,1)S(1)} collective-permute-done((bf16[2,160,512]{2,1,0:T(8,128)(2,1)S(1)}, bf16[2,160,512]{2,1,0:T(8,128)(2,1)S(1)}, u32[]{:S(2)}, u32[]{:S(2)}) %collective-permute-start.12) | collective-permute-done | bytes 327712 | tf_op jit(solution)/shard_map/ppermute | solution.py:126
  195.3 6.2 %all-to-all-start.5 = ((bf16[4,64,256]{2,1,0:T(8,128)(2,1)}), bf16[4,64,256]{2,1,0:T(8,128)(2,1)}, u32[]{:S(2)}, u32[]{:S(2)}) async-start(bf16[4,64,256]{2,1,0:T(8,128)(2,1)} %pad_maximum_fusion.11), calls=%async_computation.5 | async-start | bytes 262144 | tf_op jit(solution)/shard_map/all_to_all | solution.py:274
  205.4 4.5 %all-to-all-start.9 = ((bf16[8,64,1024]{2,1,0:T(8,128)(2,1)}), bf16[8,64,1024]{2,1,0:T(8,128)(2,1)}, u32[]{:S(2)}, u32[]{:S(2)}) async-start(bf16[8,64,1024]{2,1,0:T(8,128)(2,1)} %pad_maximum_fusion.2), calls=%async_computation.9 | async-start | bytes 2097152 | tf_op jit(solution)/shard_map/all_to_all | solution.py:168
  217.6 6.5 %collective-permute-done.15 = bf16[2,160,512]{2,1,0:T(8,128)(2,1)S(1)} collective-permute-done((bf16[2,160,512]{2,1,0:T(8,128)(2,1)S(1)}, bf16[2,160,512]{2,1,0:T(8,128)(2,1)S(1)}, u32[]{:S(2)}, u32[]{:S(2)}) %collective-permute-start.15) | collective-permute-done | bytes 327712 | tf_op jit(solution)/shard_map/ppermute | solution.py:126
  227.8 7.8 %all-to-all-done.9 = bf16[8,64,1024]{2,1,0:T(8,128)(2,1)} async-done(((bf16[8,64,1024]{2,1,0:T(8,128)(2,1)}), bf16[8,64,1024]{2,1,0:T(8,128)(2,1)}, u32[]{:S(2)}, u32[]{:S(2)}) %all-to-all-start.9) | async-done | bytes 1048608 | tf_op jit(solution)/shard_map/all_to_all | solution.py:168
  243.4 6.0 %fusion.2 = f32[2,64,2560]{2,1,0:T(8,128)S(1)} fusion(bf16[640,2,64]{0,2,1:T(8,128)(2,1)S(1)} %bitcast.376, f32[2,640,2560]{2,1,0:T(8,128)} %copy-done.2, f32[2,640]{1,0:T(2,128)S(1)} %log_add_fusion), kind=kOutput, calls=%fused_computation.9 | convolution fusion | flops 425984000 | bytes 14586880 | tf_op jit(solution)/shard_map/hqk,qhd->khd/dot_general | solution.py:80
  249.5 8.9 %multiply_reduce_fusion = (f32[2,640]{1,0:T(2,128)S(1)}, f32[2,640,2560]{2,1,0:T(8,128)}) fusion(f32[2,640,2560]{2,1,0:T(8,128)} %copy-done.2, f32[2,640]{1,0:T(2,128)S(1)} %log_add_fusion, bf16[640,2,64]{0,2,1:T(8,128)(2,1)S(1)} %bitcast.377, bf16[2560,2,64]{0,2,1:T(8,128)(2,1)S(1)} %bitcast.362), kind=kOutput, calls=%fused_computation.1 | convolution fusion | flops 429259520 | bytes 27043840 | tf_op jit(solution)/shard_map/qhd,khd->hqk/dot_general | solution.py:81
  258.8 9.9 %multiply_convert_fusion = bf16[2,640,2560]{2,1,0:T(8,128)(2,1)S(1)} fusion(f32[2,640,2560]{2,1,0:T(8,128)} %get-tuple-element.86, f32[2,640,2560]{2,1,0:T(8,128)} %copy-done.2, f32[2,640]{1,0:T(2,128)S(1)} %get-tuple-element.85, f32[2,640]{1,0:T(2,128)S(1)} %log_add_fusion), kind=kLoop, calls=%fused_computation | loop fusion | flops 13107200 | bytes 32778240 | tf_op jit(solution)/shard_map/convert_element_type | solution.py:83
  276.0 6.5 %collective-permute-start.19 = (bf16[640,256]{1,0:T(8,128)(2,1)}, bf16[640,256]{1,0:T(8,128)(2,1)}, u32[]{:S(2)}, u32[]{:S(2)}) collective-permute-start(bf16[640,256]{1,0:T(8,128)(2,1)} %get-tuple-element.47), channel_id=1, source_target_pairs={{12,8},{16,12},{20,16},{28,24},{0,28},{4,0},{13,9},{17,13},{21,17}... | collective-permute-start | bytes 983048 | tf_op jit(solution)/shard_map/ppermute | solution.py:293
  284.8 4.9 %fusion.19 = bf16[2,64,640]{2,1,0:T(8,128)(2,1)S(1)} fusion(bf16[2560,2,64]{0,2,1:T(8,128)(2,1)S(1)} %bitcast.364, bf16[2,640,2560]{2,1,0:T(8,128)(2,1)} %copy-done.3), kind=kOutput, calls=%fused_computation.65 | convolution fusion | flops 419594240 | bytes 7372800 | tf_op jit(solution)/shard_map/hqk,khd->qhd/dot_general | solution.py:84
  301.2 5.1 %collective-permute-done.21 = bf16[160,512]{1,0:T(8,128)(2,1)S(1)} collective-permute-done((bf16[160,512]{1,0:T(8,128)(2,1)S(1)}, bf16[160,512]{1,0:T(8,128)(2,1)S(1)}, u32[]{:S(2)}, u32[]{:S(2)}) %collective-permute-start.21) | collective-permute-done | bytes 163872 | tf_op jit(solution)/shard_map/ppermute | solution.py:126
  308.4 4.7 %all-to-all-start.6 = ((f32[32,1,320]{2,1,0:T(1,128)}), f32[32,1,320]{2,1,0:T(1,128)S(1)}, u32[]{:S(2)}, u32[]{:S(2)}) async-start(f32[32,1,320]{2,1,0:T(1,128)} %reshape.611), calls=%async_computation.6 | async-start | bytes 98304 | tf_op jit(solution)/shard_map/all_to_all | solution.py:310
  314.0 6.5 %all-to-all-done.6 = f32[32,1,320]{2,1,0:T(1,128)S(1)} async-done(((f32[32,1,320]{2,1,0:T(1,128)}), f32[32,1,320]{2,1,0:T(1,128)S(1)}, u32[]{:S(2)}, u32[]{:S(2)}) %all-to-all-start.6) | async-done | bytes 40992 | tf_op jit(solution)/shard_map/all_to_all | solution.py:310
  327.3 11.6 %all-to-all-done.7 = bf16[8,64,512]{2,1,0:T(8,128)(2,1)S(1)} async-done(((bf16[8,64,512]{2,1,0:T(8,128)(2,1)}), bf16[8,64,512]{2,1,0:T(8,128)(2,1)S(1)}, u32[]{:S(2)}, u32[]{:S(2)}) %all-to-all-start.7) | async-done | bytes 524320 | tf_op jit(solution)/shard_map/all_to_all | solution.py:168
  (390 shorter events, 151.3 us)
Async XLA Ops:
  10.1 14.4 %all-to-all-start = ((bf16[8,16,384]{2,1,0:T(8,128)(2,1)}), bf16[8,16,384]{2,1,0:T(8,128)(2,1)S(1)}, u32[]{:S(2)}, u32[]{:S(2)}) async-start(bf16[8,16,384]{2,1,0:T(8,128)(2,1)} %broadcast_in_dim.68), calls=%async_computation | async-start | bytes 196608 | tf_op jit(solution)/shard_map/all_to_all | solution.py:162
  17.4 22.6 %all-gather.3.cloned.1.call-start = ((), (), s32[]{:S(2)}) async-start(), calls=%async_computation.10 | async-start | bytes 1638400 | tf_op jit(solution)/shard_map/all_gather | solution.py:200
  25.3 19.1 %all-to-all-start.1 = ((bf16[8,64,384]{2,1,0:T(8,128)(2,1)}), bf16[8,64,384]{2,1,0:T(8,128)(2,1)S(1)}, u32[]{:S(2)}, u32[]{:S(2)}) async-start(bf16[8,64,384]{2,1,0:T(8,128)(2,1)} %broadcast_in_dim.70), calls=%async_computation.1 | async-start | bytes 786432 | tf_op jit(solution)/shard_map/all_to_all | solution.py:162
  45.4 43.4 %all-to-all-start.2 = ((bf16[8,64,640]{2,1,0:T(8,128)(2,1)}), bf16[8,64,640]{2,1,0:T(8,128)(2,1)S(1)}, u32[]{:S(2)}, u32[]{:S(2)}) async-start(bf16[8,64,640]{2,1,0:T(8,128)(2,1)} %broadcast_in_dim.73), calls=%async_computation.2 | async-start | bytes 1310720 | tf_op jit(solution)/shard_map/all_to_all | solution.py:162
  51.5 23.4 %collective-permute-start.2 = (bf16[640,256]{0,1:T(8,128)(2,1)S(1)}, bf16[640,256]{0,1:T(8,128)(2,1)S(1)}, u32[]{:S(2)}, u32[]{:S(2)}) collective-permute-start(bf16[640,256]{0,1:T(8,128)(2,1)S(1)} %slice.185), channel_id=1, source_target_pairs={{8,12},{12,16},{16,20},{24,28},{28,0},{0,4},{9,13},{13,17},{17,21}... | collective-permute-start | bytes 983048 | tf_op jit(solution)/shard_map/ppermute | solution.py:232
  55.4 19.5 %collective-permute-start.1 = (bf16[640,256]{0,1:T(8,128)(2,1)S(1)}, bf16[640,256]{0,1:T(8,128)(2,1)S(1)}, u32[]{:S(2)}, u32[]{:S(2)}) collective-permute-start(bf16[640,256]{0,1:T(8,128)(2,1)S(1)} %slice.185), channel_id=1, source_target_pairs={{8,16},{12,20},{24,0},{28,4},{9,17},{13,21},{25,1},{29,5},{10,18},... | collective-permute-start | bytes 983048 | tf_op jit(solution)/shard_map/ppermute | solution.py:232
  56.7 18.2 %collective-permute-start = (bf16[640,256]{0,1:T(8,128)(2,1)S(1)}, bf16[640,256]{0,1:T(8,128)(2,1)}, u32[]{:S(2)}, u32[]{:S(2)}) collective-permute-start(bf16[640,256]{0,1:T(8,128)(2,1)S(1)} %slice.185), channel_id=1, source_target_pairs={{8,20},{24,4},{9,21},{25,5},{10,22},{26,6},{11,23},{27,7}} | collective-permute-start | bytes 983048 | tf_op jit(solution)/shard_map/ppermute | solution.py:232
  93.2 12.8 %collective-permute-start.4 = (bf16[2,160,512]{2,1,0:T(8,128)(2,1)S(1)}, bf16[2,160,512]{2,1,0:T(8,128)(2,1)S(1)}, u32[]{:S(2)}, u32[]{:S(2)}) collective-permute-start(bf16[2,160,512]{2,1,0:T(8,128)(2,1)S(1)} %fusion.45), channel_id=1, source_target_pairs={{0,2},{1,3},{2,0},{3,1},{4,6},{5,7},{6,4},{7,5},{8,10},{9,11},{10,... | collective-permute-start | bytes 983048 | tf_op jit(solution)/shard_map/ppermute | solution.py:126
  94.5 16.0 %all-to-all-start.3 = ((bf16[4,64,512]{2,1,0:T(8,128)(2,1)}), bf16[4,64,512]{2,1,0:T(8,128)(2,1)S(1)}, u32[]{:S(2)}, u32[]{:S(2)}) async-start(bf16[4,64,512]{2,1,0:T(8,128)(2,1)} %broadcast_in_dim.74), calls=%async_computation.3 | async-start | bytes 524288 | tf_op jit(solution)/shard_map/all_to_all | solution.py:162
  115.3 11.5 %collective-permute-start.6 = (bf16[2,160,512]{2,1,0:T(8,128)(2,1)}, bf16[2,160,512]{2,1,0:T(8,128)(2,1)}, u32[]{:S(2)}, u32[]{:S(2)}) collective-permute-start(bf16[2,160,512]{2,1,0:T(8,128)(2,1)} %fusion.62), channel_id=1, source_target_pairs={{0,1},{1,0},{2,3},{3,2},{4,5},{5,4},{6,7},{7,6},{8,9},{9,8},{10,11... | collective-permute-start | bytes 983048 | tf_op jit(solution)/shard_map/ppermute | solution.py:122
  116.5 34.0 %all-to-all-start.4 = ((bf16[8,64,1024]{2,1,0:T(8,128)(2,1)}), bf16[8,64,1024]{2,1,0:T(8,128)(2,1)}, u32[]{:S(2)}, u32[]{:S(2)}) async-start(bf16[8,64,1024]{2,1,0:T(8,128)(2,1)} %broadcast_in_dim.75), calls=%async_computation.4 | async-start | bytes 2097152 | tf_op jit(solution)/shard_map/all_to_all | solution.py:162
  128.2 9.9 %collective-permute-start.7 = (bf16[2,160,512]{2,1,0:T(8,128)(2,1)S(1)}, bf16[2,160,512]{2,1,0:T(8,128)(2,1)}, u32[]{:S(2)}, u32[]{:S(2)}) collective-permute-start(bf16[2,160,512]{2,1,0:T(8,128)(2,1)S(1)} %fusion.44), channel_id=1, source_target_pairs={{0,2},{1,3},{2,0},{3,1},{4,6},{5,7},{6,4},{7,5},{8,10},{9,11},{10,... | collective-permute-start | bytes 983048 | tf_op jit(solution)/shard_map/ppermute | solution.py:126
  173.2 10.6 %collective-permute-start.12 = (bf16[2,160,512]{2,1,0:T(8,128)(2,1)S(1)}, bf16[2,160,512]{2,1,0:T(8,128)(2,1)S(1)}, u32[]{:S(2)}, u32[]{:S(2)}) collective-permute-start(bf16[2,160,512]{2,1,0:T(8,128)(2,1)S(1)} %fusion.39), channel_id=1, source_target_pairs={{0,2},{1,3},{2,0},{3,1},{4,6},{5,7},{6,4},{7,5},{8,10},{9,11},{10,... | collective-permute-start | bytes 983048 | tf_op jit(solution)/shard_map/ppermute | solution.py:126
  174.0 12.7 %collective-permute-start.10 = (bf16[160,512]{1,0:T(8,128)(2,1)S(1)}, bf16[160,512]{1,0:T(8,128)(2,1)S(1)}, u32[]{:S(2)}, u32[]{:S(2)}) collective-permute-start(bf16[160,512]{1,0:T(8,128)(2,1)S(1)} %fusion.77), channel_id=1, source_target_pairs={{0,2},{1,3},{2,0},{3,1},{4,6},{5,7},{6,4},{7,5},{8,10},{9,11},{10,... | collective-permute-start | bytes 491528 | tf_op jit(solution)/shard_map/ppermute | solution.py:126
  195.3 10.2 %all-to-all-start.5 = ((bf16[4,64,256]{2,1,0:T(8,128)(2,1)}), bf16[4,64,256]{2,1,0:T(8,128)(2,1)}, u32[]{:S(2)}, u32[]{:S(2)}) async-start(bf16[4,64,256]{2,1,0:T(8,128)(2,1)} %pad_maximum_fusion.11), calls=%async_computation.5 | async-start | bytes 262144 | tf_op jit(solution)/shard_map/all_to_all | solution.py:274
  205.4 30.3 %all-to-all-start.9 = ((bf16[8,64,1024]{2,1,0:T(8,128)(2,1)}), bf16[8,64,1024]{2,1,0:T(8,128)(2,1)}, u32[]{:S(2)}, u32[]{:S(2)}) async-start(bf16[8,64,1024]{2,1,0:T(8,128)(2,1)} %pad_maximum_fusion.2), calls=%async_computation.9 | async-start | bytes 2097152 | tf_op jit(solution)/shard_map/all_to_all | solution.py:168
  214.5 9.6 %collective-permute-start.15 = (bf16[2,160,512]{2,1,0:T(8,128)(2,1)S(1)}, bf16[2,160,512]{2,1,0:T(8,128)(2,1)S(1)}, u32[]{:S(2)}, u32[]{:S(2)}) collective-permute-start(bf16[2,160,512]{2,1,0:T(8,128)(2,1)S(1)} %fusion.38), channel_id=1, source_target_pairs={{0,2},{1,3},{2,0},{3,1},{4,6},{5,7},{6,4},{7,5},{8,10},{9,11},{10,... | collective-permute-start | bytes 983048 | tf_op jit(solution)/shard_map/ppermute | solution.py:126
  227.8 14.1 %collective-permute-start.16 = (bf16[2,160,512]{2,1,0:T(8,128)(2,1)S(1)}, bf16[2,160,512]{2,1,0:T(8,128)(2,1)S(1)}, u32[]{:S(2)}, u32[]{:S(2)}) collective-permute-start(bf16[2,160,512]{2,1,0:T(8,128)(2,1)S(1)} %get-tuple-element.29), channel_id=1, source_target_pairs={{0,1},{1,0},{2,3},{3,2},{4,5},{5,4},{6,7},{7,6},{8,9},{9,8},{10,11... | collective-permute-start | bytes 983048 | tf_op jit(solution)/shard_map/ppermute | solution.py:122
  235.7 63.0 %all-to-all-start.8 = ((bf16[8,64,512]{2,1,0:T(8,128)(2,1)}), bf16[8,64,512]{2,1,0:T(8,128)(2,1)}, u32[]{:S(2)}, u32[]{:S(2)}) async-start(bf16[8,64,512]{2,1,0:T(8,128)(2,1)} %pad_maximum_fusion.8), calls=%async_computation.8 | async-start | bytes 1048576 | tf_op jit(solution)/shard_map/all_to_all | solution.py:168
  274.6 17.5 %collective-permute-start.17 = (bf16[640,256]{1,0:T(8,128)(2,1)}, bf16[640,256]{1,0:T(8,128)(2,1)}, u32[]{:S(2)}, u32[]{:S(2)}) collective-permute-start(bf16[640,256]{1,0:T(8,128)(2,1)} %get-tuple-element.46), channel_id=1, source_target_pairs={{20,8},{4,24},{21,9},{5,25},{22,10},{6,26},{23,11},{7,27}} | collective-permute-start | bytes 983048 | tf_op jit(solution)/shard_map/ppermute | solution.py:293
  276.0 16.1 %collective-permute-start.19 = (bf16[640,256]{1,0:T(8,128)(2,1)}, bf16[640,256]{1,0:T(8,128)(2,1)}, u32[]{:S(2)}, u32[]{:S(2)}) collective-permute-start(bf16[640,256]{1,0:T(8,128)(2,1)} %get-tuple-element.47), channel_id=1, source_target_pairs={{12,8},{16,12},{20,16},{28,24},{0,28},{4,0},{13,9},{17,13},{21,17}... | collective-permute-start | bytes 983048 | tf_op jit(solution)/shard_map/ppermute | solution.py:293
  282.6 13.3 %collective-permute-start.18 = (bf16[640,256]{1,0:T(8,128)(2,1)}, bf16[640,256]{1,0:T(8,128)(2,1)}, u32[]{:S(2)}, u32[]{:S(2)}) collective-permute-start(bf16[640,256]{1,0:T(8,128)(2,1)} %get-tuple-element.48), channel_id=1, source_target_pairs={{16,8},{20,12},{0,24},{4,28},{17,9},{21,13},{1,25},{5,29},{18,10},... | collective-permute-start | bytes 983048 | tf_op jit(solution)/shard_map/ppermute | solution.py:293
  308.4 12.0 %all-to-all-start.6 = ((f32[32,1,320]{2,1,0:T(1,128)}), f32[32,1,320]{2,1,0:T(1,128)S(1)}, u32[]{:S(2)}, u32[]{:S(2)}) async-start(f32[32,1,320]{2,1,0:T(1,128)} %reshape.611), calls=%async_computation.6 | async-start | bytes 98304 | tf_op jit(solution)/shard_map/all_to_all | solution.py:310
  320.4 18.5 %all-to-all-start.7 = ((bf16[8,64,512]{2,1,0:T(8,128)(2,1)}), bf16[8,64,512]{2,1,0:T(8,128)(2,1)S(1)}, u32[]{:S(2)}, u32[]{:S(2)}) async-start(bf16[8,64,512]{2,1,0:T(8,128)(2,1)} %pad_maximum_fusion.7), calls=%async_computation.7 | async-start | bytes 1048576 | tf_op jit(solution)/shard_map/all_to_all | solution.py:168
  (88 other events, 456.1 us)
Sparse Core Ops, SparseCore 0:
  20.4 19.5 all-gather.2

commit v2 on v1

v2 whole, which is shorter than its diff:
```python
import jax
import jax.numpy as jnp
from jax import lax
from jax.experimental import pallas as pl
from jax.experimental.pallas import tpu as pltpu
from jax.sharding import PartitionSpec as P

HEADS = 8
TRUNK_BLKS = 8
BRANCHES = 4
LEAVES = 2
eps = 1e-05
bf16 = jnp.bfloat16
f32 = jnp.float32
i32 = jnp.int32
NEG = -1e30


def mm(a, b):
    return lax.dot_general(a, b, (((1,), (0,)), ((), ())), preferred_element_type=f32)


def mm_tn(a, b):
    return lax.dot_general(a, b, (((0,), (0,)), ((), ())), preferred_element_type=f32)


def mm_nt(a, b):
    return lax.dot_general(a, b, (((1,), (1,)), ((), ())), preferred_element_type=f32)


def normalize(v):
    centered = v - jnp.mean(v, axis=-1, keepdims=True)
    inv = lax.rsqrt(jnp.mean(centered * centered, axis=-1, keepdims=True) + eps)
    return centered * inv, inv


def norm_back(grad_act, resid, gain):
    normed, inv = normalize(resid)
    scaled = grad_act * gain
    mean_g = jnp.mean(scaled, axis=-1, keepdims=True)
    mean_gx = jnp.mean(scaled * normed, axis=-1, keepdims=True)
    return inv * (scaled - mean_g - normed * mean_gx), jnp.sum(grad_act * normed, axis=0, keepdims=True)


def shaped(shape, dtype):
    return jax.ShapeDtypeStruct(shape, dtype)


def part(array, width, index):
    return (array, (array.shape[0], width), index)


def run(body, outs, ins, scratch=()):
    arrays, specs = [], []
    for item in ins:
        if isinstance(item, tuple):
            array, block, index = item
            specs.append(pl.BlockSpec(block, lambda i, index=index: (0, index)))
        else:
            array = item
            if array.dtype == i32:
                specs.append(pl.BlockSpec(memory_space=pltpu.SMEM))
            else:
                specs.append(pl.BlockSpec(array.shape, lambda i, r=array.ndim: (0,) * r))
        arrays.append(array)
    out_specs = [pl.BlockSpec(o.shape, lambda i, r=len(o.shape): (0,) * r) for o in outs]
    return pl.pallas_call(
        body,
        grid=(1,),
        out_shape=outs,
        in_specs=specs,
        out_specs=out_specs,
        scratch_shapes=list(scratch),
        compiler_params=pltpu.CompilerParams(vmem_limit_bytes=56 * 1024 * 1024),
    )(*arrays)


def project_body(sc, half, other, w, small, act, q, kv, rows):
    turned = small[...].astype(f32).T
    ids = lax.broadcasted_iota(i32, turned.shape, 0)
    time_row = jnp.sum(jnp.where(ids == 3 + sc[4], turned, 0.0), axis=0, keepdims=True)
    rows[0:3, :] = turned[0:3]
    rows[3:4, :] = time_row
    gain = turned[0:1]
    own_rows = half.shape[1]
    for k in range(4):
        src = half[k] if k < 2 else other[k - 2]
        normed, _ = normalize(src.astype(f32) + time_row)
        act[pl.ds(pl.multiple_of(sc[k], 16), own_rows), :] = (normed * gain).astype(bf16)
    cols = q.shape[1]
    result = mm(act[...], w[...]).astype(bf16)
    q[...] = result[:, :cols]
    kv[...] = result[:, cols:]


def scores_t(keys, queries):
    return mm_nt(keys, queries)


def fill_kv(buffer, parts):
    rows = parts[0].shape[0]
    for index, one in enumerate(parts):
        buffer[index * rows : (index + 1) * rows, :] = one[...]
    done = len(parts) * rows
    if buffer.shape[0] > done:
        buffer[done:, :] = jnp.zeros((buffer.shape[0] - done, buffer.shape[1]), buffer.dtype)


def self_scores(sc, buffer, own, qh, h, hd, block):
    count = qh.shape[0] // block
    col = h * hd
    start = pl.multiple_of(sc[5], block)
    trunk_rows = TRUNK_BLKS * block
    keys = buffer[pl.ds(start, trunk_rows), col : col + hd]
    trunk = mm_nt(keys, qh)
    query_block = lax.broadcasted_iota(i32, (1, qh.shape[0]), 1) // block + sc[6]
    pieces = []
    for j in range(TRUNK_BLKS):
        bias = jnp.where(query_block > j, 0.0, NEG)
        pieces.append(trunk[j * block : (j + 1) * block] + bias)
    key_pos = lax.broadcasted_iota(i32, (block, block), 0)
    query_pos = lax.broadcasted_iota(i32, (block, block), 1)
    own_s, par_s = [], []
    for i in range(count):
        q_i = qh[i * block : (i + 1) * block]
        o = mm_nt(own[i * block : (i + 1) * block, col : col + hd], q_i)
        own_s.append(jnp.where(key_pos <= query_pos, o, NEG))
        par = buffer[pl.ds(pl.multiple_of(sc[8 + i], block), block), col : col + hd]
        leaf = (lax.broadcasted_iota(i32, (1, block), 1) * 0 + sc[8 + count + i]) > 0
        par_s.append(mm_nt(par, q_i) + jnp.where(leaf, 0.0, NEG))
    pieces.append(jnp.concatenate(own_s, axis=1))
    pieces.append(jnp.concatenate(par_s, axis=1))
    return pieces, keys


def out_partial(sc, source, w, kept, sent):
    own_rows = kept.shape[1]
    for k in range(4):
        p = mm_nt(source[pl.ds(pl.multiple_of(sc[k], 16), own_rows), :], w[...])
        if k < 2:
            kept[k] = p
        else:
            sent[k - 2] = p.astype(bf16)


def self_body(block, heads, n_parts, sc, q, *refs):
    parts = refs[:n_parts]
    w = refs[n_parts]
    attn, lse, kept, sent, buffer = refs[n_parts + 1 :]
    own = parts[-1]
    fill_kv(buffer, parts)
    cols = q.shape[1]
    hd = cols // heads
    count = q.shape[0] // block
    trunk_rows = TRUNK_BLKS * block
    start = pl.multiple_of(sc[5], block)
    for h in range(heads):
        col = h * hd
        qh = q[:, col : col + hd] * jnp.asarray(hd**-0.5, bf16)
        pieces, _ = self_scores(sc, buffer, own, qh, h, hd, block)
        peak = pieces[0]
        for s in pieces[1:]:
            peak = jnp.maximum(peak, s)
        peak = jnp.max(peak, axis=0, keepdims=True)
        exps = [jnp.exp(s - peak) for s in pieces]
        total = exps[0]
        for e in exps[1:]:
            total = total + e
        total = jnp.sum(total, axis=0, keepdims=True)
        inv = 1.0 / total
        lse[h : h + 1, :] = peak + jnp.log(total)
        low = [(e * inv).astype(bf16) for e in exps]
        vals = buffer[pl.ds(start, trunk_rows), cols + col : cols + col + hd]
        mixed = mm_tn(jnp.concatenate(low[:TRUNK_BLKS], axis=0), vals)
        for i in range(count):
            rows = slice(i * block, (i + 1) * block)
            par = buffer[pl.ds(pl.multiple_of(sc[8 + i], block), block), cols + col : cols + col + hd]
            both = jnp.concatenate([low[TRUNK_BLKS][:, rows], low[TRUNK_BLKS + 1][:, rows]], axis=0)
            two = jnp.concatenate([own[rows, cols + col : cols + col + hd], par], axis=0)
            attn[rows, col : col + hd] = (mixed[rows] + mm_tn(both, two)).astype(bf16)
    out_partial(sc, attn, w, kept, sent)


def norm_body(first, time_at, gain_at, resid, chip, far, rows, resid_out, act):
    for k in range(2):
        base = resid[k].astype(f32)
        if first:
            base = base + rows[time_at : time_at + 1, :]
        v = base + (chip[k].astype(f32) + far[1 - k].astype(f32))
        resid_out[k] = v
        normed, _ = normalize(v)
        act[k] = (normed * rows[gain_at : gain_at + 1, :]).astype(bf16)


def both_halves(own, other):
    r, d = own.shape[1], own.shape[2]
    return jnp.concatenate([own[...].reshape(2 * r, d), other[...].reshape(2 * r, d)], axis=0)


def split_store(p, kept, sent):
    r = kept.shape[1]
    for k in range(2):
        kept[k] = p[k * r : (k + 1) * r]
        sent[k] = p[(2 + k) * r : (3 + k) * r].astype(bf16)


def cross_body(heads, own, other, enc, wq, wk, wv, wo, q, kv, low_out, lse, kept, sent):
    act = both_halves(own, other)
    queries = mm(act, wq[...]).astype(bf16)
    q[...] = queries
    cols = queries.shape[1]
    hd = cols // heads
    keys = mm(enc[...], wk[...]).astype(bf16)
    vals = mm(enc[...], wv[...]).astype(bf16)
    kv[:, :cols] = keys
    kv[:, cols:] = vals
    for h in range(heads):
        sl = slice(h * hd, (h + 1) * hd)
        s = mm_nt(keys[:, sl], queries[:, sl] * jnp.asarray(hd**-0.5, bf16))
        peak = jnp.max(s, axis=0, keepdims=True)
        e = jnp.exp(s - peak)
        total = jnp.sum(e, axis=0, keepdims=True)
        lse[h : h + 1, :] = peak + jnp.log(total)
        low_out[:, sl] = mm_tn((e * (1.0 / total)).astype(bf16), vals[:, sl]).astype(bf16)
    split_store(mm_nt(low_out[...], wo[...]), kept, sent)


def ffn_body(own, other, g_own, g_other, up, down_t, hidden, grad_pre, kept, sent):
    r = own.shape[1]
    for k in range(4):
        act = own[k] if k < 2 else other[k - 2]
        top = g_own[k] if k < 2 else g_other[k - 2]
        pre = mm(act, up[...])
        cdf = 0.5 * (1.0 + lax.erf(pre * 0.7071067811865476))
        hidden[k * r : (k + 1) * r, :] = (pre * cdf).astype(bf16)
        slope = cdf + pre * (jnp.exp(-0.5 * pre * pre) * 0.3989422804014327)
        gp = (mm(top, down_t[...]) * slope).astype(bf16)
        grad_pre[k * r : (k + 1) * r, :] = gp
        p = mm_nt(gp, up[...])
        if k < 2:
            kept[k] = p
        else:
            sent[k - 2] = p.astype(bf16)


def ffn_rest_body(own, other, g_own, g_other, hidden, grad_pre, down_t, kept, sent, sums):
    split_store(mm_nt(hidden[...], down_t[...]), kept, sent)
    cols = hidden.shape[1]
    sums[:, :cols] = mm_tn(both_halves(own, other), grad_pre[...]).astype(bf16)
    sums[:, cols:] = mm_tn(both_halves(g_own, g_other), hidden[...]).astype(bf16)


def back_body(gain_at, base, chip, far, resid, rows, grad, low, dgain):
    for k in range(2):
        g = chip[k].astype(f32) + far[1 - k].astype(f32)
        back, sums = norm_back(g, resid[k], rows[gain_at : gain_at + 1, :])
        v = base[k].astype(f32) + back
        grad[k] = v
        low[k] = v.astype(bf16)
        if k == 0:
            dgain[...] = sums


def inner_rows(grad, out):
    return (grad.astype(f32) * out.astype(f32)).T


def cross_back_body(heads, g_own, g_other, q, kv, low_in, lse, wq, wo, grad_q, grad_kv, kept, sent):
    top = both_halves(g_own, g_other)
    grad_mixed = mm(top, wo[...]).astype(bf16)
    cols = q.shape[1]
    hd = cols // heads
    inner = inner_rows(grad_mixed, low_in[...])
    for h in range(heads):
        sl = slice(h * hd, (h + 1) * hd)
        vl = slice(cols + h * hd, cols + (h + 1) * hd)
        qh = q[:, sl] * jnp.asarray(hd**-0.5, bf16)
        gh = grad_mixed[:, sl]
        probs = jnp.exp(mm_nt(kv[:, sl], qh) - lse[h : h + 1, :])
        grad_kv[:, vl] = mm(probs.astype(bf16), gh).astype(bf16)
        delta = jnp.sum(inner[sl], axis=0, keepdims=True)
        ds = (probs * (mm_nt(kv[:, vl], gh) - delta)).astype(bf16)
        grad_kv[:, sl] = mm(ds, qh).astype(bf16)
        grad_q[:, sl] = (mm_tn(ds, kv[:, sl]) * hd**-0.5).astype(bf16)
    split_store(mm_nt(grad_q[...], wq[...]), kept, sent)


def cross_rest_body(own, other, g_own, g_other, grad_q, low_in, sums):
    cols = grad_q.shape[1]
    sums[:, :cols] = mm_tn(both_halves(own, other), grad_q[...]).astype(bf16)
    sums[:, cols:] = mm_tn(both_halves(g_own, g_other), low_in[...]).astype(bf16)


def self_back_body(block, heads, n_parts, sc, g_own, g_other, q, attn, lse, *refs):
    parts = refs[:n_parts]
    w = refs[n_parts]
    outs = refs[n_parts + 1 :]
    top, grad_q, grad_own = outs[0], outs[1], outs[2]
    remote = outs[3 : 3 + n_parts - 1]
    buffer, sums = outs[3 + n_parts - 1 :]
    own = parts[-1]
    fill_kv(buffer, parts)
    sums[...] = jnp.zeros(sums.shape, f32)
    own_rows = g_own.shape[1]
    for k in range(4):
        src = g_own[k] if k < 2 else g_other[k - 2]
        top[pl.ds(pl.multiple_of(sc[k], 16), own_rows), :] = src
    cols = q.shape[1]
    hd = cols // heads
    count = q.shape[0] // block
    trunk_rows = TRUNK_BLKS * block
    start = pl.multiple_of(sc[5], block)
    grad_attn = mm(top[...], w[...]).astype(bf16)
    inner = inner_rows(grad_attn, attn[...])
    rows_all = own.shape[0]
    for h in range(heads):
        col = h * hd
        sl, vl = slice(col, col + hd), slice(cols + col, cols + col + hd)
        qh = q[:, sl] * jnp.asarray(hd**-0.5, bf16)
        gh = grad_attn[:, sl]
        pieces, keys = self_scores(sc, buffer, own, qh, h, hd, block)
        delta = jnp.sum(inner[sl], axis=0, keepdims=True)
        level = lse[h : h + 1, :]
        vals = buffer[pl.ds(start, trunk_rows), vl]
        probs = jnp.exp(jnp.concatenate(pieces[:TRUNK_BLKS], axis=0) - level)
        ds = (probs * (mm_nt(vals, gh) - delta)).astype(bf16)
        sums[pl.ds(start, trunk_rows), sl] += mm(ds, qh)
        sums[pl.ds(start, trunk_rows), vl] += mm(probs.astype(bf16), gh)
        grad_trunk = mm_tn(ds, keys)
        base = (n_parts - 1) * rows_all
        for i in range(count):
            rows = slice(i * block, (i + 1) * block)
            par_at = pl.ds(pl.multiple_of(sc[8 + i], block), block)
            own_at = slice(base + i * block, base + (i + 1) * block)
            q_i, g_i = qh[rows], gh[rows]
            grad_i = grad_trunk[rows]
            for piece, at in ((pieces[TRUNK_BLKS], own_at), (pieces[TRUNK_BLKS + 1], par_at)):
                p = jnp.exp(piece[:, rows] - level[:, rows])
                d = (p * (mm_nt(buffer[at, vl], g_i) - delta[:, rows])).astype(bf16)
                sums[at, sl] += mm(d, q_i)
                sums[at, vl] += mm(p.astype(bf16), g_i)
                grad_i = grad_i + mm_tn(d, buffer[at, sl])
            grad_q[rows, sl] = (grad_i * hd**-0.5).astype(bf16)
    for index, one in enumerate(remote):
        one[...] = sums[index * rows_all : (index + 1) * rows_all, :].astype(bf16)
    grad_own[...] = sums[base : base + rows_all, :]


def self_rest_body(act, top, attn, grad_q, wq, sum_q, sum_o, grad_act):
    sum_q[...] = mm_tn(act[...], grad_q[...]).astype(bf16)
    sum_o[...] = mm_tn(top[...], attn[...]).astype(bf16)
    grad_act[...] = mm_nt(grad_q[...], wq[...])


def self_end_body(n_parts, sc, act, grad_own, *refs):
    remote = refs[: n_parts - 1]
    wk, wv, sum_q, sum_o, grad_act, sums, kept, sent, total = refs[n_parts - 1 :]
    t = grad_own[...]
    for one in remote:
        t = t + one[...].astype(f32)
    total[...] = t.astype(bf16)
    cols = sum_q.shape[1]
    own_rows = kept.shape[1]
    for k in range(4):
        at = pl.ds(pl.multiple_of(sc[k], 16), own_rows)
        p = grad_act[at, :] + mm_nt(total[at, :cols], wk[...]) + mm_nt(total[at, cols:], wv[...])
        if k < 2:
            kept[k] = p
        else:
            sent[k - 2] = p.astype(bf16)
    sums[:, :cols] = sum_q[...]
    sums[:, cols : 3 * cols] = mm_tn(act[...], total[...]).astype(bf16)
    sums[:, 3 * cols :] = sum_o[...]


def last_body(sc, chip, far, tokens, grad_mid, rows, dgain_cross, dgain_ffn, grad_in, vectors):
    g = chip[...].astype(f32) + far[...].astype(f32)
    resid = tokens[...].astype(f32) + rows[3:4, :]
    back, dgain = norm_back(g, resid, rows[0:1, :])
    v = grad_mid[0] + back
    grad_in[...] = v
    vectors[0:1, :] = dgain
    vectors[1:2, :] = dgain_cross[...]
    vectors[2:3, :] = dgain_ffn[...]
    vectors[3:4, :] = jnp.sum(v, axis=0, keepdims=True)
    vectors[4:8, :] = jnp.zeros((4, v.shape[1]), f32) + sc[7].astype(f32)


def xor_route(axis, bit):
    return [(i, i ^ bit) for i in range(lax.axis_size(axis))]


def sibling(x):
    return lax.ppermute(x, "tensor", xor_route("tensor", 1))


def across(x):
    return lax.ppermute(x, "tensor", xor_route("tensor", 2))


def chip_sum(kept, sent):
    return kept + sibling(sent).astype(f32)


def gather_dp(x, groups=None):
    count = lax.axis_size("dp") if groups is None else len(groups[0])
    copies = jnp.broadcast_to(x[None], (count,) + x.shape)
    return lax.all_to_all(copies, "dp", 0, 0, axis_index_groups=groups).reshape(-1, x.shape[-1])


def scatter_dp(full):
    count = lax.axis_size("dp")
    parts = full.reshape(count, full.shape[0] // count, full.shape[1])
    return jnp.sum(lax.all_to_all(parts, "dp", 0, 0).astype(f32), axis=0)


def on_device(
    tokens_in, grad_out, enc_states, parents, tree_ids, timesteps, time_table, norm_self,
    w_query, w_key, w_value, w_out, norm_cross, c_query, c_key, c_value, c_out, norm_ffn,
    w_hidden, w_back,
):
    count = lax.axis_size("dp")
    tensor = lax.axis_size("tensor")
    heads = HEADS // tensor
    blocks_dev = parents.shape[0]
    tree_blocks = TRUNK_BLKS + BRANCHES * (1 + LEAVES)
    group = tree_blocks // blocks_dev
    hops_back = group - 1
    me = lax.axis_index("tensor")
    logical_dev = (lax.axis_index("dp") - group // 2) % count
    trees = timesteps.shape[0]
    width = tokens_in.shape[1]
    own_rows = tokens_in.shape[0]
    token_rows = own_rows * tensor
    block = token_rows // blocks_dev
    shard = norm_self.shape[0]
    cols = w_query.shape[1]
    hidden_cols = w_hidden.shape[1]
    groups = [
        [(tree * group + member + group // 2) % count for member in range(group)]
        for tree in range(count // group)
    ]
    steps_hot = (jnp.arange(time_table.shape[0], dtype=i32)[:, None] == timesteps[None, :]).astype(bf16)
    table_cols = mm_tn(time_table, steps_hot).astype(bf16)
    small = jnp.concatenate([norm_self[:, None], norm_cross[:, None], norm_ffn[:, None], table_cols], axis=1)
    small = jnp.pad(small, ((0, 0), (0, 128 - small.shape[1])))
    first = gather_dp(jnp.concatenate([w_query, w_key, w_value, small], axis=1))
    tokens_half = jnp.stack([tokens_in, across(tokens_in)])
    tokens_other = sibling(tokens_half)
    grad_half = jnp.stack([grad_out, across(grad_out)])
    grad_other = sibling(grad_half)
    enc_tree = gather_dp(enc_states, groups)
    second = gather_dp(jnp.concatenate([w_out.T, c_query, c_key, c_value, c_out.T], axis=1))
    third = gather_dp(jnp.concatenate([w_hidden, w_back.T], axis=1))
    position = logical_dev % group
    lead_blocks = group // 2 * blocks_dev
    parent_log = (parents - lead_blocks) % (count * blocks_dev)
    parent_rel = parent_log - logical_dev // group * tree_blocks
    query_block = position * blocks_dev + jnp.arange(blocks_dev, dtype=i32)
    is_leaf = query_block >= TRUNK_BLKS + BRANCHES
    shift = (hops_back - position) * blocks_dev
    parent_at = jnp.where(is_leaf, parent_rel, query_block) + shift
    step_id = jnp.sum(jnp.where(jnp.arange(trees, dtype=i32) == tree_ids[0], timesteps, 0))
    scalars = jnp.concatenate(
        [
            (me ^ jnp.array([0, 2, 1, 3], i32)) * own_rows,
            jnp.stack([tree_ids[0], shift * block, position * blocks_dev, step_id]),
            parent_at * block,
            is_leaf.astype(i32),
        ]
    ).astype(i32)
    half = (2, own_rows, width)
    act_self, q, kv, rows = run(
        project_body,
        [
            shaped((token_rows, width), bf16), shaped((token_rows, cols), bf16),
            shaped((token_rows, 2 * cols), bf16), shaped((4, width), f32),
        ],
        [scalars, tokens_half, tokens_other, part(first, 3 * cols, 0), part(first, 128, 3 * cols // 128)],
    )

    def later(distance):
        return [
            ((l + group // 2) % count, (l + distance + group // 2) % count)
            for l in range(count)
            if l % group + distance < group
        ]

    parts = [lax.ppermute(kv, "dp", later(d)) for d in range(hops_back, 0, -1)] + [kv]
    buffer_rows = group * token_rows + max(0, TRUNK_BLKS - blocks_dev) * block
    attn, lse, kept, sent = run(
        lambda *refs: self_body(block, heads, group, *refs),
        [shaped((token_rows, cols), bf16), shaped((8, token_rows), f32), shaped(half, f32), shaped(half, bf16)],
        [scalars, q, *parts, part(second, cols, 0)],
        [pltpu.VMEM((buffer_rows, 2 * cols), bf16)],
    )
    chip = chip_sum(kept, sent).astype(bf16)
    resid_mid, act_own = run(
        lambda *refs: norm_body(True, 3, 1, *refs),
        [shaped(half, f32), shaped(half, bf16)],
        [tokens_half, chip, across(chip), rows],
    )
    act_other = sibling(act_own)
    enc_rows = enc_tree.shape[0]
    cross_q, cross_kv, cross_low, cross_lse, kept, sent = run(
        lambda *refs: cross_body(heads, *refs),
        [
            shaped((token_rows, cols), bf16), shaped((enc_rows, 2 * cols), bf16), shaped((token_rows, cols), bf16),
            shaped((8, token_rows), f32), shaped(half, f32), shaped(half, bf16),
        ],
        [act_own, act_other, enc_tree, *[part(second, cols, i) for i in (1, 2, 3, 4)]],
    )
    chip = chip_sum(kept, sent).astype(bf16)
    resid_ffn, ffn_own = run(
        lambda *refs: norm_body(False, 3, 2, *refs),
        [shaped(half, f32), shaped(half, bf16)],
        [resid_mid, chip, across(chip), rows],
    )
    ffn_other = sibling(ffn_own)
    hidden, grad_pre, kept, sent = run(
        ffn_body,
        [
            shaped((token_rows, hidden_cols), bf16), shaped((token_rows, hidden_cols), bf16),
            shaped(half, f32), shaped(half, bf16),
        ],
        [ffn_own, ffn_other, grad_half, grad_other, part(third, hidden_cols, 0), part(third, hidden_cols, 1)],
    )
    chip = chip_sum(kept, sent).astype(bf16)
    out_kept, out_sent, ffn_sums = run(
        ffn_rest_body,
        [shaped(half, f32), shaped(half, bf16), shaped((width, 2 * hidden_cols), bf16)],
        [ffn_own, ffn_other, grad_half, grad_other, hidden, grad_pre, part(third, hidden_cols, 1)],
    )
    grad_resid_ffn, top_own, dgain_ffn = run(
        lambda *refs: back_body(2, *refs),
        [shaped(half, f32), shaped(half, bf16), shaped((1, width), f32)],
        [grad_half, chip, across(chip), resid_ffn, rows],
    )
    ffn_sums = scatter_dp(ffn_sums)
    out_chip = chip_sum(out_kept, out_sent)
    output = (resid_ffn[0] + (out_chip[0] + across(out_chip[1].astype(bf16)).astype(f32))).astype(bf16)
    top_other = sibling(top_own)
    grad_cq, grad_cross_kv, kept, sent = run(
        lambda *refs: cross_back_body(heads, *refs),
        [
            shaped((token_rows, cols), bf16), shaped((enc_rows, 2 * cols), bf16),
            shaped(half, f32), shaped(half, bf16),
        ],
        [top_own, top_other, cross_q, cross_kv, cross_low, cross_lse, part(second, cols, 1), part(second, cols, 4)],
    )
    chip = chip_sum(kept, sent).astype(bf16)
    (cross_part,) = run(
        cross_rest_body,
        [shaped((width, 2 * cols), bf16)],
        [act_own, act_other, top_own, top_other, grad_cq, cross_low],
    )
    enc_sum = jnp.sum(
        lax.all_to_all(grad_cross_kv.reshape(group, -1, 2 * cols), "dp", 0, 0, axis_index_groups=groups).astype(f32),
        axis=0,
    ).astype(bf16)
    enc_part = mm_nt(enc_sum, second[:, 2 * cols : 4 * cols])
    enc_chip = (enc_part + sibling(enc_part.astype(bf16)).astype(f32)).astype(bf16)
    grad_enc = enc_chip.astype(f32) + across(enc_chip).astype(f32)
    cross_sums = scatter_dp(jnp.concatenate([cross_part, mm_tn(enc_states, enc_sum).astype(bf16)], axis=1))
    grad_resid_mid, self_own, dgain_cross = run(
        lambda *refs: back_body(1, *refs),
        [shaped(half, f32), shaped(half, bf16), shaped((1, width), f32)],
        [grad_resid_ffn, chip, across(chip), resid_mid, rows],
    )
    self_other = sibling(self_own)
    kv_shape = (token_rows, 2 * cols)
    top, grad_q, grad_own, *remote = run(
        lambda *refs: self_back_body(block, heads, group, *refs),
        [shaped((token_rows, width), bf16), shaped((token_rows, cols), bf16), shaped(kv_shape, f32)]
        + [shaped(kv_shape, bf16)] * hops_back,
        [scalars, self_own, self_other, q, attn, lse, *parts, part(second, cols, 0)],
        [pltpu.VMEM((buffer_rows, 2 * cols), bf16), pltpu.VMEM((buffer_rows, 2 * cols), f32)],
    )
    back = [
        lax.ppermute(one, "dp", [(b, a) for a, b in later(d)]) for one, d in zip(remote, range(hops_back, 0, -1))
    ]
    sum_q, sum_o, grad_act = run(
        self_rest_body,
        [shaped((width, cols), bf16), shaped((width, cols), bf16), shaped((token_rows, width), f32)],
        [act_self, top, attn, grad_q, part(first, cols, 0)],
    )
    self_sums, kept, sent = run(
        lambda *refs: self_end_body(group, *refs),
        [shaped((width, 4 * cols), bf16), shaped(half, f32), shaped(half, bf16)],
        [scalars, act_self, grad_own, *back, part(first, cols, 1), part(first, cols, 2), sum_q, sum_o, grad_act],
        [pltpu.VMEM(kv_shape, bf16)],
    )
    chip = chip_sum(kept, sent)
    self_sums = scatter_dp(self_sums)
    grad_in, vectors = run(
        last_body,
        [shaped((own_rows, width), f32), shaped((8, width), f32)],
        [scalars, chip[0], across(chip[1].astype(bf16)), tokens_in, grad_resid_mid, rows, dgain_cross, dgain_ffn],
    )
    vectors = vectors.reshape(8, count, 1, shard).transpose(1, 2, 0, 3)
    vectors = jnp.broadcast_to(vectors, (count, tensor, 8, shard)).reshape(count * tensor, 8, shard)
    received = lax.all_to_all(vectors, ("dp", "tensor"), 0, 0)
    gain_sums = jnp.sum(received[:, :3], axis=0)
    table_hot = jnp.arange(time_table.shape[0], dtype=i32)[:, None, None] == received[:, 4].astype(i32)[None]
    grad_table = jnp.sum(jnp.where(table_hot, received[:, 3][None], 0.0), axis=1)
    gq, gk, gv, go = [self_sums[:, i * cols : (i + 1) * cols] for i in range(4)]
    gcq, gco, gck, gcv = [cross_sums[:, i * cols : (i + 1) * cols] for i in range(4)]
    return (
        output, grad_in, grad_enc, grad_table, gain_sums[0], gq, gk, gv, go.T, gain_sums[1],
        gcq, gck, gcv, gco.T, gain_sums[2], ffn_sums[:, :hidden_cols], ffn_sums[:, hidden_cols:].T,
    )


def solution(mesh):
    rows, cols, repl = P(("dp", "tensor"), None), P("dp", "tensor"), P("tensor", "dp")
    in_specs = (
        rows, rows, P("dp", None), P("dp"), P("dp"), P(), P(None, "dp"), P("dp"), cols, cols, cols, repl,
        P("dp"), cols, cols, cols, repl, P("dp"), cols, repl,
    )
    out_specs = (
        rows, rows, P("dp", None), P(None, "dp"), P("dp"), cols, cols, cols, repl, P("dp"), cols, cols, cols,
        repl, P("dp"), cols, repl,
    )
    return jax.shard_map(on_device, mesh=mesh, in_specs=in_specs, out_specs=out_specs, check_vma=False)
```

time: 352 us -> 279 us (0.79)
  Pallas kernels: 0 us -> 59.9 us
  matrix products: 56.1 us -> 2.26 us
  other arithmetic: 51.4 us -> 9.52 us
  local copies, waits for them, and re-layouts: 44.7 us -> 22 us
  between operations: 16.7 us -> 1.36 us
  waiting for transfers between devices: 95.4 us -> 106 us
  starting transfers between devices: 82.4 us -> 75.8 us
    pallas_call x0 -> x15, Pallas kernels: none -> 59.9 us  [run(): pl.pallas_call(body, grid=(1,), out_shape=outs, in_specs=specs, out_specs...]
    dot_general x21 -> x0, matrix products: 45.5 us -> none  [the longest x9 14.2 us: mm(): return jnp.dot(a, b, preferred_element_type=f32)]
    convert_element_type x16 -> x8, other arithmetic: 22 us -> 4.41 us  [the longest x4 3.63 us: on_device(): chip = chip_sum(kept, sent).astype(bf16)]
    all_to_all x6 -> x5, starting transfers between devices: 41.4 us -> 27.8 us  [the longest x4 20.5 us: gather_dp(): lax.all_to_all(copies, 'dp', 0, 0, axis_index_groups=groups)]
    all_gather x1 -> x0, waiting for transfers between devices: 10.3 us -> none  [on_device(): both = lax.all_gather(jnp.stack([tokens_in, grad_out]), 'tensor', axis=1)]
    reduce_sum x17 -> x2, other arithmetic: 10.2 us -> 0.69 us  [the longest x1 0.66 us: on_device(): jnp.sum(jnp.where(jnp.arange(trees, dtype=i32) == tree_ids[0], timesteps,...]
    ppermute x6, waiting for transfers between devices: 15.8 us -> 24.7 us  [the longest x3 16.9 us: on_device(): lax.ppermute(kv, 'dp', later(d))]
    dot_general x8 -> x0, local copies, waits for them, and re-layouts: 8.3 us -> none  [the longest x7 8.09 us: mm_tn(): lax.dot_general(a, b, (((0,), (0,)), ((), ())), preferred_element_type=f32)]
  transfers between devices with their start and end apart: 35 -> 37, of which waited for: 17 -> 20; matrix products, arithmetic and copies ran while one was open for 31% -> 6% of each run, Pallas kernels for 0% -> 17%
where the time goes in v2:
time: 279 us; the launch traced here: 277 us
  waiting for transfers between devices  106 us (38%)
  starting transfers between devices  75.8 us (27%)
  Pallas kernels  59.9 us (21%)
  local copies, waits for them, and re-layouts  22 us (8%)
  other arithmetic  9.52 us (3%)
    pallas_call x15, Pallas kernels, run(): pl.pallas_call(body, grid=(1,), out_shape=outs, in_specs=specs, out_specs...  59.9 us
    ppermute x9, waiting for transfers between devices, across(): return lax.ppermute(x, 'tensor', xor_route('tensor', 2))  32.1 us
    all_to_all x4, starting transfers between devices, gather_dp(): lax.all_to_all(copies, 'dp', 0, 0, axis_index_groups=groups)  20.5 us
    ppermute x3, waiting for transfers between devices, on_device(): lax.ppermute(kv, 'dp', later(d))  16.9 us
    all_to_all x4, waiting for transfers between devices, gather_dp(): lax.all_to_all(copies, 'dp', 0, 0, axis_index_groups=groups)  16.8 us
    all_to_all x3, waiting for transfers between devices, scatter_dp(): return jnp.sum(lax.all_to_all(parts, 'dp', 0, 0).astype(f32), axis=0)  14.7 us
    all_to_all x3, starting transfers between devices, scatter_dp(): return jnp.sum(lax.all_to_all(parts, 'dp', 0, 0).astype(f32), axis=0)  14.5 us
    ppermute x9, starting transfers between devices, across(): return lax.ppermute(x, 'tensor', xor_route('tensor', 2))  12.3 us
  transfers between devices with their start and end apart: 37, of which 20 were waited for; matrix products, arithmetic and copies ran while one was open for 6% of the time, Pallas kernels for 17%

profile of v2, /device:TPU:0, one launch (start us, length us, event | category | flops | bytes accessed | tf_op | source)
XLA Modules:
  0.0 277.1 jit_solution(11034989629214781269)
XLA Ops:
  5.8 7.3 %all-to-all-start = ((bf16[8,64,512]{2,1,0:T(8,128)(2,1)}), bf16[8,64,512]{2,1,0:T(8,128)(2,1)S(1)}, u32[]{:S(2)}, u32[]{:S(2)}) async-start(bf16[8,64,512]{2,1,0:T(8,128)(2,1)} %broadcast_in_dim.66), calls=%async_computation | async-start | bytes 1048576 | tf_op jit(solution)/shard_map/all_to_all | solution.py:408
  13.3 14.3 %all-to-all-done = bf16[8,64,512]{2,1,0:T(8,128)(2,1)S(1)} async-done(((bf16[8,64,512]{2,1,0:T(8,128)(2,1)}), bf16[8,64,512]{2,1,0:T(8,128)(2,1)S(1)}, u32[]{:S(2)}, u32[]{:S(2)}) %all-to-all-start) | async-done | bytes 524320 | tf_op jit(solution)/shard_map/all_to_all | solution.py:408
  45.8 4.2 %collective-permute-start.4 = (bf16[640,256]{1,0:T(8,128)(2,1)}, bf16[640,256]{1,0:T(8,128)(2,1)S(1)}, u32[]{:S(2)}, u32[]{:S(2)}) collective-permute-start(bf16[640,256]{1,0:T(8,128)(2,1)} %get-tuple-element.67.refs_5_.refs_9_), channel_id=1, source_target_pairs={{8,12},{12,16},{16,20},{24,28},{28,0},{0,4},{9,13},{13,17},{17,21}... | collective-permute-start | bytes 983048 | tf_op jit(solution)/shard_map/ppermute | solution.py:489
  50.0 15.7 %collective-permute-done.3.refs_3_.refs_7_ = bf16[640,256]{1,0:T(8,128)(2,1)S(1)} collective-permute-done((bf16[640,256]{1,0:T(8,128)(2,1)}, bf16[640,256]{1,0:T(8,128)(2,1)S(1)}, u32[]{:S(2)}, u32[]{:S(2)}) %collective-permute-start.3) | collective-permute-done | bytes 327712 | tf_op jit(solution)/shard_map/ppermute | solution.py:489
  67.6 6.1 %shard_map.333 = (bf16[640,128]{1,0:T(8,128)(2,1)}, f32[8,640]{1,0:T(8,128)}, f32[2,160,512]{2,1,0:T(8,128)}, bf16[2,160,512]{2,1,0:T(8,128)(2,1)}) custom-call(s32[18]{0:T(128)} %concatenate.18.sc.refs_0_, bf16[640,128]{1,0:T(8,128)(2,1)} %get-tuple-element.66.refs_1_.refs_3_, bf16[640,256]{1,0:T(8,128)(2,1)} %copy-done.7, bf16[640,256]{1,0:T(8,128)(2,1)} %copy-done.8, ...), custom_call_target="tpu_custom_call" | custom-call | tf_op jit(solution)/shard_map/pallas_call | solution.py:67
  74.5 5.1 %all-to-all-start.2 = ((bf16[4,64,512]{2,1,0:T(8,128)(2,1)}), bf16[4,64,512]{2,1,0:T(8,128)(2,1)S(1)}, u32[]{:S(2)}, u32[]{:S(2)}) async-start(bf16[4,64,512]{2,1,0:T(8,128)(2,1)} %broadcast_in_dim.68), calls=%async_computation.2 | async-start | bytes 524288 | tf_op jit(solution)/shard_map/all_to_all | solution.py:408
  86.0 4.5 %all-to-all-start.3 = ((bf16[8,64,1024]{2,1,0:T(8,128)(2,1)}), bf16[8,64,1024]{2,1,0:T(8,128)(2,1)S(1)}, u32[]{:S(2)}, u32[]{:S(2)}) async-start(bf16[8,64,1024]{2,1,0:T(8,128)(2,1)} %broadcast_in_dim.69), calls=%async_computation.3 | async-start | bytes 2097152 | tf_op jit(solution)/shard_map/all_to_all | solution.py:408
  96.1 4.0 %shard_map.335 = (bf16[640,128]{1,0:T(8,128)(2,1)}, bf16[256,256]{1,0:T(8,128)(2,1)}, bf16[640,128]{1,0:T(8,128)(2,1)}, f32[8,640]{1,0:T(8,128)}, f32[2,160,512]{2,1,0:T(8,128)}, /*index=5*/bf16[2,160,512]{2,1,0:T(8,128)(2,1)}) custom-call(bf16[2,160,512]{2,1,0:T(8,128)(2,1)} %get-tuple-element.72.refs_0_.own, bf16[2,160,512]{2,1,0:T(8,128)(2,1)} %copy-done.13, ...), custom_call_target="tpu_custom_call" | custom-call | tf_op jit(solution)/shard_map/pallas_call | solution.py:67
  105.2 11.2 %collective-permute-done.11 = bf16[160,512]{1,0:T(8,128)(2,1)S(1)} collective-permute-done((bf16[160,512]{1,0:T(8,128)(2,1)S(1)}, bf16[160,512]{1,0:T(8,128)(2,1)S(1)}, u32[]{:S(2)}, u32[]{:S(2)}) %collective-permute-start.11) | collective-permute-done | bytes 163872 | tf_op jit(solution)/shard_map/ppermute | solution.py:398
  122.4 4.7 %shard_map.337 = (bf16[640,512]{1,0:T(8,128)(2,1)}, bf16[640,512]{1,0:T(8,128)(2,1)}, f32[2,160,512]{2,1,0:T(8,128)}, bf16[2,160,512]{2,1,0:T(8,128)(2,1)}) custom-call(bf16[2,160,512]{2,1,0:T(8,128)(2,1)} %get-tuple-element.76.own, bf16[2,160,512]{2,1,0:T(8,128)(2,1)} %copy-done.16, bf16[2,160,512]{2,1,0:T(8,128)(2,1)} %copy-done.4, ...), custom_call_target="tpu_custom_call" | custom-call | tf_op jit(solution)/shard_map/pallas_call | solution.py:67
  131.7 8.5 %collective-permute-done.16.refs_2_ = bf16[2,160,512]{2,1,0:T(8,128)(2,1)S(1)} collective-permute-done((bf16[2,160,512]{2,1,0:T(8,128)(2,1)S(1)}, bf16[2,160,512]{2,1,0:T(8,128)(2,1)S(1)}, u32[]{:S(2)}, u32[]{:S(2)}) %collective-permute-start.16) | collective-permute-done | bytes 327712 | tf_op jit(solution)/shard_map/ppermute | solution.py:398
  143.8 4.2 %shard_map.338 = (f32[2,160,512]{2,1,0:T(8,128)}, bf16[2,160,512]{2,1,0:T(8,128)(2,1)}, bf16[512,1024]{1,0:T(8,128)(2,1)}) custom-call(bf16[2,160,512]{2,1,0:T(8,128)(2,1)} %get-tuple-element.76.own, bf16[2,160,512]{2,1,0:T(8,128)(2,1)} %copy-done.16, bf16[2,160,512]{2,1,0:T(8,128)(2,1)} %copy-done.4, bf16[2,160,512]{2,1,0:T(8,128)(2,1)} %copy-done.15, ...), custom_call_target="tpu_custom_call" | custom-call | tf_op jit(solution)/shard_map/pallas_call | solution.py:67
  149.3 4.2 %shard_map.340 = (bf16[640,128]{1,0:T(8,128)(2,1)}, bf16[256,256]{1,0:T(8,128)(2,1)}, f32[2,160,512]{2,1,0:T(8,128)}, bf16[2,160,512]{2,1,0:T(8,128)(2,1)}) custom-call(bf16[2,160,512]{2,1,0:T(8,128)(2,1)} %get-tuple-element.85.refs_0_.g_own, bf16[2,160,512]{2,1,0:T(8,128)(2,1)} %copy-done.14, bf16[640,128]{1,0:T(8,128)(2,1)} %get-tuple-element.86.refs_2_, ...), custom_call_target="tpu_custom_call" | custom-call | tf_op jit(solution)/shard_map/pallas_call | solution.py:67
  153.4 7.2 %all-to-all-start.4 = ((bf16[4,64,256]{2,1,0:T(8,128)(2,1)}), bf16[4,64,256]{2,1,0:T(8,128)(2,1)S(1)}, u32[]{:S(2)}, u32[]{:S(2)}) async-start(bf16[4,64,256]{2,1,0:T(8,128)(2,1)} %bitcast.90), calls=%async_computation.4 | async-start | bytes 262144 | tf_op jit(solution)/shard_map/all_to_all | solution.py:558
  164.6 4.5 %all-to-all-start.8 = ((bf16[8,64,1024]{2,1,0:T(8,128)(2,1)}), bf16[8,64,1024]{2,1,0:T(8,128)(2,1)S(1)}, u32[]{:S(2)}, u32[]{:S(2)}) async-start(bf16[8,64,1024]{2,1,0:T(8,128)(2,1)} %bitcast.38), calls=%async_computation.8 | async-start | bytes 2097152 | tf_op jit(solution)/shard_map/all_to_all | solution.py:414
  171.9 4.6 %collective-permute-done.14 = bf16[160,512]{1,0:T(8,128)(2,1)S(1)} collective-permute-done((bf16[160,512]{1,0:T(8,128)(2,1)S(1)}, bf16[160,512]{1,0:T(8,128)(2,1)S(1)}, u32[]{:S(2)}, u32[]{:S(2)}) %collective-permute-start.14) | collective-permute-done | bytes 163872 | tf_op jit(solution)/shard_map/ppermute | solution.py:398
  187.8 11.1 %shard_map.342 = (bf16[640,512]{1,0:T(8,128)(2,1)}, bf16[640,128]{1,0:T(8,128)(2,1)}, f32[640,256]{1,0:T(8,128)}, bf16[640,256]{1,0:T(8,128)(2,1)}, bf16[640,256]{1,0:T(8,128)(2,1)}, /*index=5*/bf16[640,256]{1,0:T(8,128)(2,1)}) custom-call(s32[18]{0:T(128)} %concatenate.18.sc.refs_0_, bf16[2,160,512]{2,1,0:T(8,128)(2,1)} %get-tuple-element.92.refs_1_, ...), custom_call_target="tpu_custom_call" | custom-call | tf_op jit(solution)/shard_map/pallas_call | solution.py:67
  199.6 6.3 %collective-permute-start.22 = (bf16[640,256]{1,0:T(8,128)(2,1)}, bf16[640,256]{1,0:T(8,128)(2,1)S(1)}, u32[]{:S(2)}, u32[]{:S(2)}) collective-permute-start(bf16[640,256]{1,0:T(8,128)(2,1)} %get-tuple-element.97), channel_id=1, source_target_pairs={{16,8},{20,12},{0,24},{4,28},{17,9},{21,13},{1,25},{5,29},{18,10},... | collective-permute-start | bytes 983048 | tf_op jit(solution)/shard_map/ppermute | solution.py:580
  214.3 6.0 %collective-permute-done.23.refs_5_ = bf16[640,256]{1,0:T(8,128)(2,1)S(1)} collective-permute-done((bf16[640,256]{1,0:T(8,128)(2,1)}, bf16[640,256]{1,0:T(8,128)(2,1)S(1)}, u32[]{:S(2)}, u32[]{:S(2)}) %collective-permute-start.23) | collective-permute-done | bytes 327712 | tf_op jit(solution)/shard_map/ppermute | solution.py:580
  221.1 4.1 %shard_map.344 = (bf16[512,512]{1,0:T(8,128)(2,1)}, f32[2,160,512]{2,1,0:T(8,128)}, bf16[2,160,512]{2,1,0:T(8,128)(2,1)}) custom-call(s32[18]{0:T(128)} %concatenate.18.sc.refs_0_, bf16[640,512]{1,0:T(8,128)(2,1)} %get-tuple-element.81.act.refs_1_, f32[640,256]{1,0:T(8,128)} %get-tuple-element.95.refs_2_, bf16[640,256]{1,0:T(8,128)(2,1)} %copy-done.24, ...), custom_call_target="tpu_custom_call" | custom-call | tf_op jit(solution)/shard_map/pallas_call | solution.py:67
  225.2 6.5 %all-to-all-start.7 = ((bf16[8,64,512]{2,1,0:T(8,128)(2,1)}), bf16[8,64,512]{2,1,0:T(8,128)(2,1)S(1)}, u32[]{:S(2)}, u32[]{:S(2)}) async-start(bf16[8,64,512]{2,1,0:T(8,128)(2,1)} %bitcast.35), calls=%async_computation.7 | async-start | bytes 1048576 | tf_op jit(solution)/shard_map/all_to_all | solution.py:414
  235.0 4.1 %collective-permute-done.25.far = bf16[160,512]{1,0:T(8,128)(2,1)S(1)} collective-permute-done((bf16[160,512]{1,0:T(8,128)(2,1)S(1)}, bf16[160,512]{1,0:T(8,128)(2,1)S(1)}, u32[]{:S(2)}, u32[]{:S(2)}) %collective-permute-start.25) | collective-permute-done | bytes 163872 | tf_op jit(solution)/shard_map/ppermute | solution.py:398
  250.6 7.3 %all-to-all-done.5 = f32[32,1,512]{2,1,0:T(1,128)S(1)} async-done(((f32[32,1,512]{2,1,0:T(1,128)}), f32[32,1,512]{2,1,0:T(1,128)S(1)}, u32[]{:S(2)}, u32[]{:S(2)}) %all-to-all-start.5) | async-done | bytes 65568 | tf_op jit(solution)/shard_map/all_to_all | solution.py:602
  264.8 11.5 %all-to-all-done.6 = bf16[8,64,512]{2,1,0:T(8,128)(2,1)S(1)} async-done(((bf16[8,64,512]{2,1,0:T(8,128)(2,1)}), bf16[8,64,512]{2,1,0:T(8,128)(2,1)S(1)}, u32[]{:S(2)}, u32[]{:S(2)}) %all-to-all-start.6) | async-done | bytes 524320 | tf_op jit(solution)/shard_map/all_to_all | solution.py:414
  (216 shorter events, 108.4 us)
Async XLA Ops:
  5.8 21.8 %all-to-all-start = ((bf16[8,64,512]{2,1,0:T(8,128)(2,1)}), bf16[8,64,512]{2,1,0:T(8,128)(2,1)S(1)}, u32[]{:S(2)}, u32[]{:S(2)}) async-start(bf16[8,64,512]{2,1,0:T(8,128)(2,1)} %broadcast_in_dim.66), calls=%async_computation | async-start | bytes 1048576 | tf_op jit(solution)/shard_map/all_to_all | solution.py:408
  28.5 21.4 %all-to-all-start.1 = ((bf16[8,64,640]{2,1,0:T(8,128)(2,1)}), bf16[8,64,640]{2,1,0:T(8,128)(2,1)S(1)}, u32[]{:S(2)}, u32[]{:S(2)}) async-start(bf16[8,64,640]{2,1,0:T(8,128)(2,1)} %broadcast_in_dim.67), calls=%async_computation.1 | async-start | bytes 1310720 | tf_op jit(solution)/shard_map/all_to_all | solution.py:408
  44.5 21.2 %collective-permute-start.3 = (bf16[640,256]{1,0:T(8,128)(2,1)}, bf16[640,256]{1,0:T(8,128)(2,1)S(1)}, u32[]{:S(2)}, u32[]{:S(2)}) collective-permute-start(bf16[640,256]{1,0:T(8,128)(2,1)} %get-tuple-element.67.refs_5_.refs_9_), channel_id=1, source_target_pairs={{8,16},{12,20},{24,0},{28,4},{9,17},{13,21},{25,1},{29,5},{10,18},... | collective-permute-start | bytes 983048 | tf_op jit(solution)/shard_map/ppermute | solution.py:489
  45.8 21.1 %collective-permute-start.4 = (bf16[640,256]{1,0:T(8,128)(2,1)}, bf16[640,256]{1,0:T(8,128)(2,1)S(1)}, u32[]{:S(2)}, u32[]{:S(2)}) collective-permute-start(bf16[640,256]{1,0:T(8,128)(2,1)} %get-tuple-element.67.refs_5_.refs_9_), channel_id=1, source_target_pairs={{8,12},{12,16},{16,20},{24,28},{28,0},{0,4},{9,13},{13,17},{17,21}... | collective-permute-start | bytes 983048 | tf_op jit(solution)/shard_map/ppermute | solution.py:489
  74.5 10.3 %all-to-all-start.2 = ((bf16[4,64,512]{2,1,0:T(8,128)(2,1)}), bf16[4,64,512]{2,1,0:T(8,128)(2,1)S(1)}, u32[]{:S(2)}, u32[]{:S(2)}) async-start(bf16[4,64,512]{2,1,0:T(8,128)(2,1)} %broadcast_in_dim.68), calls=%async_computation.2 | async-start | bytes 524288 | tf_op jit(solution)/shard_map/all_to_all | solution.py:408
  80.8 9.7 %collective-permute-start.6 = (bf16[2,160,512]{2,1,0:T(8,128)(2,1)S(1)}, bf16[2,160,512]{2,1,0:T(8,128)(2,1)S(1)}, u32[]{:S(2)}, u32[]{:S(2)}) collective-permute-start(bf16[2,160,512]{2,1,0:T(8,128)(2,1)S(1)} %add_convert_fusion.3.refs_1_), channel_id=1, source_target_pairs={{0,2},{1,3},{2,0},{3,1},{4,6},{5,7},{6,4},{7,5},{8,10},{9,11},{10,... | collective-permute-start | bytes 983048 | tf_op jit(solution)/shard_map/ppermute | solution.py:398
  86.0 34.2 %all-to-all-start.3 = ((bf16[8,64,1024]{2,1,0:T(8,128)(2,1)}), bf16[8,64,1024]{2,1,0:T(8,128)(2,1)S(1)}, u32[]{:S(2)}, u32[]{:S(2)}) async-start(bf16[8,64,1024]{2,1,0:T(8,128)(2,1)} %broadcast_in_dim.69), calls=%async_computation.3 | async-start | bytes 2097152 | tf_op jit(solution)/shard_map/all_to_all | solution.py:408
  103.1 13.5 %collective-permute-start.9 = (bf16[2,160,512]{2,1,0:T(8,128)(2,1)S(1)}, bf16[2,160,512]{2,1,0:T(8,128)(2,1)S(1)}, u32[]{:S(2)}, u32[]{:S(2)}) collective-permute-start(bf16[2,160,512]{2,1,0:T(8,128)(2,1)S(1)} %add_convert_fusion.2.refs_1_), channel_id=1, source_target_pairs={{0,2},{1,3},{2,0},{3,1},{4,6},{5,7},{6,4},{7,5},{8,10},{9,11},{10,... | collective-permute-start | bytes 983048 | tf_op jit(solution)/shard_map/ppermute | solution.py:398
  104.7 11.8 %collective-permute-start.11 = (bf16[160,512]{1,0:T(8,128)(2,1)S(1)}, bf16[160,512]{1,0:T(8,128)(2,1)S(1)}, u32[]{:S(2)}, u32[]{:S(2)}) collective-permute-start(bf16[160,512]{1,0:T(8,128)(2,1)S(1)} %copy-done.34), channel_id=1, source_target_pairs={{0,2},{1,3},{2,0},{3,1},{4,6},{5,7},{6,4},{7,5},{8,10},{9,11},{10,... | collective-permute-start | bytes 491528 | tf_op jit(solution)/shard_map/ppermute | solution.py:398
  130.1 10.1 %collective-permute-start.16 = (bf16[2,160,512]{2,1,0:T(8,128)(2,1)S(1)}, bf16[2,160,512]{2,1,0:T(8,128)(2,1)S(1)}, u32[]{:S(2)}, u32[]{:S(2)}) collective-permute-start(bf16[2,160,512]{2,1,0:T(8,128)(2,1)S(1)} %add_convert_fusion.1.refs_1_), channel_id=1, source_target_pairs={{0,2},{1,3},{2,0},{3,1},{4,6},{5,7},{6,4},{7,5},{8,10},{9,11},{10,... | collective-permute-start | bytes 983048 | tf_op jit(solution)/shard_map/ppermute | solution.py:398
  148.0 21.1 %collective-permute-start.13 = (bf16[2,160,512]{2,1,0:T(8,128)(2,1)}, bf16[2,160,512]{2,1,0:T(8,128)(2,1)S(1)}, u32[]{:S(2)}, u32[]{:S(2)}) collective-permute-start(bf16[2,160,512]{2,1,0:T(8,128)(2,1)} %get-tuple-element.80), channel_id=1, source_target_pairs={{0,1},{1,0},{2,3},{3,2},{4,5},{5,4},{6,7},{7,6},{8,9},{9,8},{10,11... | collective-permute-start | bytes 983048 | tf_op jit(solution)/shard_map/ppermute | solution.py:394
  153.4 11.1 %all-to-all-start.4 = ((bf16[4,64,256]{2,1,0:T(8,128)(2,1)}), bf16[4,64,256]{2,1,0:T(8,128)(2,1)S(1)}, u32[]{:S(2)}, u32[]{:S(2)}) async-start(bf16[4,64,256]{2,1,0:T(8,128)(2,1)} %bitcast.90), calls=%async_computation.4 | async-start | bytes 262144 | tf_op jit(solution)/shard_map/all_to_all | solution.py:558
  160.7 10.2 %collective-permute-start.18 = (bf16[2,160,512]{2,1,0:T(8,128)(2,1)}, bf16[2,160,512]{2,1,0:T(8,128)(2,1)S(1)}, u32[]{:S(2)}, u32[]{:S(2)}) collective-permute-start(bf16[2,160,512]{2,1,0:T(8,128)(2,1)} %get-tuple-element.91), channel_id=1, source_target_pairs={{0,1},{1,0},{2,3},{3,2},{4,5},{5,4},{6,7},{7,6},{8,9},{9,8},{10,11... | collective-permute-start | bytes 983048 | tf_op jit(solution)/shard_map/ppermute | solution.py:394
  164.6 60.6 %all-to-all-start.8 = ((bf16[8,64,1024]{2,1,0:T(8,128)(2,1)}), bf16[8,64,1024]{2,1,0:T(8,128)(2,1)S(1)}, u32[]{:S(2)}, u32[]{:S(2)}) async-start(bf16[8,64,1024]{2,1,0:T(8,128)(2,1)} %bitcast.38), calls=%async_computation.8 | async-start | bytes 2097152 | tf_op jit(solution)/shard_map/all_to_all | solution.py:414
  169.3 7.2 %collective-permute-start.14 = (bf16[160,512]{1,0:T(8,128)(2,1)S(1)}, bf16[160,512]{1,0:T(8,128)(2,1)S(1)}, u32[]{:S(2)}, u32[]{:S(2)}) collective-permute-start(bf16[160,512]{1,0:T(8,128)(2,1)S(1)} %fusion.7), channel_id=1, source_target_pairs={{0,2},{1,3},{2,0},{3,1},{4,6},{5,7},{6,4},{7,5},{8,10},{9,11},{10,... | collective-permute-start | bytes 491528 | tf_op jit(solution)/shard_map/ppermute | solution.py:398
  171.0 10.1 %collective-permute-start.19 = (bf16[2,160,512]{2,1,0:T(8,128)(2,1)S(1)}, bf16[2,160,512]{2,1,0:T(8,128)(2,1)S(1)}, u32[]{:S(2)}, u32[]{:S(2)}) collective-permute-start(bf16[2,160,512]{2,1,0:T(8,128)(2,1)S(1)} %add_convert_fusion.refs_1_), channel_id=1, source_target_pairs={{0,2},{1,3},{2,0},{3,1},{4,6},{5,7},{6,4},{7,5},{8,10},{9,11},{10,... | collective-permute-start | bytes 983048 | tf_op jit(solution)/shard_map/ppermute | solution.py:398
  185.5 23.2 %collective-permute-start.27 = (bf16[64,512]{1,0:T(8,128)(2,1)S(1)}, bf16[64,512]{1,0:T(8,128)(2,1)S(1)}, u32[]{:S(2)}, u32[]{:S(2)}) collective-permute-start(bf16[64,512]{1,0:T(8,128)(2,1)S(1)} %add_convert_fusion.4), channel_id=1, source_target_pairs={{0,2},{1,3},{2,0},{3,1},{4,6},{5,7},{6,4},{7,5},{8,10},{9,11},{10,... | collective-permute-start | bytes 196616 | tf_op jit(solution)/shard_map/ppermute | solution.py:398
  198.9 13.7 %collective-permute-start.21 = (bf16[640,256]{1,0:T(8,128)(2,1)}, bf16[640,256]{1,0:T(8,128)(2,1)S(1)}, u32[]{:S(2)}, u32[]{:S(2)}) collective-permute-start(bf16[640,256]{1,0:T(8,128)(2,1)} %get-tuple-element.96), channel_id=1, source_target_pairs={{20,8},{4,24},{21,9},{5,25},{22,10},{6,26},{23,11},{7,27}} | collective-permute-start | bytes 983048 | tf_op jit(solution)/shard_map/ppermute | solution.py:580
  199.6 14.7 %collective-permute-start.22 = (bf16[640,256]{1,0:T(8,128)(2,1)}, bf16[640,256]{1,0:T(8,128)(2,1)S(1)}, u32[]{:S(2)}, u32[]{:S(2)}) collective-permute-start(bf16[640,256]{1,0:T(8,128)(2,1)} %get-tuple-element.97), channel_id=1, source_target_pairs={{16,8},{20,12},{0,24},{4,28},{17,9},{21,13},{1,25},{5,29},{18,10},... | collective-permute-start | bytes 983048 | tf_op jit(solution)/shard_map/ppermute | solution.py:580
  206.0 14.4 %collective-permute-start.23 = (bf16[640,256]{1,0:T(8,128)(2,1)}, bf16[640,256]{1,0:T(8,128)(2,1)S(1)}, u32[]{:S(2)}, u32[]{:S(2)}) collective-permute-start(bf16[640,256]{1,0:T(8,128)(2,1)} %get-tuple-element.98), channel_id=1, source_target_pairs={{12,8},{16,12},{20,16},{28,24},{0,28},{4,0},{13,9},{17,13},{21,17}... | collective-permute-start | bytes 983048 | tf_op jit(solution)/shard_map/ppermute | solution.py:580
  225.2 7.4 %collective-permute-start.24 = (bf16[2,160,512]{2,1,0:T(8,128)(2,1)}, bf16[2,160,512]{2,1,0:T(8,128)(2,1)S(1)}, u32[]{:S(2)}, u32[]{:S(2)}) collective-permute-start(bf16[2,160,512]{2,1,0:T(8,128)(2,1)} %get-tuple-element.105), channel_id=1, source_target_pairs={{0,1},{1,0},{2,3},{3,2},{4,5},{5,4},{6,7},{7,6},{8,9},{9,8},{10,11... | collective-permute-start | bytes 983048 | tf_op jit(solution)/shard_map/ppermute | solution.py:394
  225.2 21.6 %all-to-all-start.7 = ((bf16[8,64,512]{2,1,0:T(8,128)(2,1)}), bf16[8,64,512]{2,1,0:T(8,128)(2,1)S(1)}, u32[]{:S(2)}, u32[]{:S(2)}) async-start(bf16[8,64,512]{2,1,0:T(8,128)(2,1)} %bitcast.35), calls=%async_computation.7 | async-start | bytes 1048576 | tf_op jit(solution)/shard_map/all_to_all | solution.py:414
  246.8 11.1 %all-to-all-start.5 = ((f32[32,1,512]{2,1,0:T(1,128)}), f32[32,1,512]{2,1,0:T(1,128)S(1)}, u32[]{:S(2)}, u32[]{:S(2)}) async-start(f32[32,1,512]{2,1,0:T(1,128)} %reshape.88), calls=%async_computation.5 | async-start | bytes 131072 | tf_op jit(solution)/shard_map/all_to_all | solution.py:602
  257.9 18.5 %all-to-all-start.6 = ((bf16[8,64,512]{2,1,0:T(8,128)(2,1)}), bf16[8,64,512]{2,1,0:T(8,128)(2,1)S(1)}, u32[]{:S(2)}, u32[]{:S(2)}) async-start(bf16[8,64,512]{2,1,0:T(8,128)(2,1)} %bitcast.31), calls=%async_computation.6 | async-start | bytes 1048576 | tf_op jit(solution)/shard_map/all_to_all | solution.py:414
  (60 other events, 441.0 us)

commit v3 on v2

v3 whole, which is shorter than its diff:
```python
import jax
import jax.numpy as jnp
from jax import lax
from jax.experimental import pallas as pl
from jax.experimental.pallas import tpu as pltpu
from jax.sharding import PartitionSpec as P

HEADS = 8
TRUNK_BLKS = 8
BRANCHES = 4
LEAVES = 2
eps = 1e-05
bf16 = jnp.bfloat16
f32 = jnp.float32
i32 = jnp.int32
NEG = -1e30


def mm(a, b):
    return lax.dot_general(a, b, (((1,), (0,)), ((), ())), preferred_element_type=f32)


def mm_tn(a, b):
    return lax.dot_general(a, b, (((0,), (0,)), ((), ())), preferred_element_type=f32)


def mm_nt(a, b):
    return lax.dot_general(a, b, (((1,), (1,)), ((), ())), preferred_element_type=f32)


def normalize(v):
    centered = v - jnp.mean(v, axis=-1, keepdims=True)
    inv = lax.rsqrt(jnp.mean(centered * centered, axis=-1, keepdims=True) + eps)
    return centered * inv, inv


def norm_back(grad_act, resid, gain):
    normed, inv = normalize(resid)
    scaled = grad_act * gain
    mean_g = jnp.mean(scaled, axis=-1, keepdims=True)
    mean_gx = jnp.mean(scaled * normed, axis=-1, keepdims=True)
    return inv * (scaled - mean_g - normed * mean_gx), jnp.sum(grad_act * normed, axis=0, keepdims=True)


def shaped(shape, dtype):
    return jax.ShapeDtypeStruct(shape, dtype)


class Cols:
    def __init__(self, ref, start, width):
        self.ref, self.cols, self.dtype = ref, slice(start, start + width), ref.dtype
        self.shape = (ref.shape[0], width)

    def __getitem__(self, key):
        return self.ref[:, self.cols]


def part(array, width, index):
    return (array, width * index, width)


def loading(body, n_scalars, n_loads, n_ins):
    def wrapped(*refs):
        sources = refs[n_scalars : n_scalars + n_loads]
        held = refs[len(refs) - n_loads - 1 : len(refs) - 1]
        sems = refs[-1]
        copies = [pltpu.make_async_copy(src, dst, sems.at[i]) for i, (src, dst) in enumerate(zip(sources, held))]
        for one in copies:
            one.start()
        for one in copies:
            one.wait()
        body(*refs[:n_scalars], *held, *refs[n_ins : len(refs) - n_loads - 1])

    return wrapped


def run(body, outs, ins, scratch=(), us=2, load=False, limit=24):
    arrays = [item[0] if isinstance(item, tuple) else item for item in ins]
    spaces = [pltpu.SMEM if array.dtype == i32 else (pltpu.HBM if load else pltpu.VMEM) for array in arrays]
    scratch = list(scratch)

    def wrapped(*refs):
        seen = [Cols(ref, item[1], item[2]) if isinstance(item, tuple) else ref for ref, item in zip(refs, ins)]
        body(*seen, *refs[len(ins) :])

    if load:
        loads = [array for array in arrays if array.dtype != i32]
        wrapped = loading(body, len(arrays) - len(loads), len(loads), len(arrays))
        scratch += [pltpu.VMEM(array.shape, array.dtype) for array in loads]
        scratch.append(pltpu.SemaphoreType.DMA((len(loads),)))
    return pl.pallas_call(
        wrapped,
        out_shape=outs,
        in_specs=[pl.BlockSpec(memory_space=space) for space in spaces],
        out_specs=[pl.BlockSpec(memory_space=pltpu.VMEM) for _ in outs],
        scratch_shapes=scratch,
        cost_estimate=pl.CostEstimate(flops=us * 3 * 10**9, bytes_accessed=10**6, transcendentals=0),
        compiler_params=pltpu.CompilerParams(vmem_limit_bytes=limit * 1024 * 1024),
    )(*arrays)


def pack_body(trees, n_first, steps, table, n_self, n_cross, n_ffn, *refs):
    weights, later, out, rest = refs[:n_first], refs[n_first:-2], refs[-2], refs[-1]
    at = 0
    for one in later:
        rest[:, at : at + one.shape[1]] = one[...]
        at += one.shape[1]
    lines = lax.broadcasted_iota(i32, table.shape, 0)
    full = table[...].astype(f32)
    small = [n_self[...].astype(f32), n_cross[...].astype(f32), n_ffn[...].astype(f32)]
    for i in range(trees):
        small.append(jnp.sum(jnp.where(lines == steps[i], full, 0.0), axis=0, keepdims=True))
    shard = table.shape[1]
    small.append(jnp.zeros((1, out.shape[2] - len(small) * shard), f32))
    tail = jnp.broadcast_to(jnp.concatenate(small, axis=1), (8, out.shape[2])).astype(bf16)
    for d in range(out.shape[0]):
        at = 0
        for one in weights:
            out[d, :shard, at : at + one.shape[1]] = one[...]
            at += one.shape[1]
        out[d, shard:, :] = tail


def assemble_body(slots, base, near, far, out):
    for i, ref in enumerate((near, far)):
        for k in range(ref.shape[0]):
            out[slots[base + i * ref.shape[0] + k]] = ref[k]


def project_body(sc, half, other, first, act, q, kv, rows, w):
    shard = first.shape[1] - 8
    count = first.shape[0]
    for d in range(count):
        w[d * shard : (d + 1) * shard, :] = first[d, :shard, :]
    tails = [first[d, shard:, :].astype(f32)[0:1] for d in range(count)]

    def line(k):
        return jnp.concatenate([one[:, k * shard : (k + 1) * shard] for one in tails], axis=1)

    trees = (first.shape[2] // shard) - 3
    time_row = jnp.zeros((1, count * shard), f32)
    for i in range(min(trees, rows.shape[0] - 4)):
        time_row = time_row + jnp.where(sc[4] == i, line(3 + i), 0.0)
    gain = line(0)
    rows[0:1, :] = gain
    rows[1:2, :] = line(1)
    rows[2:3, :] = line(2)
    rows[3:4, :] = time_row
    own_rows = half.shape[1]
    for k in range(4):
        src = half[k] if k < 2 else other[k - 2]
        normed, _ = normalize(src.astype(f32) + time_row)
        act[pl.ds(pl.multiple_of(sc[k], 16), own_rows), :] = (normed * gain).astype(bf16)
    cols = q.shape[1]
    result = mm(act[...], w[...]).astype(bf16)
    q[...] = result[:, :cols]
    kv[...] = result[:, cols:]


def fill_kv(buffer, parts):
    rows = parts[0].shape[0]
    for index, one in enumerate(parts):
        buffer[index * rows : (index + 1) * rows, :] = one[...]
    done = len(parts) * rows
    if buffer.shape[0] > done:
        buffer[done:, :] = jnp.zeros((buffer.shape[0] - done, buffer.shape[1]), buffer.dtype)


def self_scores(sc, buffer, own, qh, h, hd, block):
    count = qh.shape[0] // block
    col = h * hd
    start = pl.multiple_of(sc[5], block)
    trunk_rows = TRUNK_BLKS * block
    keys = buffer[pl.ds(start, trunk_rows), col : col + hd]
    trunk = mm_nt(keys, qh)
    query_block = lax.broadcasted_iota(i32, (1, qh.shape[0]), 1) // block + sc[6]
    pieces = []
    for j in range(TRUNK_BLKS):
        bias = jnp.where(query_block > j, 0.0, NEG)
        pieces.append(trunk[j * block : (j + 1) * block] + bias)
    key_pos = lax.broadcasted_iota(i32, (block, block), 0)
    query_pos = lax.broadcasted_iota(i32, (block, block), 1)
    own_s, par_s = [], []
    for i in range(count):
        q_i = qh[i * block : (i + 1) * block]
        o = mm_nt(own[i * block : (i + 1) * block, col : col + hd], q_i)
        own_s.append(jnp.where(key_pos <= query_pos, o, NEG))
        par = buffer[pl.ds(pl.multiple_of(sc[8 + i], block), block), col : col + hd]
        leaf = (lax.broadcasted_iota(i32, (1, block), 1) * 0 + sc[8 + count + i]) > 0
        par_s.append(mm_nt(par, q_i) + jnp.where(leaf, 0.0, NEG))
    pieces.append(jnp.concatenate(own_s, axis=1))
    pieces.append(jnp.concatenate(par_s, axis=1))
    return pieces, keys


def out_partial(sc, source, w, kept, sent):
    own_rows = kept.shape[1]
    for k in range(4):
        p = mm_nt(source[pl.ds(pl.multiple_of(sc[k], 16), own_rows), :], w[...])
        if k < 2:
            kept[k] = p
        else:
            sent[k - 2] = p.astype(bf16)


def self_body(block, heads, n_parts, sc, q, *refs):
    parts = refs[:n_parts]
    w = refs[n_parts]
    attn, lse, kept, sent, buffer = refs[n_parts + 1 :]
    own = parts[-1]
    fill_kv(buffer, parts)
    cols = q.shape[1]
    hd = cols // heads
    count = q.shape[0] // block
    trunk_rows = TRUNK_BLKS * block
    start = pl.multiple_of(sc[5], block)
    for h in range(heads):
        col = h * hd
        qh = q[:, col : col + hd] * jnp.asarray(hd**-0.5, bf16)
        pieces, _ = self_scores(sc, buffer, own, qh, h, hd, block)
        peak = pieces[0]
        for s in pieces[1:]:
            peak = jnp.maximum(peak, s)
        peak = jnp.max(peak, axis=0, keepdims=True)
        exps = [jnp.exp(s - peak) for s in pieces]
        total = exps[0]
        for e in exps[1:]:
            total = total + e
        total = jnp.sum(total, axis=0, keepdims=True)
        inv = 1.0 / total
        lse[h : h + 1, :] = peak + jnp.log(total)
        low = [(e * inv).astype(bf16) for e in exps]
        vals = buffer[pl.ds(start, trunk_rows), cols + col : cols + col + hd]
        mixed = mm_tn(jnp.concatenate(low[:TRUNK_BLKS], axis=0), vals)
        for i in range(count):
            rows = slice(i * block, (i + 1) * block)
            par = buffer[pl.ds(pl.multiple_of(sc[8 + i], block), block), cols + col : cols + col + hd]
            both = jnp.concatenate([low[TRUNK_BLKS][:, rows], low[TRUNK_BLKS + 1][:, rows]], axis=0)
            two = jnp.concatenate([own[rows, cols + col : cols + col + hd], par], axis=0)
            attn[rows, col : col + hd] = (mixed[rows] + mm_tn(both, two)).astype(bf16)
    out_partial(sc, attn, w, kept, sent)


def norm_body(first, time_at, gain_at, resid, chip, far, rows, resid_out, act):
    for k in range(2):
        base = resid[k].astype(f32)
        if first:
            base = base + rows[time_at : time_at + 1, :]
        v = base + (chip[k].astype(f32) + far[1 - k].astype(f32))
        resid_out[k] = v
        normed, _ = normalize(v)
        act[k] = (normed * rows[gain_at : gain_at + 1, :]).astype(bf16)


def both_halves(own, other):
    r, d = own.shape[1], own.shape[2]
    return jnp.concatenate([own[...].reshape(2 * r, d), other[...].reshape(2 * r, d)], axis=0)


def split_store(p, kept, sent):
    r = kept.shape[1]
    for k in range(2):
        kept[k] = p[k * r : (k + 1) * r]
        sent[k] = p[(2 + k) * r : (3 + k) * r].astype(bf16)


def cross_body(heads, n_enc, own, other, *refs):
    encs = refs[:n_enc]
    w, q, kv, low_out, lse, kept, sent = refs[n_enc:]
    act = both_halves(own, other)
    cols = q.shape[1]
    hd = cols // heads
    queries = mm(act, w[:, :cols]).astype(bf16)
    q[...] = queries
    pairs = mm(jnp.concatenate([enc[...] for enc in encs], axis=0), w[:, cols : 3 * cols]).astype(bf16)
    kv[...] = pairs
    for h in range(heads):
        sl = slice(h * hd, (h + 1) * hd)
        s = mm_nt(pairs[:, sl], queries[:, sl] * jnp.asarray(hd**-0.5, bf16))
        peak = jnp.max(s, axis=0, keepdims=True)
        e = jnp.exp(s - peak)
        total = jnp.sum(e, axis=0, keepdims=True)
        lse[h : h + 1, :] = peak + jnp.log(total)
        vals = pairs[:, cols + h * hd : cols + (h + 1) * hd]
        low_out[:, sl] = mm_tn((e * (1.0 / total)).astype(bf16), vals).astype(bf16)
    split_store(mm_nt(low_out[...], w[:, 3 * cols : 4 * cols]), kept, sent)


def ffn_body(own, other, g_own, g_other, up, down_t, hidden, grad_pre, kept, sent):
    r = own.shape[1]
    for k in range(4):
        act = own[k] if k < 2 else other[k - 2]
        top = g_own[k] if k < 2 else g_other[k - 2]
        pre = mm(act, up[...])
        cdf = 0.5 * (1.0 + lax.erf(pre * 0.7071067811865476))
        hidden[k * r : (k + 1) * r, :] = (pre * cdf).astype(bf16)
        slope = cdf + pre * (jnp.exp(-0.5 * pre * pre) * 0.3989422804014327)
        gp = (mm(top, down_t[...]) * slope).astype(bf16)
        grad_pre[k * r : (k + 1) * r, :] = gp
        p = mm_nt(gp, up[...])
        if k < 2:
            kept[k] = p
        else:
            sent[k - 2] = p.astype(bf16)


def relative(slots, base, scratch, value, kept, sent):
    scratch[...] = value.reshape(scratch.shape).astype(bf16)
    for i, ref in enumerate((kept, sent)):
        for k in range(ref.shape[0]):
            ref[k] = scratch[slots[base + i * ref.shape[0] + k]]


def grads_body(n_enc, slots, *refs):
    own, other, top_own, top_other, grad_q, low_in = refs[:6]
    encs, grad_encs = refs[6 : 6 + n_enc], refs[6 + n_enc : 6 + 2 * n_enc]
    ffn_own, ffn_other, g_own, g_other, hidden, grad_pre, near, far, scratch = refs[6 + 2 * n_enc :]
    sums = [
        mm_tn(both_halves(own, other), grad_q[...]),
        mm_tn(
            jnp.concatenate([one[...] for one in encs], axis=0), jnp.concatenate([one[...] for one in grad_encs], axis=0)
        ),
        mm_tn(both_halves(top_own, top_other), low_in[...]),
        mm_tn(both_halves(ffn_own, ffn_other), grad_pre[...]),
        mm_tn(both_halves(g_own, g_other), hidden[...]),
    ]
    relative(slots, 2 * near.shape[0], scratch, jnp.concatenate(sums, axis=1), near, far)


def out_body(hidden, down_t, kept, sent):
    split_store(mm_nt(hidden[...], down_t[...]), kept, sent)


def back_body(gain_at, base, chip, far, resid, rows, grad, low, dgain):
    for k in range(2):
        g = chip[k].astype(f32) + far[1 - k].astype(f32)
        back, sums = norm_back(g, resid[k], rows[gain_at : gain_at + 1, :])
        v = base[k].astype(f32) + back
        grad[k] = v
        low[k] = v.astype(bf16)
        if k == 0:
            dgain[...] = sums


def inner_rows(grad, out):
    return (grad.astype(f32) * out.astype(f32)).T


def cross_back_body(heads, g_own, g_other, q, kv, low_in, lse, w, grad_q, kept, sent, *grad_encs):
    top = both_halves(g_own, g_other)
    cols = q.shape[1]
    hd = cols // heads
    grad_mixed = mm(top, w[:, 3 * cols : 4 * cols]).astype(bf16)
    inner = inner_rows(grad_mixed, low_in[...])
    enc_rows = grad_encs[0].shape[0]
    for h in range(heads):
        sl = slice(h * hd, (h + 1) * hd)
        vl = slice(cols + h * hd, cols + (h + 1) * hd)
        qh = q[:, sl] * jnp.asarray(hd**-0.5, bf16)
        gh = grad_mixed[:, sl]
        probs = jnp.exp(mm_nt(kv[:, sl], qh) - lse[h : h + 1, :])
        grad_v = mm(probs.astype(bf16), gh).astype(bf16)
        delta = jnp.sum(inner[sl], axis=0, keepdims=True)
        ds = (probs * (mm_nt(kv[:, vl], gh) - delta)).astype(bf16)
        grad_k = mm(ds, qh).astype(bf16)
        for i, one in enumerate(grad_encs):
            one[:, sl] = grad_k[i * enc_rows : (i + 1) * enc_rows]
            one[:, vl] = grad_v[i * enc_rows : (i + 1) * enc_rows]
        grad_q[:, sl] = (mm_tn(ds, kv[:, sl]) * hd**-0.5).astype(bf16)
    split_store(mm_nt(grad_q[...], w[:, :cols]), kept, sent)


def enc_body(n_enc, w, *refs):
    parts, out = refs[:n_enc], refs[n_enc]
    total = parts[0][...].astype(f32)
    for one in parts[1:]:
        total = total + one[...].astype(f32)
    cols = total.shape[1] // 2
    out[...] = mm_nt(total.astype(bf16), w[:, cols : 3 * cols]).astype(bf16)


def self_back_body(block, heads, n_parts, sc, g_own, g_other, q, attn, lse, *refs):
    parts = refs[:n_parts]
    w = refs[n_parts]
    outs = refs[n_parts + 1 :]
    top, ds_trunk, ds_near, grad_own = outs[:4]
    remote = outs[4 : 4 + n_parts - 1]
    buffer, sums = outs[4 + n_parts - 1 :]
    own = parts[-1]
    fill_kv(buffer, parts)
    sums[...] = jnp.zeros(sums.shape, f32)
    own_rows = g_own.shape[1]
    for k in range(4):
        src = g_own[k] if k < 2 else g_other[k - 2]
        top[pl.ds(pl.multiple_of(sc[k], 16), own_rows), :] = src
    cols = q.shape[1]
    hd = cols // heads
    count = q.shape[0] // block
    trunk_rows = TRUNK_BLKS * block
    start = pl.multiple_of(sc[5], block)
    grad_attn = mm(top[...], w[...]).astype(bf16)
    inner = inner_rows(grad_attn, attn[...])
    rows_all = own.shape[0]
    base = (n_parts - 1) * rows_all
    for h in range(heads):
        col = h * hd
        sl, vl = slice(col, col + hd), slice(cols + col, cols + col + hd)
        qh = q[:, sl] * jnp.asarray(hd**-0.5, bf16)
        gh = grad_attn[:, sl]
        pieces, keys = self_scores(sc, buffer, own, qh, h, hd, block)
        delta = jnp.sum(inner[sl], axis=0, keepdims=True)
        level = lse[h : h + 1, :]
        vals = buffer[pl.ds(start, trunk_rows), vl]
        probs = jnp.exp(jnp.concatenate(pieces[:TRUNK_BLKS], axis=0) - level)
        ds = (probs * (mm_nt(vals, gh) - delta)).astype(bf16)
        ds_trunk[h] = ds
        sums[pl.ds(start, trunk_rows), sl] += mm(ds, qh)
        sums[pl.ds(start, trunk_rows), vl] += mm(probs.astype(bf16), gh)
        for i in range(count):
            rows = slice(i * block, (i + 1) * block)
            par_at = pl.ds(pl.multiple_of(sc[8 + i], block), block)
            own_at = slice(base + i * block, base + (i + 1) * block)
            q_i, g_i = qh[rows], gh[rows]
            near = ((pieces[TRUNK_BLKS], own_at), (pieces[TRUNK_BLKS + 1], par_at))
            for j, (piece, at) in enumerate(near):
                p = jnp.exp(piece[:, rows] - level[:, rows])
                d = (p * (mm_nt(buffer[at, vl], g_i) - delta[:, rows])).astype(bf16)
                ds_near[h, j, :, rows] = d
                sums[at, sl] += mm(d, q_i)
                sums[at, vl] += mm(p.astype(bf16), g_i)
    for index, one in enumerate(remote):
        one[...] = sums[index * rows_all : (index + 1) * rows_all, :].astype(bf16)
    grad_own[...] = sums[base : base + rows_all, :]


def self_rest_body(block, heads, n_parts, sc, act, top, attn, ds_trunk, ds_near, *refs):
    parts = refs[:n_parts]
    wq, sum_q, sum_o, grad_act, grad_q, buffer = refs[n_parts:]
    fill_kv(buffer, parts)
    own = parts[-1]
    cols = grad_q.shape[1]
    hd = cols // heads
    trunk_rows = TRUNK_BLKS * block
    start = pl.multiple_of(sc[5], block)
    for h in range(heads):
        sl = slice(h * hd, (h + 1) * hd)
        trunk = mm_tn(ds_trunk[h], buffer[pl.ds(start, trunk_rows), sl])
        for i in range(grad_q.shape[0] // block):
            rows = slice(i * block, (i + 1) * block)
            par = buffer[pl.ds(pl.multiple_of(sc[8 + i], block), block), sl]
            both = jnp.concatenate([ds_near[h, 0, :, rows], ds_near[h, 1, :, rows]], axis=0)
            near = mm_tn(both, jnp.concatenate([own[rows, sl], par], axis=0))
            grad_q[rows, sl] = ((trunk[rows] + near) * hd**-0.5).astype(bf16)
    sum_q[...] = mm_tn(act[...], grad_q[...])
    sum_o[...] = mm_tn(top[...], attn[...])
    grad_act[...] = mm_nt(grad_q[...], wq[...])


def self_end_body(n_parts, sc, slots, act, grad_own, *refs):
    remote = refs[: n_parts - 1]
    wk, wv, sum_q, sum_o, grad_act, near, far, kept, sent, total, scratch = refs[n_parts - 1 :]
    t = grad_own[...]
    for one in remote:
        t = t + one[...].astype(f32)
    total[...] = t.astype(bf16)
    cols = sum_q.shape[1]
    own_rows = kept.shape[1]
    for k in range(4):
        at = pl.ds(pl.multiple_of(sc[k], 16), own_rows)
        p = grad_act[at, :] + mm_nt(total[at, :cols], wk[...]) + mm_nt(total[at, cols:], wv[...])
        if k < 2:
            kept[k] = p
        else:
            sent[k - 2] = p.astype(bf16)
    weights = jnp.concatenate([sum_q[...], mm_tn(act[...], total[...]), sum_o[...]], axis=1)
    relative(slots, 2 * near.shape[0], scratch, weights, near, far)


def vector_body(trees, sc, kept, sent, half, other, grad_mid, rows, dgain_cross, dgain_ffn, out):
    gain = rows[0:1, :]
    dgain = jnp.zeros(gain.shape, f32)
    column = jnp.sum(grad_mid[0], axis=0, keepdims=True)
    for k in range(4):
        g = kept[k] if k < 2 else sent[k - 2].astype(f32)
        src = half[k] if k < 2 else other[k - 2]
        back, one = norm_back(g, src.astype(f32) + rows[3:4, :], gain)
        dgain = dgain + one
        column = column + jnp.sum(back, axis=0, keepdims=True)
    lines = lax.broadcasted_iota(i32, (out.shape[1], gain.shape[1]), 0)
    block = jnp.where(lines == 3 + sc[4], column, 0.0)
    for i, one in enumerate((dgain, dgain_cross[...], dgain_ffn[...])):
        block = jnp.where(lines == i, one, block)
    shard = out.shape[2]
    for d in range(out.shape[0]):
        out[d] = block[:, d * shard : (d + 1) * shard]


def last_body(chip, far, tokens, grad_mid, rows, grad_in):
    g = chip[0] + far[...].astype(f32)
    back, _ = norm_back(g, tokens[...].astype(f32) + rows[3:4, :], rows[0:1, :])
    grad_in[...] = grad_mid[0] + back


def small_body(trees, steps, slots, near, far, gains, table):
    me = slots[slots.shape[0] - 1]
    total = near[me] + far[me]
    gains[...] = total[:8]
    lines = lax.broadcasted_iota(i32, table.shape, 0)
    sums = jnp.zeros(table.shape, f32)
    for i in range(trees):
        sums = sums + jnp.where(lines == steps[i], total[3 + i : 4 + i], 0.0)
    table[...] = sums


def finish_pair_body(near, far, *outs):
    total = near[0].astype(f32) + far[0].astype(f32)
    at = 0
    for one in outs:
        one[...] = total[:, at : at + one.shape[1]]
        at += one.shape[1]


def xor_route(axis, bit):
    return [(i, i ^ bit) for i in range(lax.axis_size(axis))]


def sibling(x):
    return lax.ppermute(x, "tensor", xor_route("tensor", 1))


def across(x):
    return lax.ppermute(x, "tensor", xor_route("tensor", 2))


def chip_sum(kept, sent):
    return kept + sibling(sent).astype(f32)


def tie(x, *others):
    return lax.optimization_barrier((x, *others))[0]


def doubling(x):
    held = x[None]
    bit = lax.axis_size("dp") // 2
    while bit > 1:
        held = jnp.concatenate([held, lax.ppermute(held, "dp", xor_route("dp", bit))], axis=0)
        bit //= 2
    return held


def neighbour(x):
    return lax.ppermute(x, "dp", xor_route("dp", 1))


class Halving:
    def __init__(self, near, far):
        self.bit = 2
        self.near, self.received = near, neighbour(far)

    def step(self, *dues):
        self.received = tie(self.received, *dues)
        if self.bit >= lax.axis_size("dp"):
            return self.received
        total = (self.near.astype(f32) + self.received.astype(f32)).astype(bf16)
        middle = total.shape[0] // 2
        self.near = total[:middle]
        self.received = lax.ppermute(total[middle:], "dp", xor_route("dp", self.bit))
        self.bit *= 2
        return self.near

    def end(self, *dues):
        while self.bit < lax.axis_size("dp"):
            self.step(*dues)
        return self.near, tie(self.received, *dues)


def on_device(
    tokens_in, grad_out, enc_states, parents, tree_ids, timesteps, time_table, norm_self,
    w_query, w_key, w_value, w_out, norm_cross, c_query, c_key, c_value, c_out, norm_ffn,
    w_hidden, w_back,
):
    count = lax.axis_size("dp")
    tensor = lax.axis_size("tensor")
    heads = HEADS // tensor
    blocks_dev = parents.shape[0]
    tree_blocks = TRUNK_BLKS + BRANCHES * (1 + LEAVES)
    group = tree_blocks // blocks_dev
    hops_back = group - 1
    me = lax.axis_index("tensor")
    dp_index = lax.axis_index("dp")
    logical_dev = (dp_index - group // 2) % count
    trees = timesteps.shape[0]
    width = tokens_in.shape[1]
    own_rows = tokens_in.shape[0]
    token_rows = own_rows * tensor
    block = token_rows // blocks_dev
    shard = norm_self.shape[0]
    cols = w_query.shape[1]
    hidden_cols = w_hidden.shape[1]
    packed, rest = run(
        lambda *refs: pack_body(trees, 3, *refs),
        [shaped((count, shard + 8, 3 * cols), bf16), shaped((shard, 4 * cols + 2 * hidden_cols), bf16)],
        [
            timesteps, time_table, norm_self[None], norm_cross[None], norm_ffn[None],
            w_query, w_key, w_value, c_query, c_key, c_value, c_out.T, w_hidden, w_back.T,
        ],
        load=True,
        limit=60,
    )
    first = lax.all_to_all(packed, "dp", 0, 0)
    tokens_half = jnp.stack([tokens_in, across(tokens_in)])
    tokens_other = sibling(tokens_half)
    grad_half = jnp.stack([grad_out, across(grad_out)])
    grad_other = sibling(grad_half)
    rest_near = doubling(rest)

    def turn(distance):
        return [
            ((l + group // 2) % count, (l - l % group + (l + distance) % group + group // 2) % count)
            for l in range(count)
        ]

    position = logical_dev % group
    lead_blocks = group // 2 * blocks_dev
    parent_log = (parents - lead_blocks) % (count * blocks_dev)
    parent_rel = parent_log - logical_dev // group * tree_blocks
    query_block = position * blocks_dev + jnp.arange(blocks_dev, dtype=i32)
    is_leaf = query_block >= TRUNK_BLKS + BRANCHES
    shift = (hops_back - position) * blocks_dev
    parent_at = jnp.where(is_leaf, parent_rel, query_block) + shift
    step_id = jnp.sum(jnp.where(jnp.arange(trees, dtype=i32) == tree_ids[0], timesteps, 0))
    scalars = jnp.concatenate(
        [
            (me ^ jnp.array([0, 2, 1, 3], i32)) * own_rows,
            jnp.stack([tree_ids[0], shift * block, position * blocks_dev, step_id]),
            parent_at * block,
            is_leaf.astype(i32),
        ]
    ).astype(i32)
    bits = count.bit_length() - 1
    near_masks = [sum(((k >> j) & 1) * (count >> (j + 1)) for j in range(bits - 1)) for k in range(count // 2)]
    half_masks = [sum(((k >> j) & 1) * (count >> (j + 1)) for j in range(bits - 1)) for k in range(count // 2)]
    masks = near_masks + [m | 1 for m in near_masks] + half_masks + [m | 1 for m in half_masks] + [0]
    slots = (dp_index ^ jnp.array(masks, i32)).astype(i32)

    def assemble(near, far):
        far = far if far is not None else neighbour(near)
        (full,) = run(
            lambda *refs: assemble_body(refs[0], 0, *refs[1:]),
            [shaped((count,) + near.shape[1:], bf16)],
            [slots, near, far],
            us=1,
        )
        return full.reshape(width, near.shape[2])

    half = (2, own_rows, width)
    act_self, q, kv, rows, qkv_w = run(
        project_body,
        [
            shaped((token_rows, width), bf16), shaped((token_rows, cols), bf16),
            shaped((token_rows, 2 * cols), bf16), shaped((4 + trees, width), f32),
            shaped((width, 3 * cols), bf16),
        ],
        [scalars, tokens_half, tokens_other, first],
    )
    out_near = doubling(w_out.T)
    w_o = assemble(out_near, neighbour(out_near))

    def later(distance):
        return [
            ((l + group // 2) % count, (l + distance + group // 2) % count)
            for l in range(count)
            if l % group + distance < group
        ]

    parts = [lax.ppermute(kv, "dp", later(d)) for d in range(hops_back, 0, -1)] + [kv]
    buffer_rows = group * token_rows + max(0, TRUNK_BLKS - blocks_dev) * block
    cross_near, ffn_near = rest_near[:, :, : 4 * cols], rest_near[:, :, 4 * cols :]
    cross_far = neighbour(cross_near)
    q = tie(q, cross_far, grad_other)
    ffn_far = neighbour(ffn_near)
    attn, lse, kept, sent = run(
        lambda *refs: self_body(block, heads, group, *refs),
        [shaped((token_rows, cols), bf16), shaped((8, token_rows), f32), shaped(half, f32), shaped(half, bf16)],
        [scalars, q, *parts, w_o],
        [pltpu.VMEM((buffer_rows, 2 * cols), bf16)],
        us=5,
    )
    chip = chip_sum(kept, sent).astype(bf16)
    enc_rows = enc_states.shape[0]
    enc_sent = tie(enc_states, attn)
    enc_parts = [enc_states] + [lax.ppermute(enc_sent, "dp", turn(d)) for d in range(1, group)]
    resid_mid, act_own = run(
        lambda *refs: norm_body(True, 3, 1, *refs),
        [shaped(half, f32), shaped(half, bf16)],
        [tokens_half, chip, tie(across(chip), ffn_far, *enc_parts), rows],
        us=1,
    )
    act_other = sibling(act_own)
    rest_w = assemble(cross_near, cross_far)
    ffn_w = assemble(ffn_near, ffn_far)
    cross_q, cross_kv, cross_low, cross_lse, kept, sent = run(
        lambda *refs: cross_body(heads, group, *refs),
        [
            shaped((token_rows, cols), bf16), shaped((group * enc_rows, 2 * cols), bf16),
            shaped((token_rows, cols), bf16), shaped((8, token_rows), f32), shaped(half, f32), shaped(half, bf16),
        ],
        [act_own, act_other, *enc_parts, rest_w],
    )
    chip = chip_sum(kept, sent).astype(bf16)
    resid_ffn, ffn_own = run(
        lambda *refs: norm_body(False, 3, 2, *refs),
        [shaped(half, f32), shaped(half, bf16)],
        [resid_mid, chip, across(chip), rows],
        us=1,
    )
    ffn_other = sibling(ffn_own)
    hidden, grad_pre, kept, sent = run(
        ffn_body,
        [
            shaped((token_rows, hidden_cols), bf16), shaped((token_rows, hidden_cols), bf16),
            shaped(half, f32), shaped(half, bf16),
        ],
        [ffn_own, ffn_other, grad_half, grad_other, part(ffn_w, hidden_cols, 0), part(ffn_w, hidden_cols, 1)],
        us=3,
    )
    chip = chip_sum(kept, sent).astype(bf16)
    out_kept, out_sent = run(
        out_body, [shaped(half, f32), shaped(half, bf16)], [hidden, part(ffn_w, hidden_cols, 1)]
    )
    grad_resid_ffn, top_own, dgain_ffn = run(
        lambda *refs: back_body(2, *refs),
        [shaped(half, f32), shaped(half, bf16), shaped((1, width), f32)],
        [grad_half, chip, tie(across(chip), out_sent), resid_ffn, rows],
        us=1,
    )
    top_other = sibling(top_own)
    grad_cq, kept, sent, *grad_encs = run(
        lambda *refs: cross_back_body(heads, *refs),
        [shaped((token_rows, cols), bf16), shaped(half, f32), shaped(half, bf16)]
        + [shaped((enc_rows, 2 * cols), bf16)] * group,
        [top_own, top_other, cross_q, cross_kv, cross_low, cross_lse, rest_w],
        us=3,
    )
    chip = chip_sum(kept, sent).astype(bf16)
    split = (count // 2, shard, 4 * cols + 2 * hidden_cols)
    rest_kept, rest_sent = run(
        lambda *refs: grads_body(group, *refs),
        [shaped(split, bf16), shaped(split, bf16)],
        [
            slots, act_own, act_other, top_own, top_other, grad_cq, cross_low, *enc_parts, *grad_encs,
            ffn_own, ffn_other, grad_half, grad_other, hidden, grad_pre,
        ],
        [pltpu.VMEM((count, shard, split[2]), bf16)],
        us=4,
    )
    rest_chain = Halving(rest_kept, rest_sent)
    grad_encs = [grad_encs[0]] + [
        lax.ppermute(grad_encs[d], "dp", [(b, a) for a, b in turn(d)]) for d in range(1, group)
    ]
    grad_resid_mid, self_own, dgain_cross = run(
        lambda *refs: back_body(1, *refs),
        [shaped(half, f32), shaped(half, bf16), shaped((1, width), f32)],
        [grad_resid_ffn, chip, tie(across(chip), rest_sent), resid_mid, rows],
        us=1,
    )
    self_other = sibling(self_own)
    kv_shape = (token_rows, 2 * cols)
    top, ds_trunk, ds_near, grad_own, *remote = run(
        lambda *refs: self_back_body(block, heads, group, *refs),
        [
            shaped((token_rows, width), bf16), shaped((heads, TRUNK_BLKS * block, token_rows), bf16),
            shaped((heads, 2, block, token_rows), bf16), shaped(kv_shape, f32),
        ]
        + [shaped(kv_shape, bf16)] * hops_back,
        [scalars, self_own, self_other, q, attn, lse, *parts, w_o],
        [pltpu.VMEM((buffer_rows, 2 * cols), bf16), pltpu.VMEM((buffer_rows, 2 * cols), f32)],
        us=8,
    )
    back = [
        lax.ppermute(one, "dp", [(b, a) for a, b in later(d)]) for one, d in zip(remote, range(hops_back, 0, -1))
    ]
    sum_q, sum_o, grad_act = run(
        lambda *refs: self_rest_body(block, heads, group, *refs),
        [shaped((width, cols), f32), shaped((width, cols), f32), shaped((token_rows, width), f32)],
        [scalars, act_self, top, attn, ds_trunk, ds_near, *parts, part(qkv_w, cols, 0)],
        [pltpu.VMEM((token_rows, cols), bf16), pltpu.VMEM((buffer_rows, 2 * cols), bf16)],
        us=4,
    )
    held = rest_chain.step(grad_act)
    (enc_part,) = run(
        lambda *refs: enc_body(group, *refs),
        [shaped((enc_rows, width), bf16)],
        [rest_w, tie(grad_encs[0], ds_trunk), *grad_encs[1:]],
        us=1,
    )
    out_chip = chip_sum(out_kept, tie(out_sent, ds_trunk))
    output = (resid_ffn[0] + (out_chip[0] + across(out_chip[1].astype(bf16)).astype(f32))).astype(bf16)
    enc_chip = (enc_part.astype(f32) + sibling(enc_part).astype(f32)).astype(bf16)
    grad_enc = enc_chip.astype(f32) + across(enc_chip).astype(f32)
    grad_own = tie(grad_own, output, grad_enc, held)
    split = (count // 2, shard, 4 * cols)
    self_kept, self_sent, kept, sent = run(
        lambda *refs: self_end_body(group, *refs),
        [shaped(split, bf16), shaped(split, bf16), shaped(half, f32), shaped(half, bf16)],
        [
            scalars, slots, act_self, grad_own, *back, part(qkv_w, cols, 1), part(qkv_w, cols, 2), sum_q, sum_o, grad_act,
        ],
        [pltpu.VMEM(kv_shape, bf16), pltpu.VMEM((count, shard, 4 * cols), bf16)],
        us=3,
    )
    self_chain = Halving(self_kept, self_sent)
    rest_chain.step(sent)
    (vectors,) = run(
        lambda *refs: vector_body(trees, *refs),
        [shaped((count, -(-(3 + trees) // 8) * 8, shard), f32)],
        [scalars, kept, sent, tokens_half, tokens_other, grad_resid_mid, rows, dgain_cross, dgain_ffn],
    )
    chip = chip_sum(kept, sent)
    vectors = vectors + sibling(vectors)
    vectors = vectors + across(vectors)
    (grad_in,) = run(
        last_body,
        [shaped((own_rows, width), f32)],
        [chip, across(chip[1].astype(bf16)), tokens_in, grad_resid_mid, rows],
        us=1,
    )
    bit = 1
    vectors = tie(vectors, grad_in, self_chain.step(vectors))
    while bit < count // 2:
        vectors = vectors + lax.ppermute(vectors, "dp", xor_route("dp", bit))
        bit *= 2
        vectors = tie(vectors, self_chain.step(vectors))
    received = lax.ppermute(vectors, "dp", xor_route("dp", bit))
    self_sums, rest_sums = self_chain.end(), rest_chain.end()
    gains, grad_table = run(
        lambda *refs: small_body(trees, *refs),
        [shaped((8, shard), f32), shaped((time_table.shape[0], shard), f32)],
        [timesteps, slots, vectors, received],
        us=1,
    )
    square = shaped((shard, cols), f32)
    gq, gk, gv, go = run(finish_pair_body, [square] * 4, [*self_sums], us=1)
    wide = shaped((shard, hidden_cols), f32)
    gcq, gck, gcv, gco, gup, gdown = run(finish_pair_body, [square] * 4 + [wide] * 2, [*rest_sums], us=1)
    return (
        output, grad_in, grad_enc, grad_table, gains[0], gq, gk, gv, go.T, gains[1],
        gcq, gck, gcv, gco.T, gains[2], gup, gdown.T,
    )


def solution(mesh):
    rows, cols, repl = P(("dp", "tensor"), None), P("dp", "tensor"), P("tensor", "dp")
    in_specs = (
        rows, rows, P("dp", None), P("dp"), P("dp"), P(), P(None, "dp"), P("dp"), cols, cols, cols, repl,
        P("dp"), cols, cols, cols, repl, P("dp"), cols, repl,
    )
    out_specs = (
        rows, rows, P("dp", None), P(None, "dp"), P("dp"), cols, cols, cols, repl, P("dp"), cols, cols, cols,
        repl, P("dp"), cols, repl,
    )
    return jax.shard_map(on_device, mesh=mesh, in_specs=in_specs, out_specs=out_specs, check_vma=False)
```

time: 279 us -> 212 us (0.76)
  Pallas kernels: 59.9 us -> 36 us
  local copies, waits for them, and re-layouts: 22 us -> 1.45 us
  waiting for transfers between devices: 106 us -> 89.5 us
  other arithmetic: 9.52 us -> 3.33 us
  starting transfers between devices: 75.8 us -> 79.9 us
    ppermute x0 -> x22, waiting for transfers between devices: none -> 51.4 us  [the longest x5 22.7 us: neighbour(): return lax.ppermute(x, 'dp', xor_route('dp', 1))]
    all_to_all x9 -> x1, waiting for transfers between devices: 42.8 us -> 0.01 us  [on_device(): first = lax.all_to_all(packed, 'dp', 0, 0)]
    all_to_all x9 -> x1, starting transfers between devices: 46 us -> 3.95 us  [on_device(): first = lax.all_to_all(packed, 'dp', 0, 0)]
    ppermute x0 -> x22, starting transfers between devices: none -> 35.5 us  [the longest x5 9.12 us: neighbour(): return lax.ppermute(x, 'dp', xor_route('dp', 1))]
    pallas_call x15 -> x24, Pallas kernels: 59.9 us -> 36 us  [run(): pl.pallas_call(wrapped, out_shape=outs, in_specs=[pl.BlockSpec(memory_spa...]
    ppermute x3, waiting for transfers between devices: 16.9 us -> 0.01 us  [on_device(): lax.ppermute(kv, 'dp', later(d))]
    unnamed x103 -> x22, local copies, waits for them, and re-layouts: 12.2 us -> 0.05 us
    ppermute x3, starting transfers between devices: 8.94 us -> 18.2 us  [on_device(): lax.ppermute(one, 'dp', [(b, a) for a, b in later(d)])]
  transfers between devices with their start and end apart: 37 -> 53, of which waited for: 20 -> 25; matrix products, arithmetic and copies ran while one was open for 6% -> 2% of each run, Pallas kernels for 17% -> 11%
where the time goes in v3:
time: 212 us; the launch traced here: 211 us
  waiting for transfers between devices  89.5 us (42%)
  starting transfers between devices  79.9 us (38%)
  Pallas kernels  36 us (17%)
  other arithmetic  3.33 us (2%)
    pallas_call x24, Pallas kernels, run(): pl.pallas_call(wrapped, out_shape=outs, in_specs=[pl.BlockSpec(memory_spa...  36 us
    ppermute x10, waiting for transfers between devices, across(): return lax.ppermute(x, 'tensor', xor_route('tensor', 2))  29.7 us
    ppermute x5, waiting for transfers between devices, neighbour(): return lax.ppermute(x, 'dp', xor_route('dp', 1))  22.7 us
    ppermute x3, starting transfers between devices, on_device(): lax.ppermute(one, 'dp', [(b, a) for a, b in later(d)])  18.2 us
    ppermute x4, waiting for transfers between devices, doubling(): lax.ppermute(held, 'dp', xor_route('dp', bit))  14.9 us
    ppermute x10, starting transfers between devices, across(): return lax.ppermute(x, 'tensor', xor_route('tensor', 2))  14.3 us
    ppermute x5, starting transfers between devices, neighbour(): return lax.ppermute(x, 'dp', xor_route('dp', 1))  9.12 us
    ppermute x4, starting transfers between devices, doubling(): lax.ppermute(held, 'dp', xor_route('dp', bit))  8.62 us
  transfers between devices with their start and end apart: 53, of which 25 were waited for; matrix products, arithmetic and copies ran while one was open for 2% of the time, Pallas kernels for 11%

profile of v3, /device:TPU:0, one launch (start us, length us, event | category | flops | bytes accessed | tf_op | source)
XLA Modules:
  0.0 211.5 jit_solution(8518947015664623980)
XLA Ops:
  0.7 4.1 %collective-permute-start.10 = (bf16[1,64,128]{2,1,0:T(8,128)(2,1)}, bf16[1,64,128]{2,1,0:T(8,128)(2,1)S(1)}, u32[]{:S(2)}, u32[]{:S(2)}) collective-permute-start(bf16[1,64,128]{2,1,0:T(8,128)(2,1)} %bitcast.60), channel_id=1, source_target_pairs={{0,16},{4,20},{8,24},{12,28},{16,0},{20,4},{24,8},{28,12},{1,17},{... | collective-permute-start | bytes 49160 | tf_op jit(solution)/shard_map/ppermute | solution.py:547
  9.7 4.0 %all-to-all-start = ((bf16[8,72,384]{2,1,0:T(8,128)(2,1)}), bf16[8,72,384]{2,1,0:T(8,128)(2,1)S(1)}, u32[]{:S(2)}, u32[]{:S(2)}) async-start(bf16[8,72,384]{2,1,0:T(8,128)(2,1)} %get-tuple-element.101), calls=%async_computation | async-start | bytes 884736 | tf_op jit(solution)/shard_map/all_to_all | solution.py:611
  13.6 2.9 %collective-permute-start.2 = (bf16[1,64,1536]{2,1,0:T(8,128)(2,1)}, bf16[1,64,1536]{2,1,0:T(8,128)(2,1)S(1)}, u32[]{:S(2)}, u32[]{:S(2)}) collective-permute-start(bf16[1,64,1536]{2,1,0:T(8,128)(2,1)} %bitcast.53), channel_id=1, source_target_pairs={{0,16},{4,20},{8,24},{12,28},{16,0},{20,4},{24,8},{28,12},{1,17},{... | collective-permute-start | bytes 589832 | tf_op jit(solution)/shard_map/ppermute | solution.py:547
  19.6 5.4 %collective-permute-done.11 = bf16[2,64,128]{2,1,0:T(8,128)(2,1)S(1)} collective-permute-done((bf16[2,64,128]{2,1,0:T(8,128)(2,1)S(1)}, bf16[2,64,128]{2,1,0:T(8,128)(2,1)S(1)}, u32[]{:S(2)}, u32[]{:S(2)}) %collective-permute-start.11) | collective-permute-done | bytes 32800 | tf_op jit(solution)/shard_map/ppermute | solution.py:547
  27.5 6.4 %collective-permute-done.2 = bf16[1,64,1536]{2,1,0:T(8,128)(2,1)S(1)} collective-permute-done((bf16[1,64,1536]{2,1,0:T(8,128)(2,1)}, bf16[1,64,1536]{2,1,0:T(8,128)(2,1)S(1)}, u32[]{:S(2)}, u32[]{:S(2)}) %collective-permute-start.2) | collective-permute-done | bytes 196640 | tf_op jit(solution)/shard_map/ppermute | solution.py:547
  35.7 3.4 %collective-permute-start.9 = (bf16[640,256]{1,0:T(8,128)(2,1)S(1)}, bf16[640,256]{1,0:T(8,128)(2,1)S(1)}, u32[]{:S(2)}, u32[]{:S(2)}) collective-permute-start(bf16[640,256]{1,0:T(8,128)(2,1)S(1)} %get-tuple-element.105.refs_5_.refs_9_), channel_id=1, source_target_pairs={{8,12},{12,16},{16,20},{24,28},{28,0},{0,4},{9,13},{13,17},{17,21}... | collective-permute-start | bytes 983048 | tf_op jit(solution)/shard_map/ppermute | solution.py:677
  40.4 3.1 %collective-permute-done.3 = bf16[2,64,1536]{2,1,0:T(8,128)(2,1)S(1)} collective-permute-done((bf16[2,64,1536]{2,1,0:T(8,128)(2,1)S(1)}, bf16[2,64,1536]{2,1,0:T(8,128)(2,1)S(1)}, u32[]{:S(2)}, u32[]{:S(2)}) %collective-permute-start.3) | collective-permute-done | bytes 393248 | tf_op jit(solution)/shard_map/ppermute | solution.py:547
  47.6 9.9 %collective-permute-done.4.refs_2_ = bf16[4,64,512]{2,1,0:T(8,128)(2,1)S(1)} collective-permute-done((bf16[4,64,512]{2,1,0:T(8,128)(2,1)S(1)}, bf16[4,64,512]{2,1,0:T(8,128)(2,1)S(1)}, u32[]{:S(2)}, u32[]{:S(2)}) %collective-permute-start.4) | collective-permute-done | bytes 262176 | tf_op jit(solution)/shard_map/ppermute | solution.py:553
  57.5 4.5 %shard_map.344 = (bf16[640,128]{1,0:T(8,128)(2,1)S(1)}, f32[8,640]{1,0:T(8,128)S(1)}, f32[2,160,512]{2,1,0:T(8,128)S(1)}, bf16[2,160,512]{2,1,0:T(8,128)(2,1)S(1)}) custom-call(s32[18]{0:T(128)S(1)} %concatenate.17.refs_0_, bf16[640,128]{1,0:T(8,128)(2,1)S(1)} %get-tuple-element.104.refs_1_.refs_3_, ...), custom_call_target="tpu_custom_call" | custom-call | flops 15000000512 | bytes 1000000 | tf_op jit(solution)/shard_map/pallas_call | solution.py:91
  66.6 4.5 %collective-permute-start.17 = (bf16[64,512]{1,0:T(8,128)(2,1)S(1)}, bf16[64,512]{1,0:T(8,128)(2,1)S(1)}, u32[]{:S(2)}, u32[]{:S(2)}) collective-permute-start(bf16[64,512]{1,0:T(8,128)(2,1)S(1)} %copy-done.1), channel_id=1, source_target_pairs={{8,16},{12,20},{16,8},{20,12},{24,0},{28,4},{0,24},{4,28},{9,17},{... | collective-permute-start | bytes 196616 | tf_op jit(solution)/shard_map/ppermute | solution.py:693
  71.2 7.8 %collective-permute-done.15.refs_2_ = bf16[4,64,1024]{2,1,0:T(8,128)(2,1)S(1)} collective-permute-done((bf16[4,64,1024]{2,1,0:T(8,128)(2,1)S(1)}, bf16[4,64,1024]{2,1,0:T(8,128)(2,1)S(1)}, u32[]{:S(2)}, u32[]{:S(2)}) %collective-permute-start.15) | collective-permute-done | bytes 524320 | tf_op jit(solution)/shard_map/ppermute | solution.py:553
  87.2 8.3 %collective-permute-done.21.refs_2_ = bf16[2,160,512]{2,1,0:T(8,128)(2,1)S(1)} collective-permute-done((bf16[2,160,512]{2,1,0:T(8,128)(2,1)S(1)}, bf16[2,160,512]{2,1,0:T(8,128)(2,1)S(1)}, u32[]{:S(2)}, u32[]{:S(2)}) %collective-permute-start.21) | collective-permute-done | bytes 327712 | tf_op jit(solution)/shard_map/ppermute | solution.py:532
  103.2 7.7 %collective-permute-done.24.refs_2_ = bf16[2,160,512]{2,1,0:T(8,128)(2,1)S(1)} collective-permute-done((bf16[2,160,512]{2,1,0:T(8,128)(2,1)S(1)}, bf16[2,160,512]{2,1,0:T(8,128)(2,1)S(1)}, u32[]{:S(2)}, u32[]{:S(2)}) %collective-permute-start.24) | collective-permute-done | bytes 327712 | tf_op jit(solution)/shard_map/ppermute | solution.py:532
  120.5 6.2 %collective-permute-done.27.refs_2_ = bf16[2,160,512]{2,1,0:T(8,128)(2,1)S(1)} collective-permute-done((bf16[2,160,512]{2,1,0:T(8,128)(2,1)S(1)}, bf16[2,160,512]{2,1,0:T(8,128)(2,1)S(1)}, u32[]{:S(2)}, u32[]{:S(2)}) %collective-permute-start.27) | collective-permute-done | bytes 327712 | tf_op jit(solution)/shard_map/ppermute | solution.py:532
  127.8 4.5 %collective-permute-start.32 = (bf16[64,256]{1,0:T(8,128)(2,1)S(1)}, bf16[64,256]{1,0:T(8,128)(2,1)S(1)}, u32[]{:S(2)}, u32[]{:S(2)}) collective-permute-start(bf16[64,256]{1,0:T(8,128)(2,1)S(1)} %get-tuple-element.135.refs_13_), channel_id=1, source_target_pairs={{16,8},{20,12},{8,16},{12,20},{0,24},{4,28},{24,0},{28,4},{17,9},{... | collective-permute-start | bytes 98312 | tf_op jit(solution)/shard_map/ppermute | solution.py:760
  133.8 6.0 %shard_map.356 = (bf16[640,512]{1,0:T(8,128)(2,1)S(1)}, bf16[2,1024,640]{2,1,0:T(8,128)(2,1)S(1)}, bf16[2,2,128,640]{3,2,1,0:T(8,128)(2,1)S(1)}, f32[640,256]{1,...) custom-call(s32[18]{0:T(128)S(1)} %concatenate.17.refs_0_, ...), custom_call_target="tpu_custom_call" | custom-call | flops 24000000000 | bytes 1000000 | tf_op jit(solution)/shard_map/pallas_call | solution.py:91
  141.3 6.4 %collective-permute-start.38 = (bf16[640,256]{1,0:T(8,128)(2,1)S(1)}, bf16[640,256]{1,0:T(8,128)(2,1)S(1)}, u32[]{:S(2)}, u32[]{:S(2)}) collective-permute-start(bf16[640,256]{1,0:T(8,128)(2,1)S(1)} %get-tuple-element.155), channel_id=1, source_target_pairs={{16,8},{20,12},{0,24},{4,28},{17,9},{21,13},{1,25},{5,29},{18,10},... | collective-permute-start | bytes 983048 | tf_op jit(solution)/shard_map/ppermute | solution.py:782
  152.4 11.1 %collective-permute-start.39 = (bf16[640,256]{1,0:T(8,128)(2,1)S(1)}, bf16[640,256]{1,0:T(8,128)(2,1)S(1)}, u32[]{:S(2)}, u32[]{:S(2)}) collective-permute-start(bf16[640,256]{1,0:T(8,128)(2,1)S(1)} %get-tuple-element.156), channel_id=1, source_target_pairs={{12,8},{16,12},{20,16},{28,24},{0,28},{4,0},{13,9},{17,13},{21,17}... | collective-permute-start | bytes 983048 | tf_op jit(solution)/shard_map/ppermute | solution.py:782
  170.4 3.2 %collective-permute-done.30 = bf16[160,512]{1,0:T(8,128)(2,1)S(1)} collective-permute-done((bf16[160,512]{1,0:T(8,128)(2,1)S(1)}, bf16[160,512]{1,0:T(8,128)(2,1)S(1)}, u32[]{:S(2)}, u32[]{:S(2)}) %collective-permute-start.30) | collective-permute-done | bytes 163872 | tf_op jit(solution)/shard_map/ppermute | solution.py:532
  180.4 3.0 %collective-permute-start.51 = (bf16[1,64,1536]{2,1,0:T(8,128)(2,1)S(1)}, bf16[1,64,1536]{2,1,0:T(8,128)(2,1)S(1)}, u32[]{:S(2)}, u32[]{:S(2)}) collective-permute-start(bf16[1,64,1536]{2,1,0:T(8,128)(2,1)S(1)} %get-tuple-element.185), channel_id=1, source_target_pairs={{0,16},{4,20},{8,24},{12,28},{16,0},{20,4},{24,8},{28,12},{1,17},{... | collective-permute-start | bytes 589832 | tf_op jit(solution)/shard_map/ppermute | solution.py:568
  183.3 2.9 %collective-permute-done.44 = bf16[4,64,512]{2,1,0:T(8,128)(2,1)S(1)} collective-permute-done((bf16[4,64,512]{2,1,0:T(8,128)(2,1)S(1)}, bf16[4,64,512]{2,1,0:T(8,128)(2,1)S(1)}, u32[]{:S(2)}, u32[]{:S(2)}) %collective-permute-start.44) | collective-permute-done | bytes 262176 | tf_op jit(solution)/shard_map/ppermute | solution.py:553
  193.3 3.4 %collective-permute-done.45 = f32[8,8,64]{2,1,0:T(8,128)S(1)} collective-permute-done((f32[8,8,64]{2,1,0:T(8,128)S(1)}, f32[8,8,64]{2,1,0:T(8,128)S(1)}, u32[]{:S(2)}, u32[]{:S(2)}) %collective-permute-start.45) | collective-permute-done | bytes 16416 | tf_op jit(solution)/shard_map/ppermute | solution.py:832
  200.8 4.2 %collective-permute-done.48.refs_1_ = bf16[1,64,512]{2,1,0:T(8,128)(2,1)S(1)} collective-permute-done((bf16[1,64,512]{2,1,0:T(8,128)(2,1)S(1)}, bf16[1,64,512]{2,1,0:T(8,128)(2,1)S(1)}, u32[]{:S(2)}, u32[]{:S(2)}) %collective-permute-start.48) | collective-permute-done | bytes 65568 | tf_op jit(solution)/shard_map/ppermute | solution.py:568
  205.6 4.2 %collective-permute-done.49.refs_3_ = f32[8,8,64]{2,1,0:T(8,128)S(1)} collective-permute-done((f32[8,8,64]{2,1,0:T(8,128)S(1)}, f32[8,8,64]{2,1,0:T(8,128)S(1)}, u32[]{:S(2)}, u32[]{:S(2)}) %collective-permute-start.49) | collective-permute-done | bytes 16416 | tf_op jit(solution)/shard_map/ppermute | solution.py:835
  (165 shorter events, 83.3 us)
Async XLA Ops:
  0.7 16.6 %collective-permute-start.10 = (bf16[1,64,128]{2,1,0:T(8,128)(2,1)}, bf16[1,64,128]{2,1,0:T(8,128)(2,1)S(1)}, u32[]{:S(2)}, u32[]{:S(2)}) collective-permute-start(bf16[1,64,128]{2,1,0:T(8,128)(2,1)} %bitcast.60), channel_id=1, source_target_pairs={{0,16},{4,20},{8,24},{12,28},{16,0},{20,4},{24,8},{28,12},{1,17},{... | collective-permute-start | bytes 49160 | tf_op jit(solution)/shard_map/ppermute | solution.py:547
  4.8 22.2 %collective-permute-start.5 = (bf16[160,512]{1,0:T(8,128)(2,1)}, bf16[160,512]{1,0:T(8,128)(2,1)S(1)}, u32[]{:S(2)}, u32[]{:S(2)}) collective-permute-start(bf16[160,512]{1,0:T(8,128)(2,1)} %param.23), channel_id=1, source_target_pairs={{0,2},{1,3},{2,0},{3,1},{4,6},{5,7},{6,4},{7,5},{8,10},{9,11},{10,... | collective-permute-start | bytes 491528 | tf_op jit(solution)/shard_map/ppermute | solution.py:532
  6.3 20.6 %collective-permute-start = (bf16[160,512]{1,0:T(8,128)(2,1)}, bf16[160,512]{1,0:T(8,128)(2,1)S(1)}, u32[]{:S(2)}, u32[]{:S(2)}) collective-permute-start(bf16[160,512]{1,0:T(8,128)(2,1)} %refs_2_.3), channel_id=1, source_target_pairs={{0,2},{1,3},{2,0},{3,1},{4,6},{5,7},{6,4},{7,5},{8,10},{9,11},{10,... | collective-permute-start | bytes 491528 | tf_op jit(solution)/shard_map/ppermute | solution.py:532
  9.7 24.4 %all-to-all-start = ((bf16[8,72,384]{2,1,0:T(8,128)(2,1)}), bf16[8,72,384]{2,1,0:T(8,128)(2,1)S(1)}, u32[]{:S(2)}, u32[]{:S(2)}) async-start(bf16[8,72,384]{2,1,0:T(8,128)(2,1)} %get-tuple-element.101), calls=%async_computation | async-start | bytes 884736 | tf_op jit(solution)/shard_map/all_to_all | solution.py:611
  13.6 20.3 %collective-permute-start.2 = (bf16[1,64,1536]{2,1,0:T(8,128)(2,1)}, bf16[1,64,1536]{2,1,0:T(8,128)(2,1)S(1)}, u32[]{:S(2)}, u32[]{:S(2)}) collective-permute-start(bf16[1,64,1536]{2,1,0:T(8,128)(2,1)} %bitcast.53), channel_id=1, source_target_pairs={{0,16},{4,20},{8,24},{12,28},{16,0},{20,4},{24,8},{28,12},{1,17},{... | collective-permute-start | bytes 589832 | tf_op jit(solution)/shard_map/ppermute | solution.py:547
  25.0 19.2 %collective-permute-start.12 = (bf16[4,64,128]{2,1,0:T(8,128)(2,1)S(1)}, bf16[4,64,128]{2,1,0:T(8,128)(2,1)S(1)}, u32[]{:S(2)}, u32[]{:S(2)}) collective-permute-start(bf16[4,64,128]{2,1,0:T(8,128)(2,1)S(1)} %pad_maximum_fusion.6.refs_1_), channel_id=1, source_target_pairs={{0,4},{4,0},{8,12},{12,8},{16,20},{20,16},{24,28},{28,24},{1,5},{5... | collective-permute-start | bytes 196616 | tf_op jit(solution)/shard_map/ppermute | solution.py:553
  27.0 20.6 %collective-permute-start.6 = (bf16[2,160,512]{2,1,0:T(8,128)(2,1)S(1)}, bf16[2,160,512]{2,1,0:T(8,128)(2,1)S(1)}, u32[]{:S(2)}, u32[]{:S(2)}) collective-permute-start(bf16[2,160,512]{2,1,0:T(8,128)(2,1)S(1)} %pad_maximum_fusion.4.refs_2_.refs_0_.refs_17_), channel_id=1, source_target_pairs={{0,1},{1,0},{2,3},{3,2},{4,5},{5,4},{6,7},{7,6},{8,9},{9,8},{10,11... | collective-permute-start | bytes 983048 | tf_op jit(solution)/shard_map/ppermute | solution.py:528
  35.7 21.8 %collective-permute-start.9 = (bf16[640,256]{1,0:T(8,128)(2,1)S(1)}, bf16[640,256]{1,0:T(8,128)(2,1)S(1)}, u32[]{:S(2)}, u32[]{:S(2)}) collective-permute-start(bf16[640,256]{1,0:T(8,128)(2,1)S(1)} %get-tuple-element.105.refs_5_.refs_9_), channel_id=1, source_target_pairs={{8,12},{12,16},{16,20},{24,28},{28,0},{0,4},{9,13},{13,17},{17,21}... | collective-permute-start | bytes 983048 | tf_op jit(solution)/shard_map/ppermute | solution.py:677
  39.1 18.4 %collective-permute-start.8 = (bf16[640,256]{1,0:T(8,128)(2,1)S(1)}, bf16[640,256]{1,0:T(8,128)(2,1)S(1)}, u32[]{:S(2)}, u32[]{:S(2)}) collective-permute-start(bf16[640,256]{1,0:T(8,128)(2,1)S(1)} %get-tuple-element.105.refs_5_.refs_9_), channel_id=1, source_target_pairs={{8,16},{12,20},{24,0},{28,4},{9,17},{13,21},{25,1},{29,5},{10,18},... | collective-permute-start | bytes 983048 | tf_op jit(solution)/shard_map/ppermute | solution.py:677
  43.5 14.1 %collective-permute-start.7 = (bf16[640,256]{1,0:T(8,128)(2,1)S(1)}, bf16[640,256]{1,0:T(8,128)(2,1)S(1)}, u32[]{:S(2)}, u32[]{:S(2)}) collective-permute-start(bf16[640,256]{1,0:T(8,128)(2,1)S(1)} %get-tuple-element.105.refs_5_.refs_9_), channel_id=1, source_target_pairs={{8,20},{24,4},{9,21},{25,5},{10,22},{26,6},{11,23},{27,7}} | collective-permute-start | bytes 983048 | tf_op jit(solution)/shard_map/ppermute | solution.py:677
  44.2 13.3 %collective-permute-start.4 = (bf16[4,64,512]{2,1,0:T(8,128)(2,1)S(1)}, bf16[4,64,512]{2,1,0:T(8,128)(2,1)S(1)}, u32[]{:S(2)}, u32[]{:S(2)}) collective-permute-start(bf16[4,64,512]{2,1,0:T(8,128)(2,1)S(1)} %pad_maximum_fusion.5.refs_1_), channel_id=1, source_target_pairs={{0,4},{4,0},{8,12},{12,8},{16,20},{20,16},{24,28},{28,24},{1,5},{5... | collective-permute-start | bytes 786440 | tf_op jit(solution)/shard_map/ppermute | solution.py:553
  62.2 16.7 %collective-permute-start.15 = (bf16[4,64,1024]{2,1,0:T(8,128)(2,1)S(1)}, bf16[4,64,1024]{2,1,0:T(8,128)(2,1)S(1)}, u32[]{:S(2)}, u32[]{:S(2)}) collective-permute-start(bf16[4,64,1024]{2,1,0:T(8,128)(2,1)S(1)} %pad_maximum_fusion.refs_1_), channel_id=1, source_target_pairs={{0,4},{4,0},{8,12},{12,8},{16,20},{20,16},{24,28},{28,24},{1,5},{5... | collective-permute-start | bytes 1572872 | tf_op jit(solution)/shard_map/ppermute | solution.py:553
  64.9 15.3 %collective-permute-start.14 = (bf16[2,160,512]{2,1,0:T(8,128)(2,1)S(1)}, bf16[2,160,512]{2,1,0:T(8,128)(2,1)S(1)}, u32[]{:S(2)}, u32[]{:S(2)}) collective-permute-start(bf16[2,160,512]{2,1,0:T(8,128)(2,1)S(1)} %add_convert_fusion.5.refs_1_), channel_id=1, source_target_pairs={{0,2},{1,3},{2,0},{3,1},{4,6},{5,7},{6,4},{7,5},{8,10},{9,11},{10,... | collective-permute-start | bytes 983048 | tf_op jit(solution)/shard_map/ppermute | solution.py:532
  66.4 13.7 %collective-permute-start.18 = (bf16[64,512]{1,0:T(8,128)(2,1)S(1)}, bf16[64,512]{1,0:T(8,128)(2,1)S(1)}, u32[]{:S(2)}, u32[]{:S(2)}) collective-permute-start(bf16[64,512]{1,0:T(8,128)(2,1)S(1)} %copy-done.1), channel_id=1, source_target_pairs={{8,20},{12,8},{16,12},{20,16},{24,4},{28,24},{0,28},{4,0},{9,21},{... | collective-permute-start | bytes 196616 | tf_op jit(solution)/shard_map/ppermute | solution.py:693
  66.6 13.5 %collective-permute-start.17 = (bf16[64,512]{1,0:T(8,128)(2,1)S(1)}, bf16[64,512]{1,0:T(8,128)(2,1)S(1)}, u32[]{:S(2)}, u32[]{:S(2)}) collective-permute-start(bf16[64,512]{1,0:T(8,128)(2,1)S(1)} %copy-done.1), channel_id=1, source_target_pairs={{8,16},{12,20},{16,8},{20,12},{24,0},{28,4},{0,24},{4,28},{9,17},{... | collective-permute-start | bytes 196616 | tf_op jit(solution)/shard_map/ppermute | solution.py:693
  127.3 12.5 %collective-permute-start.31 = (bf16[64,256]{1,0:T(8,128)(2,1)S(1)}, bf16[64,256]{1,0:T(8,128)(2,1)S(1)}, u32[]{:S(2)}, u32[]{:S(2)}) collective-permute-start(bf16[64,256]{1,0:T(8,128)(2,1)S(1)} %get-tuple-element.134.refs_12_), channel_id=1, source_target_pairs={{12,8},{16,12},{20,16},{8,20},{28,24},{0,28},{4,0},{24,4},{13,9},{... | collective-permute-start | bytes 98312 | tf_op jit(solution)/shard_map/ppermute | solution.py:760
  132.3 20.0 %collective-permute-start.36 = (bf16[4,64,1536]{2,1,0:T(8,128)(2,1)S(1)}, bf16[4,64,1536]{2,1,0:T(8,128)(2,1)S(1)}, u32[]{:S(2)}, u32[]{:S(2)}) collective-permute-start(bf16[4,64,1536]{2,1,0:T(8,128)(2,1)S(1)} %get-tuple-element.138), channel_id=1, source_target_pairs={{0,4},{4,0},{8,12},{12,8},{16,20},{20,16},{24,28},{28,24},{1,5},{5... | collective-permute-start | bytes 2359304 | tf_op jit(solution)/shard_map/ppermute | solution.py:553
  140.0 23.7 %collective-permute-start.34 = (bf16[64,512]{1,0:T(8,128)(2,1)S(1)}, bf16[64,512]{1,0:T(8,128)(2,1)S(1)}, u32[]{:S(2)}, u32[]{:S(2)}) collective-permute-start(bf16[64,512]{1,0:T(8,128)(2,1)S(1)} %shard_map.357), channel_id=1, source_target_pairs={{0,1},{1,0},{2,3},{3,2},{4,5},{5,4},{6,7},{7,6},{8,9},{9,8},{10,11... | collective-permute-start | bytes 196616 | tf_op jit(solution)/shard_map/ppermute | solution.py:528
  140.1 23.8 %collective-permute-start.29 = (bf16[2,160,512]{2,1,0:T(8,128)(2,1)S(1)}, bf16[2,160,512]{2,1,0:T(8,128)(2,1)S(1)}, u32[]{:S(2)}, u32[]{:S(2)}) collective-permute-start(bf16[2,160,512]{2,1,0:T(8,128)(2,1)S(1)} %get-tuple-element.143), channel_id=1, source_target_pairs={{0,1},{1,0},{2,3},{3,2},{4,5},{5,4},{6,7},{7,6},{8,9},{9,8},{10,11... | collective-permute-start | bytes 983048 | tf_op jit(solution)/shard_map/ppermute | solution.py:528
  140.6 33.7 %collective-permute-start.37 = (bf16[640,256]{1,0:T(8,128)(2,1)S(1)}, bf16[640,256]{1,0:T(8,128)(2,1)S(1)}, u32[]{:S(2)}, u32[]{:S(2)}) collective-permute-start(bf16[640,256]{1,0:T(8,128)(2,1)S(1)} %get-tuple-element.154), channel_id=1, source_target_pairs={{20,8},{4,24},{21,9},{5,25},{22,10},{6,26},{23,11},{7,27}} | collective-permute-start | bytes 983048 | tf_op jit(solution)/shard_map/ppermute | solution.py:782
  141.3 33.0 %collective-permute-start.38 = (bf16[640,256]{1,0:T(8,128)(2,1)S(1)}, bf16[640,256]{1,0:T(8,128)(2,1)S(1)}, u32[]{:S(2)}, u32[]{:S(2)}) collective-permute-start(bf16[640,256]{1,0:T(8,128)(2,1)S(1)} %get-tuple-element.155), channel_id=1, source_target_pairs={{16,8},{20,12},{0,24},{4,28},{17,9},{21,13},{1,25},{5,29},{18,10},... | collective-permute-start | bytes 983048 | tf_op jit(solution)/shard_map/ppermute | solution.py:782
  152.4 21.9 %collective-permute-start.39 = (bf16[640,256]{1,0:T(8,128)(2,1)S(1)}, bf16[640,256]{1,0:T(8,128)(2,1)S(1)}, u32[]{:S(2)}, u32[]{:S(2)}) collective-permute-start(bf16[640,256]{1,0:T(8,128)(2,1)S(1)} %get-tuple-element.156), channel_id=1, source_target_pairs={{12,8},{16,12},{20,16},{28,24},{0,28},{4,0},{13,9},{17,13},{21,17}... | collective-permute-start | bytes 983048 | tf_op jit(solution)/shard_map/ppermute | solution.py:782
  163.8 14.7 %collective-permute-start.50 = (bf16[2,64,1536]{2,1,0:T(8,128)(2,1)S(1)}, bf16[2,64,1536]{2,1,0:T(8,128)(2,1)S(1)}, u32[]{:S(2)}, u32[]{:S(2)}) collective-permute-start(bf16[2,64,1536]{2,1,0:T(8,128)(2,1)S(1)} %slice.83), channel_id=1, source_target_pairs={{0,8},{4,12},{8,0},{12,4},{16,24},{20,28},{24,16},{28,20},{1,9},{5... | collective-permute-start | bytes 1179656 | tf_op jit(solution)/shard_map/ppermute | solution.py:568
  180.4 13.0 %collective-permute-start.51 = (bf16[1,64,1536]{2,1,0:T(8,128)(2,1)S(1)}, bf16[1,64,1536]{2,1,0:T(8,128)(2,1)S(1)}, u32[]{:S(2)}, u32[]{:S(2)}) collective-permute-start(bf16[1,64,1536]{2,1,0:T(8,128)(2,1)S(1)} %get-tuple-element.185), channel_id=1, source_target_pairs={{0,16},{4,20},{8,24},{12,28},{16,0},{20,4},{24,8},{28,12},{1,17},{... | collective-permute-start | bytes 589832 | tf_op jit(solution)/shard_map/ppermute | solution.py:568
  (40 other events, 303.3 us)

commit v4 on v3

--- a/solution.py
+++ b/solution.py
@@ -94,17 +94,18 @@
         in_specs=[pl.BlockSpec(memory_space=space) for space in spaces],
         out_specs=[pl.BlockSpec(memory_space=pltpu.VMEM) for _ in outs],
         scratch_shapes=scratch,
-        cost_estimate=pl.CostEstimate(flops=us * 3 * 10**9, bytes_accessed=10**6, transcendentals=0),
+        cost_estimate=pl.CostEstimate(flops=us * 50 * 10**6, bytes_accessed=10**6, transcendentals=0),
         compiler_params=pltpu.CompilerParams(vmem_limit_bytes=limit * 1024 * 1024),
     )(*arrays)
 
 
 def pack_body(trees, n_first, steps, table, n_self, n_cross, n_ffn, *refs):
-    weights, later, out, rest = refs[:n_first], refs[n_first:-2], refs[-2], refs[-1]
-    at = 0
-    for one in later:
-        rest[:, at : at + one.shape[1]] = one[...]
-        at += one.shape[1]
+    weights, later, out, outs = refs[:n_first], refs[n_first:-3], refs[-3], refs[-2:]
+    for group, one in ((later[:5], outs[0]), (later[5:], outs[1])):
+        at = 0
+        for piece in group:
+            one[:, at : at + piece.shape[1]] = piece[...]
+            at += piece.shape[1]
     lines = lax.broadcasted_iota(i32, table.shape, 0)
     full = table[...].astype(f32)
     small = [n_self[...].astype(f32), n_cross[...].astype(f32), n_ffn[...].astype(f32)]
@@ -476,7 +477,7 @@
     relative(slots, 2 * near.shape[0], scratch, weights, near, far)
 
 
-def vector_body(trees, sc, kept, sent, half, other, grad_mid, rows, dgain_cross, dgain_ffn, out):
+def vector_body(tensor, trees, sc, kept, sent, half, other, grad_mid, rows, dgain_cross, dgain_ffn, out):
     gain = rows[0:1, :]
     dgain = jnp.zeros(gain.shape, f32)
     column = jnp.sum(grad_mid[0], axis=0, keepdims=True)
@@ -491,8 +492,9 @@
     for i, one in enumerate((dgain, dgain_cross[...], dgain_ffn[...])):
         block = jnp.where(lines == i, one, block)
     shard = out.shape[2]
-    for d in range(out.shape[0]):
-        out[d] = block[:, d * shard : (d + 1) * shard]
+    for d in range(out.shape[0] // tensor):
+        for t in range(tensor):
+            out[d * tensor + t] = block[:, d * shard : (d + 1) * shard]
 
 
 def last_body(chip, far, tokens, grad_mid, rows, grad_in):
@@ -501,9 +503,10 @@
     grad_in[...] = grad_mid[0] + back
 
 
-def small_body(trees, steps, slots, near, far, gains, table):
-    me = slots[slots.shape[0] - 1]
-    total = near[me] + far[me]
+def small_body(trees, steps, received, gains, table):
+    total = received[0]
+    for k in range(1, received.shape[0]):
+        total = total + received[k]
     gains[...] = total[:8]
     lines = lax.broadcasted_iota(i32, table.shape, 0)
     sums = jnp.zeros(table.shape, f32)
@@ -540,13 +543,28 @@
     return lax.optimization_barrier((x, *others))[0]
 
 
-def doubling(x):
-    held = x[None]
-    bit = lax.axis_size("dp") // 2
-    while bit > 1:
-        held = jnp.concatenate([held, lax.ppermute(held, "dp", xor_route("dp", bit))], axis=0)
-        bit //= 2
-    return held
+class Doubling:
+    def __init__(self, x):
+        self.held = x[None]
+        self.bit = lax.axis_size("dp") // 2
+        self.received = None
+        self.send()
+
+    def send(self):
+        if self.bit > 1:
+            self.received = lax.ppermute(self.held, "dp", xor_route("dp", self.bit))
+
+    def step(self, *dues):
+        if self.bit > 1:
+            self.held = jnp.concatenate([self.held, tie(self.received, *dues)], axis=0)
+            self.bit //= 2
+            self.send()
+        return self.held
+
+    def end(self, *dues):
+        while self.bit > 1:
+            self.step(*dues)
+        return self.held
 
 
 def neighbour(x):
@@ -598,22 +616,23 @@
     shard = norm_self.shape[0]
     cols = w_query.shape[1]
     hidden_cols = w_hidden.shape[1]
-    packed, rest = run(
+    packed, cross_pack, ffn_pack = run(
         lambda *refs: pack_body(trees, 3, *refs),
-        [shaped((count, shard + 8, 3 * cols), bf16), shaped((shard, 4 * cols + 2 * hidden_cols), bf16)],
+        [shaped((count, shard + 8, 3 * cols), bf16), shaped((shard, 5 * cols), bf16), shaped((shard, 2 * hidden_cols), bf16)],
         [
             timesteps, time_table, norm_self[None], norm_cross[None], norm_ffn[None],
-            w_query, w_key, w_value, c_query, c_key, c_value, c_out.T, w_hidden, w_back.T,
+            w_query, w_key, w_value, c_query, c_key, c_value, c_out.T, w_out.T, w_hidden, w_back.T,
         ],
         load=True,
         limit=60,
     )
     first = lax.all_to_all(packed, "dp", 0, 0)
-    tokens_half = jnp.stack([tokens_in, across(tokens_in)])
+    tokens_half = jnp.stack([tokens_in, across(tie(tokens_in, packed))])
     tokens_other = sibling(tokens_half)
-    grad_half = jnp.stack([grad_out, across(grad_out)])
+    grad_half = jnp.stack([grad_out, across(tie(grad_out, packed))])
     grad_other = sibling(grad_half)
-    rest_near = doubling(rest)
+    cross_chain = Doubling(cross_pack)
+    ffn_chain = Doubling(ffn_pack)
 
     def turn(distance):
         return [
@@ -664,8 +683,10 @@
         ],
         [scalars, tokens_half, tokens_other, first],
     )
-    out_near = doubling(w_out.T)
-    w_o = assemble(out_near, neighbour(out_near))
+    cross_chain.step(kv)
+    cross_near = cross_chain.end()
+    rest_w = assemble(cross_near, neighbour(cross_near))
+    w_o = part(rest_w, cols, 4)
 
     def later(distance):
         return [
@@ -676,10 +697,9 @@
 
     parts = [lax.ppermute(kv, "dp", later(d)) for d in range(hops_back, 0, -1)] + [kv]
     buffer_rows = group * token_rows + max(0, TRUNK_BLKS - blocks_dev) * block
-    cross_near, ffn_near = rest_near[:, :, : 4 * cols], rest_near[:, :, 4 * cols :]
-    cross_far = neighbour(cross_near)
-    q = tie(q, cross_far, grad_other)
-    ffn_far = neighbour(ffn_near)
+    ffn_chain.step(kv)
+    ffn_near = ffn_chain.end()
+    q = tie(q, grad_other)
     attn, lse, kept, sent = run(
         lambda *refs: self_body(block, heads, group, *refs),
         [shaped((token_rows, cols), bf16), shaped((8, token_rows), f32), shaped(half, f32), shaped(half, bf16)],
@@ -687,10 +707,11 @@
         [pltpu.VMEM((buffer_rows, 2 * cols), bf16)],
         us=5,
     )
-    chip = chip_sum(kept, sent).astype(bf16)
     enc_rows = enc_states.shape[0]
     enc_sent = tie(enc_states, attn)
     enc_parts = [enc_states] + [lax.ppermute(enc_sent, "dp", turn(d)) for d in range(1, group)]
+    chip = chip_sum(kept, sent).astype(bf16)
+    ffn_far = neighbour(tie(ffn_near, attn))
     resid_mid, act_own = run(
         lambda *refs: norm_body(True, 3, 1, *refs),
         [shaped(half, f32), shaped(half, bf16)],
@@ -698,8 +719,8 @@
         us=1,
     )
     act_other = sibling(act_own)
-    rest_w = assemble(cross_near, cross_far)
     ffn_w = assemble(ffn_near, ffn_far)
+    up_w, down_w = part(ffn_w, hidden_cols, 0), part(ffn_w, hidden_cols, 1)
     cross_q, cross_kv, cross_low, cross_lse, kept, sent = run(
         lambda *refs: cross_body(heads, group, *refs),
         [
@@ -712,7 +733,7 @@
     resid_ffn, ffn_own = run(
         lambda *refs: norm_body(False, 3, 2, *refs),
         [shaped(half, f32), shaped(half, bf16)],
-        [resid_mid, chip, across(chip), rows],
+        [resid_mid, chip, tie(across(chip)), rows],
         us=1,
     )
     ffn_other = sibling(ffn_own)
@@ -722,12 +743,12 @@
             shaped((token_rows, hidden_cols), bf16), shaped((token_rows, hidden_cols), bf16),
             shaped(half, f32), shaped(half, bf16),
         ],
-        [ffn_own, ffn_other, grad_half, grad_other, part(ffn_w, hidden_cols, 0), part(ffn_w, hidden_cols, 1)],
+        [ffn_own, ffn_other, grad_half, grad_other, up_w, down_w],
         us=3,
     )
     chip = chip_sum(kept, sent).astype(bf16)
     out_kept, out_sent = run(
-        out_body, [shaped(half, f32), shaped(half, bf16)], [hidden, part(ffn_w, hidden_cols, 1)]
+        out_body, [shaped(half, f32), shaped(half, bf16)], [hidden, down_w]
     )
     grad_resid_ffn, top_own, dgain_ffn = run(
         lambda *refs: back_body(2, *refs),
@@ -749,23 +770,33 @@
         lambda *refs: grads_body(group, *refs),
         [shaped(split, bf16), shaped(split, bf16)],
         [
-            slots, act_own, act_other, top_own, top_other, grad_cq, cross_low, *enc_parts, *grad_encs,
+            slots, tie(act_own, chip), act_other, top_own, top_other, grad_cq, cross_low, *enc_parts, *grad_encs,
             ffn_own, ffn_other, grad_half, grad_other, hidden, grad_pre,
         ],
         [pltpu.VMEM((count, shard, split[2]), bf16)],
         us=4,
     )
     rest_chain = Halving(rest_kept, rest_sent)
+    out_chip = out_kept + sibling(tie(out_sent, chip)).astype(f32)
     grad_encs = [grad_encs[0]] + [
-        lax.ppermute(grad_encs[d], "dp", [(b, a) for a, b in turn(d)]) for d in range(1, group)
+        lax.ppermute(tie(grad_encs[d], rest_sent), "dp", [(b, a) for a, b in turn(d)]) for d in range(1, group)
     ]
     grad_resid_mid, self_own, dgain_cross = run(
         lambda *refs: back_body(1, *refs),
         [shaped(half, f32), shaped(half, bf16), shaped((1, width), f32)],
-        [grad_resid_ffn, chip, tie(across(chip), rest_sent), resid_mid, rows],
+        [grad_resid_ffn, chip, tie(across(chip), rest_sent, out_chip), resid_mid, rows],
         us=1,
     )
+    (enc_part,) = run(
+        lambda *refs: enc_body(group, *refs),
+        [shaped((enc_rows, width), bf16)],
+        [rest_w, grad_encs[0], *grad_encs[1:]],
+        us=1,
+    )
+    enc_chip = (enc_part.astype(f32) + sibling(enc_part).astype(f32)).astype(bf16)
+    enc_far = across(enc_chip)
     self_other = sibling(self_own)
+    out_far = across(tie(out_chip[1].astype(bf16), self_own))
     kv_shape = (token_rows, 2 * cols)
     top, ds_trunk, ds_near, grad_own, *remote = run(
         lambda *refs: self_back_body(block, heads, group, *refs),
@@ -789,17 +820,7 @@
         us=4,
     )
     held = rest_chain.step(grad_act)
-    (enc_part,) = run(
-        lambda *refs: enc_body(group, *refs),
-        [shaped((enc_rows, width), bf16)],
-        [rest_w, tie(grad_encs[0], ds_trunk), *grad_encs[1:]],
-        us=1,
-    )
-    out_chip = chip_sum(out_kept, tie(out_sent, ds_trunk))
-    output = (resid_ffn[0] + (out_chip[0] + across(out_chip[1].astype(bf16)).astype(f32))).astype(bf16)
-    enc_chip = (enc_part.astype(f32) + sibling(enc_part).astype(f32)).astype(bf16)
-    grad_enc = enc_chip.astype(f32) + across(enc_chip).astype(f32)
-    grad_own = tie(grad_own, output, grad_enc, held)
+    grad_own = tie(grad_own, held)
     split = (count // 2, shard, 4 * cols)
     self_kept, self_sent, kept, sent = run(
         lambda *refs: self_end_body(group, *refs),
@@ -811,33 +832,28 @@
         us=3,
     )
     self_chain = Halving(self_kept, self_sent)
-    rest_chain.step(sent)
+    chip = chip_sum(kept, sent)
     (vectors,) = run(
-        lambda *refs: vector_body(trees, *refs),
-        [shaped((count, -(-(3 + trees) // 8) * 8, shard), f32)],
-        [scalars, kept, sent, tokens_half, tokens_other, grad_resid_mid, rows, dgain_cross, dgain_ffn],
-    )
-    chip = chip_sum(kept, sent)
-    vectors = vectors + sibling(vectors)
-    vectors = vectors + across(vectors)
+        lambda *refs: vector_body(tensor, trees, *refs),
+        [shaped((count * tensor, -(-(3 + trees) // 8) * 8, shard), f32)],
+        [scalars, tie(kept, chip), sent, tokens_half, tokens_other, grad_resid_mid, rows, dgain_cross, dgain_ffn],
+    )
+    received = lax.all_to_all(vectors, ("dp", "tensor"), 0, 0)
     (grad_in,) = run(
         last_body,
         [shaped((own_rows, width), f32)],
         [chip, across(chip[1].astype(bf16)), tokens_in, grad_resid_mid, rows],
         us=1,
     )
-    bit = 1
-    vectors = tie(vectors, grad_in, self_chain.step(vectors))
-    while bit < count // 2:
-        vectors = vectors + lax.ppermute(vectors, "dp", xor_route("dp", bit))
-        bit *= 2
-        vectors = tie(vectors, self_chain.step(vectors))
-    received = lax.ppermute(vectors, "dp", xor_route("dp", bit))
+    self_chain.step()
+    rest_chain.step(sent)
+    output = (resid_ffn[0] + (out_chip[0] + out_far.astype(f32))).astype(bf16)
+    grad_enc = enc_chip.astype(f32) + enc_far.astype(f32)
     self_sums, rest_sums = self_chain.end(), rest_chain.end()
     gains, grad_table = run(
         lambda *refs: small_body(trees, *refs),
         [shaped((8, shard), f32), shaped((time_table.shape[0], shard), f32)],
-        [timesteps, slots, vectors, received],
+        [timesteps, received],
         us=1,
     )
     square = shaped((shard, cols), f32)

time: 212 us -> 190 us (0.90)
  waiting for transfers between devices: 89.5 us -> 75.4 us
  starting transfers between devices: 79.9 us -> 67.5 us
  other arithmetic: 3.33 us -> 6.98 us
    ppermute x10 -> x7, waiting for transfers between devices: 23.4 us -> 3.61 us  [the longest x3 3.33 us: on_device(): lax.ppermute(tie(grad_encs[d], rest_sent), 'dp', [(b, a) for a, b in turn...]
    ppermute x3, starting transfers between devices: 18.2 us -> 6.26 us  [on_device(): lax.ppermute(one, 'dp', [(b, a) for a, b in later(d)])]
    ppermute x10 -> x9, waiting for transfers between devices: 29.7 us -> 18.5 us  [across(): return lax.ppermute(x, 'tensor', xor_route('tensor', 2))]
    ppermute x3, waiting for transfers between devices: 1.22 us -> 9 us  [on_device(): lax.ppermute(enc_sent, 'dp', turn(d))]
    ppermute x10 -> x7, starting transfers between devices: 16.2 us -> 9.92 us  [the longest x3 5.03 us: on_device(): lax.ppermute(tie(grad_encs[d], rest_sent), 'dp', [(b, a) for a, b in turn...]
    ppermute x5 -> x4, waiting for transfers between devices: 22.7 us -> 16.4 us  [neighbour(): return lax.ppermute(x, 'dp', xor_route('dp', 1))]
    all_to_all x1, waiting for transfers between devices: 0.01 us -> 6.04 us  [on_device(): first = lax.all_to_all(packed, 'dp', 0, 0)]
    ppermute x4, starting transfers between devices: 5.36 us -> 10.5 us  [step(): lax.ppermute(total[middle:], 'dp', xor_route('dp', self.bit))]
  transfers between devices with their start and end apart: 53 -> 48, of which waited for: 25 -> 19; matrix products, arithmetic and copies ran while one was open for 2% -> 5% of each run, Pallas kernels for 11% -> 13%
where the time goes in v4:
time: 190 us; the launch traced here: 189 us
  waiting for transfers between devices  75.4 us (40%)
  starting transfers between devices  67.5 us (36%)
  Pallas kernels  35.2 us (19%)
  other arithmetic  6.98 us (4%)
  local copies, waits for them, and re-layouts  2.8 us (1%)
    pallas_call x23, Pallas kernels, run(): pl.pallas_call(wrapped, out_shape=outs, in_specs=[pl.BlockSpec(memory_spa...  35.2 us
    ppermute x9, waiting for transfers between devices, across(): return lax.ppermute(x, 'tensor', xor_route('tensor', 2))  18.5 us
    ppermute x4, waiting for transfers between devices, neighbour(): return lax.ppermute(x, 'dp', xor_route('dp', 1))  16.4 us
    ppermute x9, starting transfers between devices, across(): return lax.ppermute(x, 'tensor', xor_route('tensor', 2))  12 us
    ppermute x4, starting transfers between devices, step(): lax.ppermute(total[middle:], 'dp', xor_route('dp', self.bit))  10.5 us
    ppermute x13, waiting for transfers between devices, sibling(): return lax.ppermute(x, 'tensor', xor_route('tensor', 1))  9.55 us
    ppermute x3, waiting for transfers between devices, on_device(): lax.ppermute(enc_sent, 'dp', turn(d))  9 us
    all_to_all x1, starting transfers between devices, on_device(): first = lax.all_to_all(packed, 'dp', 0, 0)  7.42 us
  transfers between devices with their start and end apart: 48, of which 19 were waited for; matrix products, arithmetic and copies ran while one was open for 5% of the time, Pallas kernels for 13%

profile of v4, /device:TPU:0, one launch (start us, length us, event | category | flops | bytes accessed | tf_op | source)
XLA Modules:
  0.0 189.1 jit_solution(562709110795386165)
XLA Ops:
  0.7 2.8 %shard_map.341 = (bf16[8,72,384]{2,1,0:T(8,128)(2,1)}, bf16[64,640]{1,0:T(8,128)(2,1)}, bf16[64,1024]{1,0:T(8,128)(2,1)}) custom-call(s32[2]{0:T(128)} %refs_0_.3, bf16[50,64]{1,0:T(8,128)(2,1)} %refs_1_.1, bf16[1,64]{1,0:T(2,128)(2,1)} %bitcast.67, bf16[1,64]{1,0:T(2,128)(2,1)} %bitcast.68, bf16[1,64]{1,0:T(2,128)(2,1)} %bitcast.69, ...), custom_call_target="tpu_custom_call" | custom-call | flops 100000000 | bytes 1000000 | tf_op jit(solution)/shard_map/pallas_call | solution.py:91
  3.5 7.4 %all-to-all-start = ((bf16[8,72,384]{2,1,0:T(8,128)(2,1)}), bf16[8,72,384]{2,1,0:T(8,128)(2,1)S(1)}, u32[]{:S(2)}, u32[]{:S(2)}) async-start(bf16[8,72,384]{2,1,0:T(8,128)(2,1)} %get-tuple-element.106), calls=%async_computation | async-start | bytes 884736 | tf_op jit(solution)/shard_map/all_to_all | solution.py:629
  11.0 2.9 %collective-permute-start.7 = (bf16[1,64,640]{2,1,0:T(8,128)(2,1)}, bf16[1,64,640]{2,1,0:T(8,128)(2,1)S(1)}, u32[]{:S(2)}, u32[]{:S(2)}) collective-permute-start(bf16[1,64,640]{2,1,0:T(8,128)(2,1)} %bitcast.54), channel_id=1, source_target_pairs={{0,16},{4,20},{8,24},{12,28},{16,0},{20,4},{24,8},{28,12},{1,17},{... | collective-permute-start | bytes 245768 | tf_op jit(solution)/shard_map/ppermute | solution.py:555
  23.7 6.0 %all-to-all-done.refs_3_ = bf16[8,72,384]{2,1,0:T(8,128)(2,1)S(1)} async-done(((bf16[8,72,384]{2,1,0:T(8,128)(2,1)}), bf16[8,72,384]{2,1,0:T(8,128)(2,1)S(1)}, u32[]{:S(2)}, u32[]{:S(2)}) %all-to-all-start) | async-done | bytes 442400 | tf_op jit(solution)/shard_map/all_to_all | solution.py:629
  31.7 3.0 %collective-permute-start.6 = (bf16[640,256]{1,0:T(8,128)(2,1)S(1)}, bf16[640,256]{1,0:T(8,128)(2,1)S(1)}, u32[]{:S(2)}, u32[]{:S(2)}) collective-permute-start(bf16[640,256]{1,0:T(8,128)(2,1)S(1)} %get-tuple-element.111.refs_5_.refs_9_), channel_id=1, source_target_pairs={{8,12},{12,16},{16,20},{24,28},{28,0},{0,4},{9,13},{13,17},{17,21}... | collective-permute-start | bytes 983048 | tf_op jit(solution)/shard_map/ppermute | solution.py:698
  40.0 16.4 %collective-permute-done.9.refs_2_ = bf16[4,64,640]{2,1,0:T(8,128)(2,1)S(1)} collective-permute-done((bf16[4,64,640]{2,1,0:T(8,128)(2,1)S(1)}, bf16[4,64,640]{2,1,0:T(8,128)(2,1)S(1)}, u32[]{:S(2)}, u32[]{:S(2)}) %collective-permute-start.9) | collective-permute-done | bytes 327712 | tf_op jit(solution)/shard_map/ppermute | solution.py:571
  57.0 4.4 %shard_map.344 = (bf16[640,128]{1,0:T(8,128)(2,1)S(1)}, f32[8,640]{1,0:T(8,128)S(1)}, f32[2,160,512]{2,1,0:T(8,128)S(1)}, bf16[2,160,512]{2,1,0:T(8,128)(2,1)S(1)}) custom-call(s32[18]{0:T(128)S(1)} %concatenate.17.refs_0_, bf16[640,128]{1,0:T(8,128)(2,1)S(1)} %get-tuple-element.110.refs_1_.refs_3_, ...), custom_call_target="tpu_custom_call" | custom-call | flops 250000000 | bytes 1000000 | tf_op jit(solution)/shard_map/pallas_call | solution.py:91
  61.6 2.6 %collective-permute-start.14 = (bf16[4,64,1024]{2,1,0:T(8,128)(2,1)S(1)}, bf16[4,64,1024]{2,1,0:T(8,128)(2,1)S(1)}, u32[]{:S(2)}, u32[]{:S(2)}) collective-permute-start(bf16[4,64,1024]{2,1,0:T(8,128)(2,1)S(1)} %pad_maximum_fusion.refs_1_), channel_id=1, source_target_pairs={{0,4},{4,0},{8,12},{12,8},{16,20},{20,16},{24,28},{28,24},{1,5},{5... | collective-permute-start | bytes 1572872 | tf_op jit(solution)/shard_map/ppermute | solution.py:571
  65.8 4.7 %collective-permute-start.16 = (bf16[64,512]{1,0:T(8,128)(2,1)S(1)}, bf16[64,512]{1,0:T(8,128)(2,1)S(1)}, u32[]{:S(2)}, u32[]{:S(2)}) collective-permute-start(bf16[64,512]{1,0:T(8,128)(2,1)S(1)} %copy-done.1), channel_id=1, source_target_pairs={{8,16},{12,20},{16,8},{20,12},{24,0},{28,4},{0,24},{4,28},{9,17},{... | collective-permute-start | bytes 196616 | tf_op jit(solution)/shard_map/ppermute | solution.py:712
  70.5 9.0 %collective-permute-done.17.refs_5_.refs_10_ = bf16[64,512]{1,0:T(8,128)(2,1)S(1)} collective-permute-done((bf16[64,512]{1,0:T(8,128)(2,1)S(1)}, bf16[64,512]{1,0:T(8,128)(2,1)S(1)}, u32[]{:S(2)}, u32[]{:S(2)}) %collective-permute-start.17) | collective-permute-done | bytes 65568 | tf_op jit(solution)/shard_map/ppermute | solution.py:712
  86.5 8.3 %collective-permute-done.20.refs_2_ = bf16[2,160,512]{2,1,0:T(8,128)(2,1)S(1)} collective-permute-done((bf16[2,160,512]{2,1,0:T(8,128)(2,1)S(1)}, bf16[2,160,512]{2,1,0:T(8,128)(2,1)S(1)}, u32[]{:S(2)}, u32[]{:S(2)}) %collective-permute-start.20) | collective-permute-done | bytes 327712 | tf_op jit(solution)/shard_map/ppermute | solution.py:535
  102.5 7.7 %collective-permute-done.23.refs_2_ = bf16[2,160,512]{2,1,0:T(8,128)(2,1)S(1)} collective-permute-done((bf16[2,160,512]{2,1,0:T(8,128)(2,1)S(1)}, bf16[2,160,512]{2,1,0:T(8,128)(2,1)S(1)}, u32[]{:S(2)}, u32[]{:S(2)}) %collective-permute-start.23) | collective-permute-done | bytes 327712 | tf_op jit(solution)/shard_map/ppermute | solution.py:535
  120.0 5.0 %collective-permute-start.37 = (bf16[64,256]{1,0:T(8,128)(2,1)S(1)}, bf16[64,256]{1,0:T(8,128)(2,1)S(1)}, u32[]{:S(2)}, u32[]{:S(2)}) collective-permute-start(bf16[64,256]{1,0:T(8,128)(2,1)S(1)} %get-tuple-element.175.refs_13_), channel_id=1, source_target_pairs={{16,8},{20,12},{8,16},{12,20},{0,24},{4,28},{24,0},{28,4},{17,9},{... | collective-permute-start | bytes 98312 | tf_op jit(solution)/shard_map/ppermute | solution.py:782
  125.0 3.4 %collective-permute-start.30 = (bf16[4,64,1536]{2,1,0:T(8,128)(2,1)S(1)}, bf16[4,64,1536]{2,1,0:T(8,128)(2,1)S(1)}, u32[]{:S(2)}, u32[]{:S(2)}) collective-permute-start(bf16[4,64,1536]{2,1,0:T(8,128)(2,1)S(1)} %get-tuple-element.151), channel_id=1, source_target_pairs={{0,4},{4,0},{8,12},{12,8},{16,20},{20,16},{24,28},{28,24},{1,5},{5... | collective-permute-start | bytes 2359304 | tf_op jit(solution)/shard_map/ppermute | solution.py:571
  128.4 3.3 %collective-permute-done.38.refs_4_ = bf16[64,256]{1,0:T(8,128)(2,1)S(1)} collective-permute-done((bf16[64,256]{1,0:T(8,128)(2,1)S(1)}, bf16[64,256]{1,0:T(8,128)(2,1)S(1)}, u32[]{:S(2)}, u32[]{:S(2)}) %collective-permute-start.38) | collective-permute-done | bytes 32800 | tf_op jit(solution)/shard_map/ppermute | solution.py:782
  135.4 5.9 %shard_map.355 = (bf16[640,512]{1,0:T(8,128)(2,1)S(1)}, bf16[2,1024,640]{2,1,0:T(8,128)(2,1)S(1)}, bf16[2,2,128,640]{3,2,1,0:T(8,128)(2,1)S(1)}, f32[640,256]{1,...) custom-call(s32[18]{0:T(128)S(1)} %concatenate.17.refs_0_, ...), custom_call_target="tpu_custom_call" | custom-call | flops 400000000 | bytes 1000000 | tf_op jit(solution)/shard_map/pallas_call | solution.py:91
  144.5 2.7 %shard_map.356 = (f32[512,128]{1,0:T(8,128)S(1)}, f32[512,128]{1,0:T(8,128)S(1)}, f32[640,512]{1,0:T(8,128)S(1)}) custom-call(s32[18]{0:T(128)S(1)} %concatenate.17.refs_0_, bf16[640,512]{1,0:T(8,128)(2,1)S(1)} %get-tuple-element.155.refs_1_.refs_2_, bf16[640,512]{1,0:T(8,128)(2,1)S(1)} %get-tuple-element.159.refs_2_, ...), custom_call_target="tpu_custom_call" | custom-call | flops 200000000 | bytes 1000000 | tf_op jit(solution)/shard_map/pallas_call | solution.py:91
  147.3 3.1 %collective-permute-start.33 = (bf16[640,256]{1,0:T(8,128)(2,1)S(1)}, bf16[640,256]{1,0:T(8,128)(2,1)S(1)}, u32[]{:S(2)}, u32[]{:S(2)}) collective-permute-start(bf16[640,256]{1,0:T(8,128)(2,1)S(1)} %get-tuple-element.168), channel_id=1, source_target_pairs={{12,8},{16,12},{20,16},{28,24},{0,28},{4,0},{13,9},{17,13},{21,17}... | collective-permute-start | bytes 983048 | tf_op jit(solution)/shard_map/ppermute | solution.py:813
  150.6 2.9 %collective-permute-start.44 = (bf16[2,64,1536]{2,1,0:T(8,128)(2,1)S(1)}, bf16[2,64,1536]{2,1,0:T(8,128)(2,1)S(1)}, u32[]{:S(2)}, u32[]{:S(2)}) collective-permute-start(bf16[2,64,1536]{2,1,0:T(8,128)(2,1)S(1)} %slice.75), channel_id=1, source_target_pairs={{0,8},{4,12},{8,0},{12,4},{16,24},{20,28},{24,16},{28,20},{1,9},{5... | collective-permute-start | bytes 1179656 | tf_op jit(solution)/shard_map/ppermute | solution.py:586
  154.9 4.8 %collective-permute-done.33.refs_6_ = bf16[640,256]{1,0:T(8,128)(2,1)S(1)} collective-permute-done((bf16[640,256]{1,0:T(8,128)(2,1)S(1)}, bf16[640,256]{1,0:T(8,128)(2,1)S(1)}, u32[]{:S(2)}, u32[]{:S(2)}) %collective-permute-start.33) | collective-permute-done | bytes 327712 | tf_op jit(solution)/shard_map/ppermute | solution.py:813
  161.5 5.2 %collective-permute-done.44 = bf16[2,64,1536]{2,1,0:T(8,128)(2,1)S(1)} collective-permute-done((bf16[2,64,1536]{2,1,0:T(8,128)(2,1)S(1)}, bf16[2,64,1536]{2,1,0:T(8,128)(2,1)S(1)}, u32[]{:S(2)}, u32[]{:S(2)}) %collective-permute-start.44) | collective-permute-done | bytes 393248 | tf_op jit(solution)/shard_map/ppermute | solution.py:586
  169.4 2.5 %collective-permute-start.42 = (bf16[2,64,512]{2,1,0:T(8,128)(2,1)S(1)}, bf16[2,64,512]{2,1,0:T(8,128)(2,1)S(1)}, u32[]{:S(2)}, u32[]{:S(2)}) collective-permute-start(bf16[2,64,512]{2,1,0:T(8,128)(2,1)S(1)} %slice.72), channel_id=1, source_target_pairs={{0,8},{4,12},{8,0},{12,4},{16,24},{20,28},{24,16},{28,20},{1,9},{5... | collective-permute-start | bytes 393224 | tf_op jit(solution)/shard_map/ppermute | solution.py:586
  174.3 2.6 %all-to-all-start.1 = ((f32[32,1,512]{2,1,0:T(1,128)}), f32[32,1,512]{2,1,0:T(1,128)S(1)}, u32[]{:S(2)}, u32[]{:S(2)}) async-start(f32[32,1,512]{2,1,0:T(1,128)} %reshape.44), calls=%async_computation.1 | async-start | bytes 131072 | tf_op jit(solution)/shard_map/all_to_all | solution.py:841
  179.4 2.6 %collective-permute-start.43 = (bf16[1,64,512]{2,1,0:T(8,128)(2,1)S(1)}, bf16[1,64,512]{2,1,0:T(8,128)(2,1)S(1)}, u32[]{:S(2)}, u32[]{:S(2)}) collective-permute-start(bf16[1,64,512]{2,1,0:T(8,128)(2,1)S(1)} %get-tuple-element.197), channel_id=1, source_target_pairs={{0,16},{4,20},{8,24},{12,28},{16,0},{20,4},{24,8},{28,12},{1,17},{... | collective-permute-start | bytes 196616 | tf_op jit(solution)/shard_map/ppermute | solution.py:586
  (149 shorter events, 68.7 us)
Async XLA Ops:
  3.5 26.2 %all-to-all-start = ((bf16[8,72,384]{2,1,0:T(8,128)(2,1)}), bf16[8,72,384]{2,1,0:T(8,128)(2,1)S(1)}, u32[]{:S(2)}, u32[]{:S(2)}) async-start(bf16[8,72,384]{2,1,0:T(8,128)(2,1)} %get-tuple-element.106), calls=%async_computation | async-start | bytes 884736 | tf_op jit(solution)/shard_map/all_to_all | solution.py:629
  11.0 20.5 %collective-permute-start.7 = (bf16[1,64,640]{2,1,0:T(8,128)(2,1)}, bf16[1,64,640]{2,1,0:T(8,128)(2,1)S(1)}, u32[]{:S(2)}, u32[]{:S(2)}) collective-permute-start(bf16[1,64,640]{2,1,0:T(8,128)(2,1)} %bitcast.54), channel_id=1, source_target_pairs={{0,16},{4,20},{8,24},{12,28},{16,0},{20,4},{24,8},{28,12},{1,17},{... | collective-permute-start | bytes 245768 | tf_op jit(solution)/shard_map/ppermute | solution.py:555
  13.9 22.1 %collective-permute-start.12 = (bf16[1,64,1024]{2,1,0:T(8,128)(2,1)}, bf16[1,64,1024]{2,1,0:T(8,128)(2,1)S(1)}, u32[]{:S(2)}, u32[]{:S(2)}) collective-permute-start(bf16[1,64,1024]{2,1,0:T(8,128)(2,1)} %bitcast.51), channel_id=1, source_target_pairs={{0,16},{4,20},{8,24},{12,28},{16,0},{20,4},{24,8},{28,12},{1,17},{... | collective-permute-start | bytes 393224 | tf_op jit(solution)/shard_map/ppermute | solution.py:555
  15.4 16.1 %collective-permute-start.2 = (bf16[160,512]{1,0:T(8,128)(2,1)}, bf16[160,512]{1,0:T(8,128)(2,1)S(1)}, u32[]{:S(2)}, u32[]{:S(2)}) collective-permute-start(bf16[160,512]{1,0:T(8,128)(2,1)} %param.23), channel_id=1, source_target_pairs={{0,2},{1,3},{2,0},{3,1},{4,6},{5,7},{6,4},{7,5},{8,10},{9,11},{10,... | collective-permute-start | bytes 491528 | tf_op jit(solution)/shard_map/ppermute | solution.py:535
  31.7 25.2 %collective-permute-start.6 = (bf16[640,256]{1,0:T(8,128)(2,1)S(1)}, bf16[640,256]{1,0:T(8,128)(2,1)S(1)}, u32[]{:S(2)}, u32[]{:S(2)}) collective-permute-start(bf16[640,256]{1,0:T(8,128)(2,1)S(1)} %get-tuple-element.111.refs_5_.refs_9_), channel_id=1, source_target_pairs={{8,12},{12,16},{16,20},{24,28},{28,0},{0,4},{9,13},{13,17},{17,21}... | collective-permute-start | bytes 983048 | tf_op jit(solution)/shard_map/ppermute | solution.py:698
  34.7 22.3 %collective-permute-start.5 = (bf16[640,256]{1,0:T(8,128)(2,1)S(1)}, bf16[640,256]{1,0:T(8,128)(2,1)S(1)}, u32[]{:S(2)}, u32[]{:S(2)}) collective-permute-start(bf16[640,256]{1,0:T(8,128)(2,1)S(1)} %get-tuple-element.111.refs_5_.refs_9_), channel_id=1, source_target_pairs={{8,16},{12,20},{24,0},{28,4},{9,17},{13,21},{25,1},{29,5},{10,18},... | collective-permute-start | bytes 983048 | tf_op jit(solution)/shard_map/ppermute | solution.py:698
  36.0 21.0 %collective-permute-start.4 = (bf16[640,256]{1,0:T(8,128)(2,1)S(1)}, bf16[640,256]{1,0:T(8,128)(2,1)S(1)}, u32[]{:S(2)}, u32[]{:S(2)}) collective-permute-start(bf16[640,256]{1,0:T(8,128)(2,1)S(1)} %get-tuple-element.111.refs_5_.refs_9_), channel_id=1, source_target_pairs={{8,20},{24,4},{9,21},{25,5},{10,22},{26,6},{11,23},{27,7}} | collective-permute-start | bytes 983048 | tf_op jit(solution)/shard_map/ppermute | solution.py:698
  36.9 19.4 %collective-permute-start.9 = (bf16[4,64,640]{2,1,0:T(8,128)(2,1)S(1)}, bf16[4,64,640]{2,1,0:T(8,128)(2,1)S(1)}, u32[]{:S(2)}, u32[]{:S(2)}) collective-permute-start(bf16[4,64,640]{2,1,0:T(8,128)(2,1)S(1)} %pad_maximum_fusion.3.refs_1_), channel_id=1, source_target_pairs={{0,4},{4,0},{8,12},{12,8},{16,20},{20,16},{24,28},{28,24},{1,5},{5... | collective-permute-start | bytes 983048 | tf_op jit(solution)/shard_map/ppermute | solution.py:571
  38.1 23.4 %collective-permute-start.13 = (bf16[2,64,1024]{2,1,0:T(8,128)(2,1)S(1)}, bf16[2,64,1024]{2,1,0:T(8,128)(2,1)S(1)}, u32[]{:S(2)}, u32[]{:S(2)}) collective-permute-start(bf16[2,64,1024]{2,1,0:T(8,128)(2,1)S(1)} %pad_maximum_fusion.4), channel_id=1, source_target_pairs={{0,8},{4,12},{8,0},{12,4},{16,24},{20,28},{24,16},{28,20},{1,9},{5... | collective-permute-start | bytes 786440 | tf_op jit(solution)/shard_map/ppermute | solution.py:555
  61.6 18.0 %collective-permute-start.14 = (bf16[4,64,1024]{2,1,0:T(8,128)(2,1)S(1)}, bf16[4,64,1024]{2,1,0:T(8,128)(2,1)S(1)}, u32[]{:S(2)}, u32[]{:S(2)}) collective-permute-start(bf16[4,64,1024]{2,1,0:T(8,128)(2,1)S(1)} %pad_maximum_fusion.refs_1_), channel_id=1, source_target_pairs={{0,4},{4,0},{8,12},{12,8},{16,20},{20,16},{24,28},{28,24},{1,5},{5... | collective-permute-start | bytes 1572872 | tf_op jit(solution)/shard_map/ppermute | solution.py:571
  64.2 15.3 %collective-permute-start.11 = (bf16[2,160,512]{2,1,0:T(8,128)(2,1)S(1)}, bf16[2,160,512]{2,1,0:T(8,128)(2,1)S(1)}, u32[]{:S(2)}, u32[]{:S(2)}) collective-permute-start(bf16[2,160,512]{2,1,0:T(8,128)(2,1)S(1)} %add_convert_fusion.5.refs_1_), channel_id=1, source_target_pairs={{0,2},{1,3},{2,0},{3,1},{4,6},{5,7},{6,4},{7,5},{8,10},{9,11},{10,... | collective-permute-start | bytes 983048 | tf_op jit(solution)/shard_map/ppermute | solution.py:535
  65.8 13.7 %collective-permute-start.17 = (bf16[64,512]{1,0:T(8,128)(2,1)S(1)}, bf16[64,512]{1,0:T(8,128)(2,1)S(1)}, u32[]{:S(2)}, u32[]{:S(2)}) collective-permute-start(bf16[64,512]{1,0:T(8,128)(2,1)S(1)} %copy-done.1), channel_id=1, source_target_pairs={{8,20},{12,8},{16,12},{20,16},{24,4},{28,24},{0,28},{4,0},{9,21},{... | collective-permute-start | bytes 196616 | tf_op jit(solution)/shard_map/ppermute | solution.py:712
  65.8 13.7 %collective-permute-start.16 = (bf16[64,512]{1,0:T(8,128)(2,1)S(1)}, bf16[64,512]{1,0:T(8,128)(2,1)S(1)}, u32[]{:S(2)}, u32[]{:S(2)}) collective-permute-start(bf16[64,512]{1,0:T(8,128)(2,1)S(1)} %copy-done.1), channel_id=1, source_target_pairs={{8,16},{12,20},{16,8},{20,12},{24,0},{28,4},{0,24},{4,28},{9,17},{... | collective-permute-start | bytes 196616 | tf_op jit(solution)/shard_map/ppermute | solution.py:712
  116.2 15.8 %collective-permute-start.26 = (bf16[2,160,512]{2,1,0:T(8,128)(2,1)S(1)}, bf16[2,160,512]{2,1,0:T(8,128)(2,1)S(1)}, u32[]{:S(2)}, u32[]{:S(2)}) collective-permute-start(bf16[2,160,512]{2,1,0:T(8,128)(2,1)S(1)} %get-tuple-element.142), channel_id=1, source_target_pairs={{0,1},{1,0},{2,3},{3,2},{4,5},{5,4},{6,7},{7,6},{8,9},{9,8},{10,11... | collective-permute-start | bytes 983048 | tf_op jit(solution)/shard_map/ppermute | solution.py:531
  116.4 15.7 %collective-permute-start.27 = (bf16[2,160,512]{2,1,0:T(8,128)(2,1)S(1)}, bf16[2,160,512]{2,1,0:T(8,128)(2,1)S(1)}, u32[]{:S(2)}, u32[]{:S(2)}) collective-permute-start(bf16[2,160,512]{2,1,0:T(8,128)(2,1)S(1)} %add_convert_fusion.2.refs_1_), channel_id=1, source_target_pairs={{0,2},{1,3},{2,0},{3,1},{4,6},{5,7},{6,4},{7,5},{8,10},{9,11},{10,... | collective-permute-start | bytes 983048 | tf_op jit(solution)/shard_map/ppermute | solution.py:535
  125.0 22.2 %collective-permute-start.30 = (bf16[4,64,1536]{2,1,0:T(8,128)(2,1)S(1)}, bf16[4,64,1536]{2,1,0:T(8,128)(2,1)S(1)}, u32[]{:S(2)}, u32[]{:S(2)}) collective-permute-start(bf16[4,64,1536]{2,1,0:T(8,128)(2,1)S(1)} %get-tuple-element.151), channel_id=1, source_target_pairs={{0,4},{4,0},{8,12},{12,8},{16,20},{20,16},{24,28},{28,24},{1,5},{5... | collective-permute-start | bytes 2359304 | tf_op jit(solution)/shard_map/ppermute | solution.py:571
  133.3 17.3 %collective-permute-start.40 = (bf16[64,512]{1,0:T(8,128)(2,1)S(1)}, bf16[64,512]{1,0:T(8,128)(2,1)S(1)}, u32[]{:S(2)}, u32[]{:S(2)}) collective-permute-start(bf16[64,512]{1,0:T(8,128)(2,1)S(1)} %add_convert_fusion.8), channel_id=1, source_target_pairs={{0,2},{1,3},{2,0},{3,1},{4,6},{5,7},{6,4},{7,5},{8,10},{9,11},{10,... | collective-permute-start | bytes 196616 | tf_op jit(solution)/shard_map/ppermute | solution.py:535
  133.9 20.3 %collective-permute-start.28 = (bf16[160,512]{1,0:T(8,128)(2,1)S(1)}, bf16[160,512]{1,0:T(8,128)(2,1)S(1)}, u32[]{:S(2)}, u32[]{:S(2)}) collective-permute-start(bf16[160,512]{1,0:T(8,128)(2,1)S(1)} %fusion.3), channel_id=1, source_target_pairs={{0,2},{1,3},{2,0},{3,1},{4,6},{5,7},{6,4},{7,5},{8,10},{9,11},{10,... | collective-permute-start | bytes 491528 | tf_op jit(solution)/shard_map/ppermute | solution.py:535
  141.3 13.6 %collective-permute-start.31 = (bf16[640,256]{1,0:T(8,128)(2,1)S(1)}, bf16[640,256]{1,0:T(8,128)(2,1)S(1)}, u32[]{:S(2)}, u32[]{:S(2)}) collective-permute-start(bf16[640,256]{1,0:T(8,128)(2,1)S(1)} %get-tuple-element.166), channel_id=1, source_target_pairs={{20,8},{4,24},{21,9},{5,25},{22,10},{6,26},{23,11},{7,27}} | collective-permute-start | bytes 983048 | tf_op jit(solution)/shard_map/ppermute | solution.py:813
  142.0 12.9 %collective-permute-start.32 = (bf16[640,256]{1,0:T(8,128)(2,1)S(1)}, bf16[640,256]{1,0:T(8,128)(2,1)S(1)}, u32[]{:S(2)}, u32[]{:S(2)}) collective-permute-start(bf16[640,256]{1,0:T(8,128)(2,1)S(1)} %get-tuple-element.167), channel_id=1, source_target_pairs={{16,8},{20,12},{0,24},{4,28},{17,9},{21,13},{1,25},{5,29},{18,10},... | collective-permute-start | bytes 983048 | tf_op jit(solution)/shard_map/ppermute | solution.py:813
  147.3 12.4 %collective-permute-start.33 = (bf16[640,256]{1,0:T(8,128)(2,1)S(1)}, bf16[640,256]{1,0:T(8,128)(2,1)S(1)}, u32[]{:S(2)}, u32[]{:S(2)}) collective-permute-start(bf16[640,256]{1,0:T(8,128)(2,1)S(1)} %get-tuple-element.168), channel_id=1, source_target_pairs={{12,8},{16,12},{20,16},{28,24},{0,28},{4,0},{13,9},{17,13},{21,17}... | collective-permute-start | bytes 983048 | tf_op jit(solution)/shard_map/ppermute | solution.py:813
  150.6 16.1 %collective-permute-start.44 = (bf16[2,64,1536]{2,1,0:T(8,128)(2,1)S(1)}, bf16[2,64,1536]{2,1,0:T(8,128)(2,1)S(1)}, u32[]{:S(2)}, u32[]{:S(2)}) collective-permute-start(bf16[2,64,1536]{2,1,0:T(8,128)(2,1)S(1)} %slice.75), channel_id=1, source_target_pairs={{0,8},{4,12},{8,0},{12,4},{16,24},{20,28},{24,16},{28,20},{1,9},{5... | collective-permute-start | bytes 1179656 | tf_op jit(solution)/shard_map/ppermute | solution.py:586
  166.8 11.8 %collective-permute-start.45 = (bf16[1,64,1536]{2,1,0:T(8,128)(2,1)S(1)}, bf16[1,64,1536]{2,1,0:T(8,128)(2,1)S(1)}, u32[]{:S(2)}, u32[]{:S(2)}) collective-permute-start(bf16[1,64,1536]{2,1,0:T(8,128)(2,1)S(1)} %get-tuple-element.195), channel_id=1, source_target_pairs={{0,16},{4,20},{8,24},{12,28},{16,0},{20,4},{24,8},{28,12},{1,17},{... | collective-permute-start | bytes 589832 | tf_op jit(solution)/shard_map/ppermute | solution.py:586
  176.9 11.2 %collective-permute-start.35 = (bf16[160,512]{1,0:T(8,128)(2,1)S(1)}, bf16[160,512]{1,0:T(8,128)(2,1)S(1)}, u32[]{:S(2)}, u32[]{:S(2)}) collective-permute-start(bf16[160,512]{1,0:T(8,128)(2,1)S(1)} %fusion.4), channel_id=1, source_target_pairs={{0,2},{1,3},{2,0},{3,1},{4,6},{5,7},{6,4},{7,5},{8,10},{9,11},{10,... | collective-permute-start | bytes 491528 | tf_op jit(solution)/shard_map/ppermute | solution.py:535
  (33 other events, 296.9 us)

commit v5 on v4

--- a/solution.py
+++ b/solution.py
@@ -94,18 +94,22 @@
         in_specs=[pl.BlockSpec(memory_space=space) for space in spaces],
         out_specs=[pl.BlockSpec(memory_space=pltpu.VMEM) for _ in outs],
         scratch_shapes=scratch,
-        cost_estimate=pl.CostEstimate(flops=us * 50 * 10**6, bytes_accessed=10**6, transcendentals=0),
+        cost_estimate=pl.CostEstimate(flops=us * 100 * 10**6, bytes_accessed=10**6, transcendentals=0),
         compiler_params=pltpu.CompilerParams(vmem_limit_bytes=limit * 1024 * 1024),
     )(*arrays)
 
 
-def pack_body(trees, n_first, steps, table, n_self, n_cross, n_ffn, *refs):
-    weights, later, out, outs = refs[:n_first], refs[n_first:-3], refs[-3], refs[-2:]
-    for group, one in ((later[:5], outs[0]), (later[5:], outs[1])):
+def side_body(n_first, *refs):
+    ins, outs = refs[:-2], refs[-2:]
+    for group, one in ((ins[:n_first], outs[0]), (ins[n_first:], outs[1])):
         at = 0
         for piece in group:
             one[:, at : at + piece.shape[1]] = piece[...]
             at += piece.shape[1]
+
+
+def pack_body(trees, steps, table, n_self, n_cross, n_ffn, *refs):
+    weights, out = refs[:-1], refs[-1]
     lines = lax.broadcasted_iota(i32, table.shape, 0)
     full = table[...].astype(f32)
     small = [n_self[...].astype(f32), n_cross[...].astype(f32), n_ffn[...].astype(f32)]
@@ -616,13 +620,17 @@
     shard = norm_self.shape[0]
     cols = w_query.shape[1]
     hidden_cols = w_hidden.shape[1]
-    packed, cross_pack, ffn_pack = run(
-        lambda *refs: pack_body(trees, 3, *refs),
-        [shaped((count, shard + 8, 3 * cols), bf16), shaped((shard, 5 * cols), bf16), shaped((shard, 2 * hidden_cols), bf16)],
-        [
-            timesteps, time_table, norm_self[None], norm_cross[None], norm_ffn[None],
-            w_query, w_key, w_value, c_query, c_key, c_value, c_out.T, w_out.T, w_hidden, w_back.T,
-        ],
+    (packed,) = run(
+        lambda *refs: pack_body(trees, *refs),
+        [shaped((count, shard + 8, 3 * cols), bf16)],
+        [timesteps, time_table, norm_self[None], norm_cross[None], norm_ffn[None], w_query, w_key, w_value],
+        load=True,
+        limit=60,
+    )
+    cross_pack, ffn_pack = run(
+        lambda *refs: side_body(5, *refs),
+        [shaped((shard, 5 * cols), bf16), shaped((shard, 2 * hidden_cols), bf16)],
+        [tie(c_query, packed), c_key, c_value, c_out.T, w_out.T, w_hidden, w_back.T],
         load=True,
         limit=60,
     )
@@ -632,7 +640,6 @@
     grad_half = jnp.stack([grad_out, across(tie(grad_out, packed))])
     grad_other = sibling(grad_half)
     cross_chain = Doubling(cross_pack)
-    ffn_chain = Doubling(ffn_pack)
 
     def turn(distance):
         return [
@@ -684,6 +691,7 @@
         [scalars, tokens_half, tokens_other, first],
     )
     cross_chain.step(kv)
+    ffn_chain = Doubling(tie(ffn_pack, kv))
     cross_near = cross_chain.end()
     rest_w = assemble(cross_near, neighbour(cross_near))
     w_o = part(rest_w, cols, 4)

time: 190 us -> 188 us (0.989)
  other arithmetic: 6.98 us -> 4.08 us
  waiting for transfers between devices: 75.4 us -> 72.8 us
  starting transfers between devices: 67.5 us -> 69.5 us
    ppermute x9, waiting for transfers between devices: 18.5 us -> 16 us  [across(): return lax.ppermute(x, 'tensor', xor_route('tensor', 2))]
    pallas_call x23 -> x24, Pallas kernels: 35.2 us -> 36.7 us  [run(): pl.pallas_call(wrapped, out_shape=outs, in_specs=[pl.BlockSpec(memory_spa...]
  transfers between devices with their start and end apart: 48 -> 48, of which waited for: 19 -> 18; matrix products, arithmetic and copies ran while one was open for 5% -> 4% of each run, Pallas kernels for 13% -> 14%
where the time goes in v5:
time: 188 us; the launch traced here: 187 us
  waiting for transfers between devices  72.8 us (39%)
  starting transfers between devices  69.5 us (37%)
  Pallas kernels  36.7 us (20%)
  other arithmetic  4.08 us (2%)
  local copies, waits for them, and re-layouts  2.81 us (1%)
    pallas_call x24, Pallas kernels, run(): pl.pallas_call(wrapped, out_shape=outs, in_specs=[pl.BlockSpec(memory_spa...  36.7 us
    ppermute x9, waiting for transfers between devices, across(): return lax.ppermute(x, 'tensor', xor_route('tensor', 2))  16 us
    ppermute x4, waiting for transfers between devices, neighbour(): return lax.ppermute(x, 'dp', xor_route('dp', 1))  15.7 us
    ppermute x9, starting transfers between devices, across(): return lax.ppermute(x, 'tensor', xor_route('tensor', 2))  12.1 us
    ppermute x4, starting transfers between devices, step(): lax.ppermute(total[middle:], 'dp', xor_route('dp', self.bit))  10.9 us
    ppermute x13, waiting for transfers between devices, sibling(): return lax.ppermute(x, 'tensor', xor_route('tensor', 1))  9.6 us
    ppermute x3, waiting for transfers between devices, on_device(): lax.ppermute(enc_sent, 'dp', turn(d))  8.99 us
    ppermute x4, starting transfers between devices, neighbour(): return lax.ppermute(x, 'dp', xor_route('dp', 1))  8.1 us
  transfers between devices with their start and end apart: 48, of which 18 were waited for; matrix products, arithmetic and copies ran while one was open for 4% of the time, Pallas kernels for 14%

profile of v5, /device:TPU:0, one launch (start us, length us, event | category | flops | bytes accessed | tf_op | source)
XLA Modules:
  0.0 187.1 jit_solution(5346265697917394111)
XLA Ops:
  3.3 7.3 %all-to-all-start = ((bf16[8,72,384]{2,1,0:T(8,128)(2,1)}), bf16[8,72,384]{2,1,0:T(8,128)(2,1)S(1)}, u32[]{:S(2)}, u32[]{:S(2)}) async-start(bf16[8,72,384]{2,1,0:T(8,128)(2,1)} %shard_map.341), calls=%async_computation | async-start | bytes 884736 | tf_op jit(solution)/shard_map/all_to_all | solution.py:637
  14.4 2.9 %collective-permute-start.7 = (bf16[1,64,640]{2,1,0:T(8,128)(2,1)}, bf16[1,64,640]{2,1,0:T(8,128)(2,1)S(1)}, u32[]{:S(2)}, u32[]{:S(2)}) collective-permute-start(bf16[1,64,640]{2,1,0:T(8,128)(2,1)} %bitcast.54), channel_id=1, source_target_pairs={{0,16},{4,20},{8,24},{12,28},{16,0},{20,4},{24,8},{28,12},{1,17},{... | collective-permute-start | bytes 245768 | tf_op jit(solution)/shard_map/ppermute | solution.py:559
  19.7 6.2 %all-to-all-done.refs_3_ = bf16[8,72,384]{2,1,0:T(8,128)(2,1)S(1)} async-done(((bf16[8,72,384]{2,1,0:T(8,128)(2,1)}), bf16[8,72,384]{2,1,0:T(8,128)(2,1)S(1)}, u32[]{:S(2)}, u32[]{:S(2)}) %all-to-all-start) | async-done | bytes 442400 | tf_op jit(solution)/shard_map/all_to_all | solution.py:637
  29.5 3.1 %collective-permute-start.6 = (bf16[640,256]{1,0:T(8,128)(2,1)S(1)}, bf16[640,256]{1,0:T(8,128)(2,1)S(1)}, u32[]{:S(2)}, u32[]{:S(2)}) collective-permute-start(bf16[640,256]{1,0:T(8,128)(2,1)S(1)} %get-tuple-element.111.refs_5_.refs_9_), channel_id=1, source_target_pairs={{8,12},{12,16},{16,20},{24,28},{28,0},{0,4},{9,13},{13,17},{17,21}... | collective-permute-start | bytes 983048 | tf_op jit(solution)/shard_map/ppermute | solution.py:706
  38.6 15.7 %collective-permute-done.9.refs_2_ = bf16[4,64,640]{2,1,0:T(8,128)(2,1)S(1)} collective-permute-done((bf16[4,64,640]{2,1,0:T(8,128)(2,1)S(1)}, bf16[4,64,640]{2,1,0:T(8,128)(2,1)S(1)}, u32[]{:S(2)}, u32[]{:S(2)}) %collective-permute-start.9) | collective-permute-done | bytes 327712 | tf_op jit(solution)/shard_map/ppermute | solution.py:575
  54.9 4.5 %shard_map.345 = (bf16[640,128]{1,0:T(8,128)(2,1)S(1)}, f32[8,640]{1,0:T(8,128)S(1)}, f32[2,160,512]{2,1,0:T(8,128)S(1)}, bf16[2,160,512]{2,1,0:T(8,128)(2,1)S(1)}) custom-call(s32[18]{0:T(128)S(1)} %concatenate.17.refs_0_, bf16[640,128]{1,0:T(8,128)(2,1)S(1)} %get-tuple-element.110.refs_1_.refs_3_, ...), custom_call_target="tpu_custom_call" | custom-call | flops 500000000 | bytes 1000000 | tf_op jit(solution)/shard_map/pallas_call | solution.py:91
  59.5 2.6 %collective-permute-start.14 = (bf16[4,64,1024]{2,1,0:T(8,128)(2,1)S(1)}, bf16[4,64,1024]{2,1,0:T(8,128)(2,1)S(1)}, u32[]{:S(2)}, u32[]{:S(2)}) collective-permute-start(bf16[4,64,1024]{2,1,0:T(8,128)(2,1)S(1)} %pad_maximum_fusion.refs_1_), channel_id=1, source_target_pairs={{0,4},{4,0},{8,12},{12,8},{16,20},{20,16},{24,28},{28,24},{1,5},{5... | collective-permute-start | bytes 1572872 | tf_op jit(solution)/shard_map/ppermute | solution.py:575
  63.7 4.7 %collective-permute-start.16 = (bf16[64,512]{1,0:T(8,128)(2,1)S(1)}, bf16[64,512]{1,0:T(8,128)(2,1)S(1)}, u32[]{:S(2)}, u32[]{:S(2)}) collective-permute-start(bf16[64,512]{1,0:T(8,128)(2,1)S(1)} %copy-done.1), channel_id=1, source_target_pairs={{8,16},{12,20},{16,8},{20,12},{24,0},{28,4},{0,24},{4,28},{9,17},{... | collective-permute-start | bytes 196616 | tf_op jit(solution)/shard_map/ppermute | solution.py:720
  68.5 9.0 %collective-permute-done.17.refs_5_.refs_10_ = bf16[64,512]{1,0:T(8,128)(2,1)S(1)} collective-permute-done((bf16[64,512]{1,0:T(8,128)(2,1)S(1)}, bf16[64,512]{1,0:T(8,128)(2,1)S(1)}, u32[]{:S(2)}, u32[]{:S(2)}) %collective-permute-start.17) | collective-permute-done | bytes 65568 | tf_op jit(solution)/shard_map/ppermute | solution.py:720
  84.5 8.3 %collective-permute-done.20.refs_2_ = bf16[2,160,512]{2,1,0:T(8,128)(2,1)S(1)} collective-permute-done((bf16[2,160,512]{2,1,0:T(8,128)(2,1)S(1)}, bf16[2,160,512]{2,1,0:T(8,128)(2,1)S(1)}, u32[]{:S(2)}, u32[]{:S(2)}) %collective-permute-start.20) | collective-permute-done | bytes 327712 | tf_op jit(solution)/shard_map/ppermute | solution.py:539
  100.4 7.7 %collective-permute-done.23.refs_2_ = bf16[2,160,512]{2,1,0:T(8,128)(2,1)S(1)} collective-permute-done((bf16[2,160,512]{2,1,0:T(8,128)(2,1)S(1)}, bf16[2,160,512]{2,1,0:T(8,128)(2,1)S(1)}, u32[]{:S(2)}, u32[]{:S(2)}) %collective-permute-start.23) | collective-permute-done | bytes 327712 | tf_op jit(solution)/shard_map/ppermute | solution.py:539
  117.9 5.0 %collective-permute-start.37 = (bf16[64,256]{1,0:T(8,128)(2,1)S(1)}, bf16[64,256]{1,0:T(8,128)(2,1)S(1)}, u32[]{:S(2)}, u32[]{:S(2)}) collective-permute-start(bf16[64,256]{1,0:T(8,128)(2,1)S(1)} %get-tuple-element.177.refs_13_), channel_id=1, source_target_pairs={{16,8},{20,12},{8,16},{12,20},{0,24},{4,28},{24,0},{28,4},{17,9},{... | collective-permute-start | bytes 98312 | tf_op jit(solution)/shard_map/ppermute | solution.py:790
  122.9 3.4 %collective-permute-start.30 = (bf16[4,64,1536]{2,1,0:T(8,128)(2,1)S(1)}, bf16[4,64,1536]{2,1,0:T(8,128)(2,1)S(1)}, u32[]{:S(2)}, u32[]{:S(2)}) collective-permute-start(bf16[4,64,1536]{2,1,0:T(8,128)(2,1)S(1)} %get-tuple-element.153), channel_id=1, source_target_pairs={{0,4},{4,0},{8,12},{12,8},{16,20},{20,16},{24,28},{28,24},{1,5},{5... | collective-permute-start | bytes 2359304 | tf_op jit(solution)/shard_map/ppermute | solution.py:575
  126.3 3.3 %collective-permute-done.38.refs_4_ = bf16[64,256]{1,0:T(8,128)(2,1)S(1)} collective-permute-done((bf16[64,256]{1,0:T(8,128)(2,1)S(1)}, bf16[64,256]{1,0:T(8,128)(2,1)S(1)}, u32[]{:S(2)}, u32[]{:S(2)}) %collective-permute-start.38) | collective-permute-done | bytes 32800 | tf_op jit(solution)/shard_map/ppermute | solution.py:790
  133.3 5.9 %shard_map.356 = (bf16[640,512]{1,0:T(8,128)(2,1)S(1)}, bf16[2,1024,640]{2,1,0:T(8,128)(2,1)S(1)}, bf16[2,2,128,640]{3,2,1,0:T(8,128)(2,1)S(1)}, f32[640,256]{1,...) custom-call(s32[18]{0:T(128)S(1)} %concatenate.17.refs_0_, ...), custom_call_target="tpu_custom_call" | custom-call | flops 800000000 | bytes 1000000 | tf_op jit(solution)/shard_map/pallas_call | solution.py:91
  140.0 2.5 %collective-permute-start.32 = (bf16[640,256]{1,0:T(8,128)(2,1)S(1)}, bf16[640,256]{1,0:T(8,128)(2,1)S(1)}, u32[]{:S(2)}, u32[]{:S(2)}) collective-permute-start(bf16[640,256]{1,0:T(8,128)(2,1)S(1)} %get-tuple-element.169), channel_id=1, source_target_pairs={{16,8},{20,12},{0,24},{4,28},{17,9},{21,13},{1,25},{5,29},{18,10},... | collective-permute-start | bytes 983048 | tf_op jit(solution)/shard_map/ppermute | solution.py:821
  142.5 2.7 %shard_map.357 = (f32[512,128]{1,0:T(8,128)S(1)}, f32[512,128]{1,0:T(8,128)S(1)}, f32[640,512]{1,0:T(8,128)S(1)}) custom-call(s32[18]{0:T(128)S(1)} %concatenate.17.refs_0_, bf16[640,512]{1,0:T(8,128)(2,1)S(1)} %get-tuple-element.157.refs_1_.refs_2_, bf16[640,512]{1,0:T(8,128)(2,1)S(1)} %get-tuple-element.161.refs_2_, ...), custom_call_target="tpu_custom_call" | custom-call | flops 400000000 | bytes 1000000 | tf_op jit(solution)/shard_map/pallas_call | solution.py:91
  145.2 3.0 %collective-permute-start.33 = (bf16[640,256]{1,0:T(8,128)(2,1)S(1)}, bf16[640,256]{1,0:T(8,128)(2,1)S(1)}, u32[]{:S(2)}, u32[]{:S(2)}) collective-permute-start(bf16[640,256]{1,0:T(8,128)(2,1)S(1)} %get-tuple-element.170), channel_id=1, source_target_pairs={{12,8},{16,12},{20,16},{28,24},{0,28},{4,0},{13,9},{17,13},{21,17}... | collective-permute-start | bytes 983048 | tf_op jit(solution)/shard_map/ppermute | solution.py:821
  148.4 3.4 %collective-permute-start.44 = (bf16[2,64,1536]{2,1,0:T(8,128)(2,1)S(1)}, bf16[2,64,1536]{2,1,0:T(8,128)(2,1)S(1)}, u32[]{:S(2)}, u32[]{:S(2)}) collective-permute-start(bf16[2,64,1536]{2,1,0:T(8,128)(2,1)S(1)} %slice.75), channel_id=1, source_target_pairs={{0,8},{4,12},{8,0},{12,4},{16,24},{20,28},{24,16},{28,20},{1,9},{5... | collective-permute-start | bytes 1179656 | tf_op jit(solution)/shard_map/ppermute | solution.py:590
  153.2 4.4 %collective-permute-done.33.refs_6_ = bf16[640,256]{1,0:T(8,128)(2,1)S(1)} collective-permute-done((bf16[640,256]{1,0:T(8,128)(2,1)S(1)}, bf16[640,256]{1,0:T(8,128)(2,1)S(1)}, u32[]{:S(2)}, u32[]{:S(2)}) %collective-permute-start.33) | collective-permute-done | bytes 327712 | tf_op jit(solution)/shard_map/ppermute | solution.py:821
  159.4 5.2 %collective-permute-done.44 = bf16[2,64,1536]{2,1,0:T(8,128)(2,1)S(1)} collective-permute-done((bf16[2,64,1536]{2,1,0:T(8,128)(2,1)S(1)}, bf16[2,64,1536]{2,1,0:T(8,128)(2,1)S(1)}, u32[]{:S(2)}, u32[]{:S(2)}) %collective-permute-start.44) | collective-permute-done | bytes 393248 | tf_op jit(solution)/shard_map/ppermute | solution.py:590
  167.3 2.6 %collective-permute-start.42 = (bf16[2,64,512]{2,1,0:T(8,128)(2,1)S(1)}, bf16[2,64,512]{2,1,0:T(8,128)(2,1)S(1)}, u32[]{:S(2)}, u32[]{:S(2)}) collective-permute-start(bf16[2,64,512]{2,1,0:T(8,128)(2,1)S(1)} %slice.72), channel_id=1, source_target_pairs={{0,8},{4,12},{8,0},{12,4},{16,24},{20,28},{24,16},{28,20},{1,9},{5... | collective-permute-start | bytes 393224 | tf_op jit(solution)/shard_map/ppermute | solution.py:590
  172.3 2.6 %all-to-all-start.1 = ((f32[32,1,512]{2,1,0:T(1,128)}), f32[32,1,512]{2,1,0:T(1,128)S(1)}, u32[]{:S(2)}, u32[]{:S(2)}) async-start(f32[32,1,512]{2,1,0:T(1,128)} %reshape.44), calls=%async_computation.1 | async-start | bytes 131072 | tf_op jit(solution)/shard_map/all_to_all | solution.py:849
  177.4 2.6 %collective-permute-start.43 = (bf16[1,64,512]{2,1,0:T(8,128)(2,1)S(1)}, bf16[1,64,512]{2,1,0:T(8,128)(2,1)S(1)}, u32[]{:S(2)}, u32[]{:S(2)}) collective-permute-start(bf16[1,64,512]{2,1,0:T(8,128)(2,1)S(1)} %get-tuple-element.199), channel_id=1, source_target_pairs={{0,16},{4,20},{8,24},{12,28},{16,0},{20,4},{24,8},{28,12},{1,17},{... | collective-permute-start | bytes 196616 | tf_op jit(solution)/shard_map/ppermute | solution.py:590
  (152 shorter events, 67.3 us)
Async XLA Ops:
  3.3 22.7 %all-to-all-start = ((bf16[8,72,384]{2,1,0:T(8,128)(2,1)}), bf16[8,72,384]{2,1,0:T(8,128)(2,1)S(1)}, u32[]{:S(2)}, u32[]{:S(2)}) async-start(bf16[8,72,384]{2,1,0:T(8,128)(2,1)} %shard_map.341), calls=%async_computation | async-start | bytes 884736 | tf_op jit(solution)/shard_map/all_to_all | solution.py:637
  12.1 17.2 %collective-permute-start.2 = (bf16[160,512]{1,0:T(8,128)(2,1)S(1)}, bf16[160,512]{1,0:T(8,128)(2,1)S(1)}, u32[]{:S(2)}, u32[]{:S(2)}) collective-permute-start(bf16[160,512]{1,0:T(8,128)(2,1)S(1)} %copy-done.5), channel_id=1, source_target_pairs={{0,2},{1,3},{2,0},{3,1},{4,6},{5,7},{6,4},{7,5},{8,10},{9,11},{10,... | collective-permute-start | bytes 491528 | tf_op jit(solution)/shard_map/ppermute | solution.py:539
  14.4 13.2 %collective-permute-start.7 = (bf16[1,64,640]{2,1,0:T(8,128)(2,1)}, bf16[1,64,640]{2,1,0:T(8,128)(2,1)S(1)}, u32[]{:S(2)}, u32[]{:S(2)}) collective-permute-start(bf16[1,64,640]{2,1,0:T(8,128)(2,1)} %bitcast.54), channel_id=1, source_target_pairs={{0,16},{4,20},{8,24},{12,28},{16,0},{20,4},{24,8},{28,12},{1,17},{... | collective-permute-start | bytes 245768 | tf_op jit(solution)/shard_map/ppermute | solution.py:559
  29.5 25.4 %collective-permute-start.6 = (bf16[640,256]{1,0:T(8,128)(2,1)S(1)}, bf16[640,256]{1,0:T(8,128)(2,1)S(1)}, u32[]{:S(2)}, u32[]{:S(2)}) collective-permute-start(bf16[640,256]{1,0:T(8,128)(2,1)S(1)} %get-tuple-element.111.refs_5_.refs_9_), channel_id=1, source_target_pairs={{8,12},{12,16},{16,20},{24,28},{28,0},{0,4},{9,13},{13,17},{17,21}... | collective-permute-start | bytes 983048 | tf_op jit(solution)/shard_map/ppermute | solution.py:706
  32.6 22.3 %collective-permute-start.5 = (bf16[640,256]{1,0:T(8,128)(2,1)S(1)}, bf16[640,256]{1,0:T(8,128)(2,1)S(1)}, u32[]{:S(2)}, u32[]{:S(2)}) collective-permute-start(bf16[640,256]{1,0:T(8,128)(2,1)S(1)} %get-tuple-element.111.refs_5_.refs_9_), channel_id=1, source_target_pairs={{8,16},{12,20},{24,0},{28,4},{9,17},{13,21},{25,1},{29,5},{10,18},... | collective-permute-start | bytes 983048 | tf_op jit(solution)/shard_map/ppermute | solution.py:706
  34.9 20.0 %collective-permute-start.4 = (bf16[640,256]{1,0:T(8,128)(2,1)S(1)}, bf16[640,256]{1,0:T(8,128)(2,1)S(1)}, u32[]{:S(2)}, u32[]{:S(2)}) collective-permute-start(bf16[640,256]{1,0:T(8,128)(2,1)S(1)} %get-tuple-element.111.refs_5_.refs_9_), channel_id=1, source_target_pairs={{8,20},{24,4},{9,21},{25,5},{10,22},{26,6},{11,23},{27,7}} | collective-permute-start | bytes 983048 | tf_op jit(solution)/shard_map/ppermute | solution.py:706
  35.6 18.6 %collective-permute-start.9 = (bf16[4,64,640]{2,1,0:T(8,128)(2,1)S(1)}, bf16[4,64,640]{2,1,0:T(8,128)(2,1)S(1)}, u32[]{:S(2)}, u32[]{:S(2)}) collective-permute-start(bf16[4,64,640]{2,1,0:T(8,128)(2,1)S(1)} %pad_maximum_fusion.3.refs_1_), channel_id=1, source_target_pairs={{0,4},{4,0},{8,12},{12,8},{16,20},{20,16},{24,28},{28,24},{1,5},{5... | collective-permute-start | bytes 983048 | tf_op jit(solution)/shard_map/ppermute | solution.py:575
  37.6 21.8 %collective-permute-start.13 = (bf16[2,64,1024]{2,1,0:T(8,128)(2,1)S(1)}, bf16[2,64,1024]{2,1,0:T(8,128)(2,1)S(1)}, u32[]{:S(2)}, u32[]{:S(2)}) collective-permute-start(bf16[2,64,1024]{2,1,0:T(8,128)(2,1)S(1)} %pad_maximum_fusion.4), channel_id=1, source_target_pairs={{0,8},{4,12},{8,0},{12,4},{16,24},{20,28},{24,16},{28,20},{1,9},{5... | collective-permute-start | bytes 786440 | tf_op jit(solution)/shard_map/ppermute | solution.py:559
  59.5 17.9 %collective-permute-start.14 = (bf16[4,64,1024]{2,1,0:T(8,128)(2,1)S(1)}, bf16[4,64,1024]{2,1,0:T(8,128)(2,1)S(1)}, u32[]{:S(2)}, u32[]{:S(2)}) collective-permute-start(bf16[4,64,1024]{2,1,0:T(8,128)(2,1)S(1)} %pad_maximum_fusion.refs_1_), channel_id=1, source_target_pairs={{0,4},{4,0},{8,12},{12,8},{16,20},{20,16},{24,28},{28,24},{1,5},{5... | collective-permute-start | bytes 1572872 | tf_op jit(solution)/shard_map/ppermute | solution.py:575
  62.2 15.3 %collective-permute-start.11 = (bf16[2,160,512]{2,1,0:T(8,128)(2,1)S(1)}, bf16[2,160,512]{2,1,0:T(8,128)(2,1)S(1)}, u32[]{:S(2)}, u32[]{:S(2)}) collective-permute-start(bf16[2,160,512]{2,1,0:T(8,128)(2,1)S(1)} %add_convert_fusion.5.refs_1_), channel_id=1, source_target_pairs={{0,2},{1,3},{2,0},{3,1},{4,6},{5,7},{6,4},{7,5},{8,10},{9,11},{10,... | collective-permute-start | bytes 983048 | tf_op jit(solution)/shard_map/ppermute | solution.py:539
  63.7 13.7 %collective-permute-start.17 = (bf16[64,512]{1,0:T(8,128)(2,1)S(1)}, bf16[64,512]{1,0:T(8,128)(2,1)S(1)}, u32[]{:S(2)}, u32[]{:S(2)}) collective-permute-start(bf16[64,512]{1,0:T(8,128)(2,1)S(1)} %copy-done.1), channel_id=1, source_target_pairs={{8,20},{12,8},{16,12},{20,16},{24,4},{28,24},{0,28},{4,0},{9,21},{... | collective-permute-start | bytes 196616 | tf_op jit(solution)/shard_map/ppermute | solution.py:720
  63.7 13.7 %collective-permute-start.16 = (bf16[64,512]{1,0:T(8,128)(2,1)S(1)}, bf16[64,512]{1,0:T(8,128)(2,1)S(1)}, u32[]{:S(2)}, u32[]{:S(2)}) collective-permute-start(bf16[64,512]{1,0:T(8,128)(2,1)S(1)} %copy-done.1), channel_id=1, source_target_pairs={{8,16},{12,20},{16,8},{20,12},{24,0},{28,4},{0,24},{4,28},{9,17},{... | collective-permute-start | bytes 196616 | tf_op jit(solution)/shard_map/ppermute | solution.py:720
  114.1 15.8 %collective-permute-start.26 = (bf16[2,160,512]{2,1,0:T(8,128)(2,1)S(1)}, bf16[2,160,512]{2,1,0:T(8,128)(2,1)S(1)}, u32[]{:S(2)}, u32[]{:S(2)}) collective-permute-start(bf16[2,160,512]{2,1,0:T(8,128)(2,1)S(1)} %get-tuple-element.144), channel_id=1, source_target_pairs={{0,1},{1,0},{2,3},{3,2},{4,5},{5,4},{6,7},{7,6},{8,9},{9,8},{10,11... | collective-permute-start | bytes 983048 | tf_op jit(solution)/shard_map/ppermute | solution.py:535
  114.3 15.7 %collective-permute-start.27 = (bf16[2,160,512]{2,1,0:T(8,128)(2,1)S(1)}, bf16[2,160,512]{2,1,0:T(8,128)(2,1)S(1)}, u32[]{:S(2)}, u32[]{:S(2)}) collective-permute-start(bf16[2,160,512]{2,1,0:T(8,128)(2,1)S(1)} %add_convert_fusion.2.refs_1_), channel_id=1, source_target_pairs={{0,2},{1,3},{2,0},{3,1},{4,6},{5,7},{6,4},{7,5},{8,10},{9,11},{10,... | collective-permute-start | bytes 983048 | tf_op jit(solution)/shard_map/ppermute | solution.py:539
  122.9 22.3 %collective-permute-start.30 = (bf16[4,64,1536]{2,1,0:T(8,128)(2,1)S(1)}, bf16[4,64,1536]{2,1,0:T(8,128)(2,1)S(1)}, u32[]{:S(2)}, u32[]{:S(2)}) collective-permute-start(bf16[4,64,1536]{2,1,0:T(8,128)(2,1)S(1)} %get-tuple-element.153), channel_id=1, source_target_pairs={{0,4},{4,0},{8,12},{12,8},{16,20},{20,16},{24,28},{28,24},{1,5},{5... | collective-permute-start | bytes 2359304 | tf_op jit(solution)/shard_map/ppermute | solution.py:575
  131.2 17.3 %collective-permute-start.40 = (bf16[64,512]{1,0:T(8,128)(2,1)S(1)}, bf16[64,512]{1,0:T(8,128)(2,1)S(1)}, u32[]{:S(2)}, u32[]{:S(2)}) collective-permute-start(bf16[64,512]{1,0:T(8,128)(2,1)S(1)} %add_convert_fusion.8), channel_id=1, source_target_pairs={{0,2},{1,3},{2,0},{3,1},{4,6},{5,7},{6,4},{7,5},{8,10},{9,11},{10,... | collective-permute-start | bytes 196616 | tf_op jit(solution)/shard_map/ppermute | solution.py:539
  131.8 20.7 %collective-permute-start.28 = (bf16[160,512]{1,0:T(8,128)(2,1)S(1)}, bf16[160,512]{1,0:T(8,128)(2,1)S(1)}, u32[]{:S(2)}, u32[]{:S(2)}) collective-permute-start(bf16[160,512]{1,0:T(8,128)(2,1)S(1)} %fusion.3), channel_id=1, source_target_pairs={{0,2},{1,3},{2,0},{3,1},{4,6},{5,7},{6,4},{7,5},{8,10},{9,11},{10,... | collective-permute-start | bytes 491528 | tf_op jit(solution)/shard_map/ppermute | solution.py:539
  139.3 14.0 %collective-permute-start.31 = (bf16[640,256]{1,0:T(8,128)(2,1)S(1)}, bf16[640,256]{1,0:T(8,128)(2,1)S(1)}, u32[]{:S(2)}, u32[]{:S(2)}) collective-permute-start(bf16[640,256]{1,0:T(8,128)(2,1)S(1)} %get-tuple-element.168), channel_id=1, source_target_pairs={{20,8},{4,24},{21,9},{5,25},{22,10},{6,26},{23,11},{7,27}} | collective-permute-start | bytes 983048 | tf_op jit(solution)/shard_map/ppermute | solution.py:821
  140.0 13.3 %collective-permute-start.32 = (bf16[640,256]{1,0:T(8,128)(2,1)S(1)}, bf16[640,256]{1,0:T(8,128)(2,1)S(1)}, u32[]{:S(2)}, u32[]{:S(2)}) collective-permute-start(bf16[640,256]{1,0:T(8,128)(2,1)S(1)} %get-tuple-element.169), channel_id=1, source_target_pairs={{16,8},{20,12},{0,24},{4,28},{17,9},{21,13},{1,25},{5,29},{18,10},... | collective-permute-start | bytes 983048 | tf_op jit(solution)/shard_map/ppermute | solution.py:821
  145.2 12.4 %collective-permute-start.33 = (bf16[640,256]{1,0:T(8,128)(2,1)S(1)}, bf16[640,256]{1,0:T(8,128)(2,1)S(1)}, u32[]{:S(2)}, u32[]{:S(2)}) collective-permute-start(bf16[640,256]{1,0:T(8,128)(2,1)S(1)} %get-tuple-element.170), channel_id=1, source_target_pairs={{12,8},{16,12},{20,16},{28,24},{0,28},{4,0},{13,9},{17,13},{21,17}... | collective-permute-start | bytes 983048 | tf_op jit(solution)/shard_map/ppermute | solution.py:821
  148.4 16.2 %collective-permute-start.44 = (bf16[2,64,1536]{2,1,0:T(8,128)(2,1)S(1)}, bf16[2,64,1536]{2,1,0:T(8,128)(2,1)S(1)}, u32[]{:S(2)}, u32[]{:S(2)}) collective-permute-start(bf16[2,64,1536]{2,1,0:T(8,128)(2,1)S(1)} %slice.75), channel_id=1, source_target_pairs={{0,8},{4,12},{8,0},{12,4},{16,24},{20,28},{24,16},{28,20},{1,9},{5... | collective-permute-start | bytes 1179656 | tf_op jit(solution)/shard_map/ppermute | solution.py:590
  159.4 10.5 %collective-permute-start.34 = (bf16[2,160,512]{2,1,0:T(8,128)(2,1)S(1)}, bf16[2,160,512]{2,1,0:T(8,128)(2,1)S(1)}, u32[]{:S(2)}, u32[]{:S(2)}) collective-permute-start(bf16[2,160,512]{2,1,0:T(8,128)(2,1)S(1)} %get-tuple-element.174.refs_2_), channel_id=1, source_target_pairs={{0,1},{1,0},{2,3},{3,2},{4,5},{5,4},{6,7},{7,6},{8,9},{9,8},{10,11... | collective-permute-start | bytes 983048 | tf_op jit(solution)/shard_map/ppermute | solution.py:535
  164.8 11.8 %collective-permute-start.45 = (bf16[1,64,1536]{2,1,0:T(8,128)(2,1)S(1)}, bf16[1,64,1536]{2,1,0:T(8,128)(2,1)S(1)}, u32[]{:S(2)}, u32[]{:S(2)}) collective-permute-start(bf16[1,64,1536]{2,1,0:T(8,128)(2,1)S(1)} %get-tuple-element.197), channel_id=1, source_target_pairs={{0,16},{4,20},{8,24},{12,28},{16,0},{20,4},{24,8},{28,12},{1,17},{... | collective-permute-start | bytes 589832 | tf_op jit(solution)/shard_map/ppermute | solution.py:590
  174.9 11.2 %collective-permute-start.35 = (bf16[160,512]{1,0:T(8,128)(2,1)S(1)}, bf16[160,512]{1,0:T(8,128)(2,1)S(1)}, u32[]{:S(2)}, u32[]{:S(2)}) collective-permute-start(bf16[160,512]{1,0:T(8,128)(2,1)S(1)} %fusion.4), channel_id=1, source_target_pairs={{0,2},{1,3},{2,0},{3,1},{4,6},{5,7},{6,4},{7,5},{8,10},{9,11},{10,... | collective-permute-start | bytes 491528 | tf_op jit(solution)/shard_map/ppermute | solution.py:539
  (34 other events, 273.6 us)

commit v6 on v5

--- a/solution.py
+++ b/solution.py
@@ -719,7 +719,7 @@
     enc_sent = tie(enc_states, attn)
     enc_parts = [enc_states] + [lax.ppermute(enc_sent, "dp", turn(d)) for d in range(1, group)]
     chip = chip_sum(kept, sent).astype(bf16)
-    ffn_far = neighbour(tie(ffn_near, attn))
+    ffn_far = neighbour(tie(ffn_near, rest_w))
     resid_mid, act_own = run(
         lambda *refs: norm_body(True, 3, 1, *refs),
         [shaped(half, f32), shaped(half, bf16)],

time: 188 us -> 188 us (level)
  no operation moved by 1% of the time
where the time goes in v6:
time: 188 us; the launch traced here: 187 us
  waiting for transfers between devices  72.8 us (39%)
  starting transfers between devices  69.5 us (37%)
  Pallas kernels  36.7 us (20%)
  other arithmetic  4.08 us (2%)
  local copies, waits for them, and re-layouts  2.81 us (1%)
    pallas_call x24, Pallas kernels, run(): pl.pallas_call(wrapped, out_shape=outs, in_specs=[pl.BlockSpec(memory_spa...  36.7 us
    ppermute x9, waiting for transfers between devices, across(): return lax.ppermute(x, 'tensor', xor_route('tensor', 2))  16 us
    ppermute x4, waiting for transfers between devices, neighbour(): return lax.ppermute(x, 'dp', xor_route('dp', 1))  15.7 us
    ppermute x9, starting transfers between devices, across(): return lax.ppermute(x, 'tensor', xor_route('tensor', 2))  12.1 us
    ppermute x4, starting transfers between devices, step(): lax.ppermute(total[middle:], 'dp', xor_route('dp', self.bit))  10.9 us
    ppermute x13, waiting for transfers between devices, sibling(): return lax.ppermute(x, 'tensor', xor_route('tensor', 1))  9.6 us
    ppermute x3, waiting for transfers between devices, on_device(): lax.ppermute(enc_sent, 'dp', turn(d))  8.99 us
    ppermute x4, starting transfers between devices, neighbour(): return lax.ppermute(x, 'dp', xor_route('dp', 1))  8.1 us
  transfers between devices with their start and end apart: 48, of which 18 were waited for; matrix products, arithmetic and copies ran while one was open for 4% of the time, Pallas kernels for 14%

profile of v6, /device:TPU:0, one launch (start us, length us, event | category | flops | bytes accessed | tf_op | source)
XLA Modules:
  0.0 187.1 jit_solution(5346265697917394111)
XLA Ops:
  3.3 7.3 %all-to-all-start = ((bf16[8,72,384]{2,1,0:T(8,128)(2,1)}), bf16[8,72,384]{2,1,0:T(8,128)(2,1)S(1)}, u32[]{:S(2)}, u32[]{:S(2)}) async-start(bf16[8,72,384]{2,1,0:T(8,128)(2,1)} %shard_map.341), calls=%async_computation | async-start | bytes 884736 | tf_op jit(solution)/shard_map/all_to_all | solution.py:637
  14.4 2.9 %collective-permute-start.7 = (bf16[1,64,640]{2,1,0:T(8,128)(2,1)}, bf16[1,64,640]{2,1,0:T(8,128)(2,1)S(1)}, u32[]{:S(2)}, u32[]{:S(2)}) collective-permute-start(bf16[1,64,640]{2,1,0:T(8,128)(2,1)} %bitcast.54), channel_id=1, source_target_pairs={{0,16},{4,20},{8,24},{12,28},{16,0},{20,4},{24,8},{28,12},{1,17},{... | collective-permute-start | bytes 245768 | tf_op jit(solution)/shard_map/ppermute | solution.py:559
  19.7 6.2 %all-to-all-done.refs_3_ = bf16[8,72,384]{2,1,0:T(8,128)(2,1)S(1)} async-done(((bf16[8,72,384]{2,1,0:T(8,128)(2,1)}), bf16[8,72,384]{2,1,0:T(8,128)(2,1)S(1)}, u32[]{:S(2)}, u32[]{:S(2)}) %all-to-all-start) | async-done | bytes 442400 | tf_op jit(solution)/shard_map/all_to_all | solution.py:637
  29.5 3.1 %collective-permute-start.6 = (bf16[640,256]{1,0:T(8,128)(2,1)S(1)}, bf16[640,256]{1,0:T(8,128)(2,1)S(1)}, u32[]{:S(2)}, u32[]{:S(2)}) collective-permute-start(bf16[640,256]{1,0:T(8,128)(2,1)S(1)} %get-tuple-element.111.refs_5_.refs_9_), channel_id=1, source_target_pairs={{8,12},{12,16},{16,20},{24,28},{28,0},{0,4},{9,13},{13,17},{17,21}... | collective-permute-start | bytes 983048 | tf_op jit(solution)/shard_map/ppermute | solution.py:706
  38.6 15.7 %collective-permute-done.9.refs_2_ = bf16[4,64,640]{2,1,0:T(8,128)(2,1)S(1)} collective-permute-done((bf16[4,64,640]{2,1,0:T(8,128)(2,1)S(1)}, bf16[4,64,640]{2,1,0:T(8,128)(2,1)S(1)}, u32[]{:S(2)}, u32[]{:S(2)}) %collective-permute-start.9) | collective-permute-done | bytes 327712 | tf_op jit(solution)/shard_map/ppermute | solution.py:575
  54.9 4.5 %shard_map.345 = (bf16[640,128]{1,0:T(8,128)(2,1)S(1)}, f32[8,640]{1,0:T(8,128)S(1)}, f32[2,160,512]{2,1,0:T(8,128)S(1)}, bf16[2,160,512]{2,1,0:T(8,128)(2,1)S(1)}) custom-call(s32[18]{0:T(128)S(1)} %concatenate.17.refs_0_, bf16[640,128]{1,0:T(8,128)(2,1)S(1)} %get-tuple-element.110.refs_1_.refs_3_, ...), custom_call_target="tpu_custom_call" | custom-call | flops 500000000 | bytes 1000000 | tf_op jit(solution)/shard_map/pallas_call | solution.py:91
  59.5 2.6 %collective-permute-start.14 = (bf16[4,64,1024]{2,1,0:T(8,128)(2,1)S(1)}, bf16[4,64,1024]{2,1,0:T(8,128)(2,1)S(1)}, u32[]{:S(2)}, u32[]{:S(2)}) collective-permute-start(bf16[4,64,1024]{2,1,0:T(8,128)(2,1)S(1)} %pad_maximum_fusion.refs_1_), channel_id=1, source_target_pairs={{0,4},{4,0},{8,12},{12,8},{16,20},{20,16},{24,28},{28,24},{1,5},{5... | collective-permute-start | bytes 1572872 | tf_op jit(solution)/shard_map/ppermute | solution.py:575
  63.7 4.7 %collective-permute-start.16 = (bf16[64,512]{1,0:T(8,128)(2,1)S(1)}, bf16[64,512]{1,0:T(8,128)(2,1)S(1)}, u32[]{:S(2)}, u32[]{:S(2)}) collective-permute-start(bf16[64,512]{1,0:T(8,128)(2,1)S(1)} %copy-done.1), channel_id=1, source_target_pairs={{8,16},{12,20},{16,8},{20,12},{24,0},{28,4},{0,24},{4,28},{9,17},{... | collective-permute-start | bytes 196616 | tf_op jit(solution)/shard_map/ppermute | solution.py:720
  68.5 9.0 %collective-permute-done.17.refs_5_.refs_10_ = bf16[64,512]{1,0:T(8,128)(2,1)S(1)} collective-permute-done((bf16[64,512]{1,0:T(8,128)(2,1)S(1)}, bf16[64,512]{1,0:T(8,128)(2,1)S(1)}, u32[]{:S(2)}, u32[]{:S(2)}) %collective-permute-start.17) | collective-permute-done | bytes 65568 | tf_op jit(solution)/shard_map/ppermute | solution.py:720
  84.5 8.3 %collective-permute-done.20.refs_2_ = bf16[2,160,512]{2,1,0:T(8,128)(2,1)S(1)} collective-permute-done((bf16[2,160,512]{2,1,0:T(8,128)(2,1)S(1)}, bf16[2,160,512]{2,1,0:T(8,128)(2,1)S(1)}, u32[]{:S(2)}, u32[]{:S(2)}) %collective-permute-start.20) | collective-permute-done | bytes 327712 | tf_op jit(solution)/shard_map/ppermute | solution.py:539
  100.4 7.7 %collective-permute-done.23.refs_2_ = bf16[2,160,512]{2,1,0:T(8,128)(2,1)S(1)} collective-permute-done((bf16[2,160,512]{2,1,0:T(8,128)(2,1)S(1)}, bf16[2,160,512]{2,1,0:T(8,128)(2,1)S(1)}, u32[]{:S(2)}, u32[]{:S(2)}) %collective-permute-start.23) | collective-permute-done | bytes 327712 | tf_op jit(solution)/shard_map/ppermute | solution.py:539
  117.9 5.0 %collective-permute-start.37 = (bf16[64,256]{1,0:T(8,128)(2,1)S(1)}, bf16[64,256]{1,0:T(8,128)(2,1)S(1)}, u32[]{:S(2)}, u32[]{:S(2)}) collective-permute-start(bf16[64,256]{1,0:T(8,128)(2,1)S(1)} %get-tuple-element.177.refs_13_), channel_id=1, source_target_pairs={{16,8},{20,12},{8,16},{12,20},{0,24},{4,28},{24,0},{28,4},{17,9},{... | collective-permute-start | bytes 98312 | tf_op jit(solution)/shard_map/ppermute | solution.py:790
  122.9 3.4 %collective-permute-start.30 = (bf16[4,64,1536]{2,1,0:T(8,128)(2,1)S(1)}, bf16[4,64,1536]{2,1,0:T(8,128)(2,1)S(1)}, u32[]{:S(2)}, u32[]{:S(2)}) collective-permute-start(bf16[4,64,1536]{2,1,0:T(8,128)(2,1)S(1)} %get-tuple-element.153), channel_id=1, source_target_pairs={{0,4},{4,0},{8,12},{12,8},{16,20},{20,16},{24,28},{28,24},{1,5},{5... | collective-permute-start | bytes 2359304 | tf_op jit(solution)/shard_map/ppermute | solution.py:575
  126.3 3.3 %collective-permute-done.38.refs_4_ = bf16[64,256]{1,0:T(8,128)(2,1)S(1)} collective-permute-done((bf16[64,256]{1,0:T(8,128)(2,1)S(1)}, bf16[64,256]{1,0:T(8,128)(2,1)S(1)}, u32[]{:S(2)}, u32[]{:S(2)}) %collective-permute-start.38) | collective-permute-done | bytes 32800 | tf_op jit(solution)/shard_map/ppermute | solution.py:790
  133.3 5.9 %shard_map.356 = (bf16[640,512]{1,0:T(8,128)(2,1)S(1)}, bf16[2,1024,640]{2,1,0:T(8,128)(2,1)S(1)}, bf16[2,2,128,640]{3,2,1,0:T(8,128)(2,1)S(1)}, f32[640,256]{1,...) custom-call(s32[18]{0:T(128)S(1)} %concatenate.17.refs_0_, ...), custom_call_target="tpu_custom_call" | custom-call | flops 800000000 | bytes 1000000 | tf_op jit(solution)/shard_map/pallas_call | solution.py:91
  140.0 2.5 %collective-permute-start.32 = (bf16[640,256]{1,0:T(8,128)(2,1)S(1)}, bf16[640,256]{1,0:T(8,128)(2,1)S(1)}, u32[]{:S(2)}, u32[]{:S(2)}) collective-permute-start(bf16[640,256]{1,0:T(8,128)(2,1)S(1)} %get-tuple-element.169), channel_id=1, source_target_pairs={{16,8},{20,12},{0,24},{4,28},{17,9},{21,13},{1,25},{5,29},{18,10},... | collective-permute-start | bytes 983048 | tf_op jit(solution)/shard_map/ppermute | solution.py:821
  142.5 2.7 %shard_map.357 = (f32[512,128]{1,0:T(8,128)S(1)}, f32[512,128]{1,0:T(8,128)S(1)}, f32[640,512]{1,0:T(8,128)S(1)}) custom-call(s32[18]{0:T(128)S(1)} %concatenate.17.refs_0_, bf16[640,512]{1,0:T(8,128)(2,1)S(1)} %get-tuple-element.157.refs_1_.refs_2_, bf16[640,512]{1,0:T(8,128)(2,1)S(1)} %get-tuple-element.161.refs_2_, ...), custom_call_target="tpu_custom_call" | custom-call | flops 400000000 | bytes 1000000 | tf_op jit(solution)/shard_map/pallas_call | solution.py:91
  145.2 3.0 %collective-permute-start.33 = (bf16[640,256]{1,0:T(8,128)(2,1)S(1)}, bf16[640,256]{1,0:T(8,128)(2,1)S(1)}, u32[]{:S(2)}, u32[]{:S(2)}) collective-permute-start(bf16[640,256]{1,0:T(8,128)(2,1)S(1)} %get-tuple-element.170), channel_id=1, source_target_pairs={{12,8},{16,12},{20,16},{28,24},{0,28},{4,0},{13,9},{17,13},{21,17}... | collective-permute-start | bytes 983048 | tf_op jit(solution)/shard_map/ppermute | solution.py:821
  148.4 3.4 %collective-permute-start.44 = (bf16[2,64,1536]{2,1,0:T(8,128)(2,1)S(1)}, bf16[2,64,1536]{2,1,0:T(8,128)(2,1)S(1)}, u32[]{:S(2)}, u32[]{:S(2)}) collective-permute-start(bf16[2,64,1536]{2,1,0:T(8,128)(2,1)S(1)} %slice.75), channel_id=1, source_target_pairs={{0,8},{4,12},{8,0},{12,4},{16,24},{20,28},{24,16},{28,20},{1,9},{5... | collective-permute-start | bytes 1179656 | tf_op jit(solution)/shard_map/ppermute | solution.py:590
  153.2 4.4 %collective-permute-done.33.refs_6_ = bf16[640,256]{1,0:T(8,128)(2,1)S(1)} collective-permute-done((bf16[640,256]{1,0:T(8,128)(2,1)S(1)}, bf16[640,256]{1,0:T(8,128)(2,1)S(1)}, u32[]{:S(2)}, u32[]{:S(2)}) %collective-permute-start.33) | collective-permute-done | bytes 327712 | tf_op jit(solution)/shard_map/ppermute | solution.py:821
  159.4 5.2 %collective-permute-done.44 = bf16[2,64,1536]{2,1,0:T(8,128)(2,1)S(1)} collective-permute-done((bf16[2,64,1536]{2,1,0:T(8,128)(2,1)S(1)}, bf16[2,64,1536]{2,1,0:T(8,128)(2,1)S(1)}, u32[]{:S(2)}, u32[]{:S(2)}) %collective-permute-start.44) | collective-permute-done | bytes 393248 | tf_op jit(solution)/shard_map/ppermute | solution.py:590
  167.3 2.6 %collective-permute-start.42 = (bf16[2,64,512]{2,1,0:T(8,128)(2,1)S(1)}, bf16[2,64,512]{2,1,0:T(8,128)(2,1)S(1)}, u32[]{:S(2)}, u32[]{:S(2)}) collective-permute-start(bf16[2,64,512]{2,1,0:T(8,128)(2,1)S(1)} %slice.72), channel_id=1, source_target_pairs={{0,8},{4,12},{8,0},{12,4},{16,24},{20,28},{24,16},{28,20},{1,9},{5... | collective-permute-start | bytes 393224 | tf_op jit(solution)/shard_map/ppermute | solution.py:590
  172.3 2.6 %all-to-all-start.1 = ((f32[32,1,512]{2,1,0:T(1,128)}), f32[32,1,512]{2,1,0:T(1,128)S(1)}, u32[]{:S(2)}, u32[]{:S(2)}) async-start(f32[32,1,512]{2,1,0:T(1,128)} %reshape.44), calls=%async_computation.1 | async-start | bytes 131072 | tf_op jit(solution)/shard_map/all_to_all | solution.py:849
  177.4 2.6 %collective-permute-start.43 = (bf16[1,64,512]{2,1,0:T(8,128)(2,1)S(1)}, bf16[1,64,512]{2,1,0:T(8,128)(2,1)S(1)}, u32[]{:S(2)}, u32[]{:S(2)}) collective-permute-start(bf16[1,64,512]{2,1,0:T(8,128)(2,1)S(1)} %get-tuple-element.199), channel_id=1, source_target_pairs={{0,16},{4,20},{8,24},{12,28},{16,0},{20,4},{24,8},{28,12},{1,17},{... | collective-permute-start | bytes 196616 | tf_op jit(solution)/shard_map/ppermute | solution.py:590
  (152 shorter events, 67.3 us)
Async XLA Ops:
  3.3 22.7 %all-to-all-start = ((bf16[8,72,384]{2,1,0:T(8,128)(2,1)}), bf16[8,72,384]{2,1,0:T(8,128)(2,1)S(1)}, u32[]{:S(2)}, u32[]{:S(2)}) async-start(bf16[8,72,384]{2,1,0:T(8,128)(2,1)} %shard_map.341), calls=%async_computation | async-start | bytes 884736 | tf_op jit(solution)/shard_map/all_to_all | solution.py:637
  12.1 17.2 %collective-permute-start.2 = (bf16[160,512]{1,0:T(8,128)(2,1)S(1)}, bf16[160,512]{1,0:T(8,128)(2,1)S(1)}, u32[]{:S(2)}, u32[]{:S(2)}) collective-permute-start(bf16[160,512]{1,0:T(8,128)(2,1)S(1)} %copy-done.5), channel_id=1, source_target_pairs={{0,2},{1,3},{2,0},{3,1},{4,6},{5,7},{6,4},{7,5},{8,10},{9,11},{10,... | collective-permute-start | bytes 491528 | tf_op jit(solution)/shard_map/ppermute | solution.py:539
  14.4 13.2 %collective-permute-start.7 = (bf16[1,64,640]{2,1,0:T(8,128)(2,1)}, bf16[1,64,640]{2,1,0:T(8,128)(2,1)S(1)}, u32[]{:S(2)}, u32[]{:S(2)}) collective-permute-start(bf16[1,64,640]{2,1,0:T(8,128)(2,1)} %bitcast.54), channel_id=1, source_target_pairs={{0,16},{4,20},{8,24},{12,28},{16,0},{20,4},{24,8},{28,12},{1,17},{... | collective-permute-start | bytes 245768 | tf_op jit(solution)/shard_map/ppermute | solution.py:559
  29.5 25.4 %collective-permute-start.6 = (bf16[640,256]{1,0:T(8,128)(2,1)S(1)}, bf16[640,256]{1,0:T(8,128)(2,1)S(1)}, u32[]{:S(2)}, u32[]{:S(2)}) collective-permute-start(bf16[640,256]{1,0:T(8,128)(2,1)S(1)} %get-tuple-element.111.refs_5_.refs_9_), channel_id=1, source_target_pairs={{8,12},{12,16},{16,20},{24,28},{28,0},{0,4},{9,13},{13,17},{17,21}... | collective-permute-start | bytes 983048 | tf_op jit(solution)/shard_map/ppermute | solution.py:706
  32.6 22.3 %collective-permute-start.5 = (bf16[640,256]{1,0:T(8,128)(2,1)S(1)}, bf16[640,256]{1,0:T(8,128)(2,1)S(1)}, u32[]{:S(2)}, u32[]{:S(2)}) collective-permute-start(bf16[640,256]{1,0:T(8,128)(2,1)S(1)} %get-tuple-element.111.refs_5_.refs_9_), channel_id=1, source_target_pairs={{8,16},{12,20},{24,0},{28,4},{9,17},{13,21},{25,1},{29,5},{10,18},... | collective-permute-start | bytes 983048 | tf_op jit(solution)/shard_map/ppermute | solution.py:706
  34.9 20.0 %collective-permute-start.4 = (bf16[640,256]{1,0:T(8,128)(2,1)S(1)}, bf16[640,256]{1,0:T(8,128)(2,1)S(1)}, u32[]{:S(2)}, u32[]{:S(2)}) collective-permute-start(bf16[640,256]{1,0:T(8,128)(2,1)S(1)} %get-tuple-element.111.refs_5_.refs_9_), channel_id=1, source_target_pairs={{8,20},{24,4},{9,21},{25,5},{10,22},{26,6},{11,23},{27,7}} | collective-permute-start | bytes 983048 | tf_op jit(solution)/shard_map/ppermute | solution.py:706
  35.6 18.6 %collective-permute-start.9 = (bf16[4,64,640]{2,1,0:T(8,128)(2,1)S(1)}, bf16[4,64,640]{2,1,0:T(8,128)(2,1)S(1)}, u32[]{:S(2)}, u32[]{:S(2)}) collective-permute-start(bf16[4,64,640]{2,1,0:T(8,128)(2,1)S(1)} %pad_maximum_fusion.3.refs_1_), channel_id=1, source_target_pairs={{0,4},{4,0},{8,12},{12,8},{16,20},{20,16},{24,28},{28,24},{1,5},{5... | collective-permute-start | bytes 983048 | tf_op jit(solution)/shard_map/ppermute | solution.py:575
  37.6 21.8 %collective-permute-start.13 = (bf16[2,64,1024]{2,1,0:T(8,128)(2,1)S(1)}, bf16[2,64,1024]{2,1,0:T(8,128)(2,1)S(1)}, u32[]{:S(2)}, u32[]{:S(2)}) collective-permute-start(bf16[2,64,1024]{2,1,0:T(8,128)(2,1)S(1)} %pad_maximum_fusion.4), channel_id=1, source_target_pairs={{0,8},{4,12},{8,0},{12,4},{16,24},{20,28},{24,16},{28,20},{1,9},{5... | collective-permute-start | bytes 786440 | tf_op jit(solution)/shard_map/ppermute | solution.py:559
  59.5 17.9 %collective-permute-start.14 = (bf16[4,64,1024]{2,1,0:T(8,128)(2,1)S(1)}, bf16[4,64,1024]{2,1,0:T(8,128)(2,1)S(1)}, u32[]{:S(2)}, u32[]{:S(2)}) collective-permute-start(bf16[4,64,1024]{2,1,0:T(8,128)(2,1)S(1)} %pad_maximum_fusion.refs_1_), channel_id=1, source_target_pairs={{0,4},{4,0},{8,12},{12,8},{16,20},{20,16},{24,28},{28,24},{1,5},{5... | collective-permute-start | bytes 1572872 | tf_op jit(solution)/shard_map/ppermute | solution.py:575
  62.2 15.3 %collective-permute-start.11 = (bf16[2,160,512]{2,1,0:T(8,128)(2,1)S(1)}, bf16[2,160,512]{2,1,0:T(8,128)(2,1)S(1)}, u32[]{:S(2)}, u32[]{:S(2)}) collective-permute-start(bf16[2,160,512]{2,1,0:T(8,128)(2,1)S(1)} %add_convert_fusion.5.refs_1_), channel_id=1, source_target_pairs={{0,2},{1,3},{2,0},{3,1},{4,6},{5,7},{6,4},{7,5},{8,10},{9,11},{10,... | collective-permute-start | bytes 983048 | tf_op jit(solution)/shard_map/ppermute | solution.py:539
  63.7 13.7 %collective-permute-start.17 = (bf16[64,512]{1,0:T(8,128)(2,1)S(1)}, bf16[64,512]{1,0:T(8,128)(2,1)S(1)}, u32[]{:S(2)}, u32[]{:S(2)}) collective-permute-start(bf16[64,512]{1,0:T(8,128)(2,1)S(1)} %copy-done.1), channel_id=1, source_target_pairs={{8,20},{12,8},{16,12},{20,16},{24,4},{28,24},{0,28},{4,0},{9,21},{... | collective-permute-start | bytes 196616 | tf_op jit(solution)/shard_map/ppermute | solution.py:720
  63.7 13.7 %collective-permute-start.16 = (bf16[64,512]{1,0:T(8,128)(2,1)S(1)}, bf16[64,512]{1,0:T(8,128)(2,1)S(1)}, u32[]{:S(2)}, u32[]{:S(2)}) collective-permute-start(bf16[64,512]{1,0:T(8,128)(2,1)S(1)} %copy-done.1), channel_id=1, source_target_pairs={{8,16},{12,20},{16,8},{20,12},{24,0},{28,4},{0,24},{4,28},{9,17},{... | collective-permute-start | bytes 196616 | tf_op jit(solution)/shard_map/ppermute | solution.py:720
  114.1 15.8 %collective-permute-start.26 = (bf16[2,160,512]{2,1,0:T(8,128)(2,1)S(1)}, bf16[2,160,512]{2,1,0:T(8,128)(2,1)S(1)}, u32[]{:S(2)}, u32[]{:S(2)}) collective-permute-start(bf16[2,160,512]{2,1,0:T(8,128)(2,1)S(1)} %get-tuple-element.144), channel_id=1, source_target_pairs={{0,1},{1,0},{2,3},{3,2},{4,5},{5,4},{6,7},{7,6},{8,9},{9,8},{10,11... | collective-permute-start | bytes 983048 | tf_op jit(solution)/shard_map/ppermute | solution.py:535
  114.3 15.7 %collective-permute-start.27 = (bf16[2,160,512]{2,1,0:T(8,128)(2,1)S(1)}, bf16[2,160,512]{2,1,0:T(8,128)(2,1)S(1)}, u32[]{:S(2)}, u32[]{:S(2)}) collective-permute-start(bf16[2,160,512]{2,1,0:T(8,128)(2,1)S(1)} %add_convert_fusion.2.refs_1_), channel_id=1, source_target_pairs={{0,2},{1,3},{2,0},{3,1},{4,6},{5,7},{6,4},{7,5},{8,10},{9,11},{10,... | collective-permute-start | bytes 983048 | tf_op jit(solution)/shard_map/ppermute | solution.py:539
  122.9 22.3 %collective-permute-start.30 = (bf16[4,64,1536]{2,1,0:T(8,128)(2,1)S(1)}, bf16[4,64,1536]{2,1,0:T(8,128)(2,1)S(1)}, u32[]{:S(2)}, u32[]{:S(2)}) collective-permute-start(bf16[4,64,1536]{2,1,0:T(8,128)(2,1)S(1)} %get-tuple-element.153), channel_id=1, source_target_pairs={{0,4},{4,0},{8,12},{12,8},{16,20},{20,16},{24,28},{28,24},{1,5},{5... | collective-permute-start | bytes 2359304 | tf_op jit(solution)/shard_map/ppermute | solution.py:575
  131.2 17.3 %collective-permute-start.40 = (bf16[64,512]{1,0:T(8,128)(2,1)S(1)}, bf16[64,512]{1,0:T(8,128)(2,1)S(1)}, u32[]{:S(2)}, u32[]{:S(2)}) collective-permute-start(bf16[64,512]{1,0:T(8,128)(2,1)S(1)} %add_convert_fusion.8), channel_id=1, source_target_pairs={{0,2},{1,3},{2,0},{3,1},{4,6},{5,7},{6,4},{7,5},{8,10},{9,11},{10,... | collective-permute-start | bytes 196616 | tf_op jit(solution)/shard_map/ppermute | solution.py:539
  131.8 20.7 %collective-permute-start.28 = (bf16[160,512]{1,0:T(8,128)(2,1)S(1)}, bf16[160,512]{1,0:T(8,128)(2,1)S(1)}, u32[]{:S(2)}, u32[]{:S(2)}) collective-permute-start(bf16[160,512]{1,0:T(8,128)(2,1)S(1)} %fusion.3), channel_id=1, source_target_pairs={{0,2},{1,3},{2,0},{3,1},{4,6},{5,7},{6,4},{7,5},{8,10},{9,11},{10,... | collective-permute-start | bytes 491528 | tf_op jit(solution)/shard_map/ppermute | solution.py:539
  139.3 14.0 %collective-permute-start.31 = (bf16[640,256]{1,0:T(8,128)(2,1)S(1)}, bf16[640,256]{1,0:T(8,128)(2,1)S(1)}, u32[]{:S(2)}, u32[]{:S(2)}) collective-permute-start(bf16[640,256]{1,0:T(8,128)(2,1)S(1)} %get-tuple-element.168), channel_id=1, source_target_pairs={{20,8},{4,24},{21,9},{5,25},{22,10},{6,26},{23,11},{7,27}} | collective-permute-start | bytes 983048 | tf_op jit(solution)/shard_map/ppermute | solution.py:821
  140.0 13.3 %collective-permute-start.32 = (bf16[640,256]{1,0:T(8,128)(2,1)S(1)}, bf16[640,256]{1,0:T(8,128)(2,1)S(1)}, u32[]{:S(2)}, u32[]{:S(2)}) collective-permute-start(bf16[640,256]{1,0:T(8,128)(2,1)S(1)} %get-tuple-element.169), channel_id=1, source_target_pairs={{16,8},{20,12},{0,24},{4,28},{17,9},{21,13},{1,25},{5,29},{18,10},... | collective-permute-start | bytes 983048 | tf_op jit(solution)/shard_map/ppermute | solution.py:821
  145.2 12.4 %collective-permute-start.33 = (bf16[640,256]{1,0:T(8,128)(2,1)S(1)}, bf16[640,256]{1,0:T(8,128)(2,1)S(1)}, u32[]{:S(2)}, u32[]{:S(2)}) collective-permute-start(bf16[640,256]{1,0:T(8,128)(2,1)S(1)} %get-tuple-element.170), channel_id=1, source_target_pairs={{12,8},{16,12},{20,16},{28,24},{0,28},{4,0},{13,9},{17,13},{21,17}... | collective-permute-start | bytes 983048 | tf_op jit(solution)/shard_map/ppermute | solution.py:821
  148.4 16.2 %collective-permute-start.44 = (bf16[2,64,1536]{2,1,0:T(8,128)(2,1)S(1)}, bf16[2,64,1536]{2,1,0:T(8,128)(2,1)S(1)}, u32[]{:S(2)}, u32[]{:S(2)}) collective-permute-start(bf16[2,64,1536]{2,1,0:T(8,128)(2,1)S(1)} %slice.75), channel_id=1, source_target_pairs={{0,8},{4,12},{8,0},{12,4},{16,24},{20,28},{24,16},{28,20},{1,9},{5... | collective-permute-start | bytes 1179656 | tf_op jit(solution)/shard_map/ppermute | solution.py:590
  159.4 10.5 %collective-permute-start.34 = (bf16[2,160,512]{2,1,0:T(8,128)(2,1)S(1)}, bf16[2,160,512]{2,1,0:T(8,128)(2,1)S(1)}, u32[]{:S(2)}, u32[]{:S(2)}) collective-permute-start(bf16[2,160,512]{2,1,0:T(8,128)(2,1)S(1)} %get-tuple-element.174.refs_2_), channel_id=1, source_target_pairs={{0,1},{1,0},{2,3},{3,2},{4,5},{5,4},{6,7},{7,6},{8,9},{9,8},{10,11... | collective-permute-start | bytes 983048 | tf_op jit(solution)/shard_map/ppermute | solution.py:535
  164.8 11.8 %collective-permute-start.45 = (bf16[1,64,1536]{2,1,0:T(8,128)(2,1)S(1)}, bf16[1,64,1536]{2,1,0:T(8,128)(2,1)S(1)}, u32[]{:S(2)}, u32[]{:S(2)}) collective-permute-start(bf16[1,64,1536]{2,1,0:T(8,128)(2,1)S(1)} %get-tuple-element.197), channel_id=1, source_target_pairs={{0,16},{4,20},{8,24},{12,28},{16,0},{20,4},{24,8},{28,12},{1,17},{... | collective-permute-start | bytes 589832 | tf_op jit(solution)/shard_map/ppermute | solution.py:590
  174.9 11.2 %collective-permute-start.35 = (bf16[160,512]{1,0:T(8,128)(2,1)S(1)}, bf16[160,512]{1,0:T(8,128)(2,1)S(1)}, u32[]{:S(2)}, u32[]{:S(2)}) collective-permute-start(bf16[160,512]{1,0:T(8,128)(2,1)S(1)} %fusion.4), channel_id=1, source_target_pairs={{0,2},{1,3},{2,0},{3,1},{4,6},{5,7},{6,4},{7,5},{8,10},{9,11},{10,... | collective-permute-start | bytes 491528 | tf_op jit(solution)/shard_map/ppermute | solution.py:539
  (34 other events, 273.6 us)
